TPU v7x, 32 devices: a whole 2x2x4 slice. The times are simulated.
32 devices in a mesh: row: 4 (over x, core), col: 8 (over z, y).
Axes of the slice: x: 2, y: 2, z: 4, core: 2. Of those that a mesh axis runs over, the one named last changes fastest.
Arguments:
- vectors: bfloat16 [32, 8192], P(None, ('row', 'col')), may hold values from -6 to 6
- tiles: bfloat16 [512, 256, 256], P(('row', 'col')), may hold values from -0.09375 to 0.09375
- tile_rows: int32 [512], P(('row', 'col')), may hold values from 0 to 7, as said below
- tile_cols: int32 [512], P(('row', 'col')), may hold values from 0 to 3, as said below
- tile_live: int32 [32], P(('row', 'col')), may hold values from 2 to 16, as said below
Outputs:
- first: bfloat16 [32, 8192], P(None, ('row', 'col'))
- second: bfloat16 [32, 8192], P(None, ('row', 'col'))
Inputs may be any that keep to these rules, and one draw needn't show every extreme that they name: `tile_rows`: A slot's row block is counted among the 8 row blocks of its device's row index, and its global row block never exceeds its global column block. `tile_cols`: A slot's column block is counted among the 4 column blocks of its device's column index. Each device uses its first tile_live slots; some device uses all 16.
All inputs are finite; a program needn't handle non-finite values.
Results may differ from a plain program's by a relative error of at most 0.0044.
Values may be sent and summed in bfloat16 or wider, within the bound.
No kernel may reach another device: no remote copies, remote signals or barrier semaphores. Data moves between devices by JAX's collectives and lax.ppermute only.
A program may use at most 64 MiB of HBM per device.

v0:
```python
import jax
import jax.numpy as jnp
from jax import lax
from jax.sharding import PartitionSpec as P


def half_direct(colset, tiles, rows, keep, count_rows):
    width = colset.shape[0]
    size = tiles.shape[1]
    picked = jnp.take(colset.reshape(width, -1, size), rows[1], axis=1)
    direct = jnp.einsum("ktj,tij->kti", picked, tiles, preferred_element_type=jnp.float32)
    row_hot = (rows[0][:, None] == jnp.arange(count_rows, dtype=jnp.int32)[None, :]).astype(
        jnp.float32
    ) * keep[:, None]
    placed = jnp.einsum("kti,ta->kai", direct, row_hot, precision=lax.Precision.HIGHEST)
    return placed.reshape(width, count_rows * size)


def half_mirror(rowset, tiles, cols, keep, count_cols):
    width = rowset.shape[0]
    size = tiles.shape[1]
    picked = jnp.take(rowset.reshape(width, -1, size), cols[1], axis=1)
    mirror = jnp.einsum("kti,tij->ktj", picked, tiles, preferred_element_type=jnp.float32)
    col_hot = (cols[0][:, None] == jnp.arange(count_cols, dtype=jnp.int32)[None, :]).astype(
        jnp.float32
    ) * keep[:, None]
    placed = jnp.einsum("ktj,tb->kbj", mirror, col_hot, precision=lax.Precision.HIGHEST)
    return placed.reshape(width, count_cols * size)


def sum_rows(direct):
    return lax.psum_scatter(direct, "col", scatter_dimension=1, tiled=True)


def sum_cols(mirror):
    return lax.psum_scatter(mirror, "row", scatter_dimension=1, tiled=True)


def gather_rowset(vec):
    return lax.all_gather(vec, "col", axis=1, tiled=True)


def both_halves(vec, rowset, tiles, tile_rows, tile_cols, tile_live):
    size = tiles.shape[1]
    count = tiles.shape[0]
    keep = (jnp.arange(count, dtype=jnp.int32) < tile_live[0]).astype(jnp.float32)
    colset = lax.all_gather(vec, "row", axis=1, tiled=True)
    count_rows = rowset.shape[1] // size
    count_cols = colset.shape[1] // size
    direct = half_direct(colset, tiles, (tile_rows, tile_cols), keep, count_rows)
    mirror = half_mirror(rowset, tiles, (tile_cols, tile_rows), keep, count_cols)
    return (direct, sum_cols(mirror))


def local(vectors, tiles, tile_rows, tile_cols, tile_live):
    direct, own_cols = both_halves(
        vectors, gather_rowset(vectors), tiles, tile_rows, tile_cols, tile_live
    )
    first = (sum_rows(direct) + own_cols).astype(jnp.bfloat16)
    next_rowset = gather_rowset(first)
    direct_two, cols_two = both_halves(first, next_rowset, tiles, tile_rows, tile_cols, tile_live)
    second_f = 2.0 * (sum_rows(direct_two) + cols_two) - vectors.astype(jnp.float32)
    return (first, second_f.astype(jnp.bfloat16))


def solution(mesh):
    placed = (
        P(None, ("row", "col")),
        P(("row", "col"), None, None),
        P(("row", "col")),
        P(("row", "col")),
        P(("row", "col")),
    )
    return jax.shard_map(
        local,
        mesh=mesh,
        in_specs=placed,
        out_specs=(P(None, ("row", "col")), P(None, ("row", "col"))),
        check_vma=False,
    )
```

profile of v0, /device:TPU:0, one launch (start us, length us, event | category | flops | bytes accessed | tf_op | source)
XLA Modules:
  0.0 261.5 jit_solution(1111360292076652762)
XLA Ops:
  7.2 0.8 compare_select_fusion
  8.0 0.7 compare_and_fusion
  9.4 32.5 %all_gather.13 = bf16[32,2048]{1,0:T(8,128)(2,1)S(1)} all-gather(bf16[32,256]{1,0:T(8,128)(2,1)} %param.9), channel_id=1, replica_groups=mesh['row'=4,'col'=8] {'col'}, dimensions={1}, use_global_device_ids=true | all-gather | bytes 147456 | tf_op jit(solution)/shard_map/all_gather | solution.py:40
  41.9 0.6 gather_fusion.1
  43.0 0.6 fusion.4
  43.7 0.7 copy.20
  44.4 5.2 %all_gather.12 = bf16[32,1024]{1,0:T(8,128)(2,1)S(1)} all-gather(bf16[32,256]{1,0:T(8,128)(2,1)S(1)} %copy-done.2), channel_id=1, replica_groups=mesh['row'=4,'col'=8] {'row'}, dimensions={1}, use_global_device_ids=true | all-gather | bytes 81920 | tf_op jit(solution)/shard_map/all_gather | solution.py:47
  49.7 0.6 gather_fusion
  50.3 0.7 convolution_bitcast_fusion.3
  51.0 0.7 fusion.6
  51.7 0.8 copy.19
  52.5 12.5 %reduce-scatter.7.cloned.1.call-done = f32[32,256]{1,0:T(8,128)} async-done(((f32[32,1024]{1,0:T(8,128)}), f32[32,256]{1,0:T(8,128)}) %reduce-scatter.7.cloned.1.call-update) | async-done | bytes 32784 | tf_op jit(solution)/shard_map/reduce_scatter | solution.py:36
  65.0 65.4 %reduce-scatter.5.cloned.1.call-done = f32[32,256]{1,0:T(8,128)} async-done(((f32[32,2048]{1,0:T(8,128)}), f32[32,256]{1,0:T(8,128)}) %reduce-scatter.5.cloned.1.call-update) | async-done | bytes 32784 | tf_op jit(solution)/shard_map/reduce_scatter | solution.py:32
  130.4 0.8 add_convert_fusion
  131.2 5.2 %all_gather.14 = bf16[32,1024]{1,0:T(8,128)(2,1)S(1)} all-gather(bf16[32,256]{1,0:T(8,128)(2,1)S(1)} %add_convert_fusion), channel_id=1, replica_groups=mesh['row'=4,'col'=8] {'row'}, dimensions={1}, use_global_device_ids=true | all-gather | bytes 81920 | tf_op jit(solution)/shard_map/all_gather | solution.py:47
  136.4 30.5 %all_gather.15 = bf16[32,2048]{1,0:T(8,128)(2,1)S(1)} all-gather(bf16[32,256]{1,0:T(8,128)(2,1)S(1)} %add_convert_fusion), channel_id=1, replica_groups=mesh['row'=4,'col'=8] {'col'}, dimensions={1}, use_global_device_ids=true | all-gather | bytes 147456 | tf_op jit(solution)/shard_map/all_gather | solution.py:40
  168.6 0.6 fusion
  169.3 0.7 copy.22
  170.0 0.7 convolution_bitcast_fusion.1
  170.7 0.7 fusion.2
  171.4 0.8 copy.21
  172.2 16.5 %reduce-scatter.11.cloned.1.call-done = f32[32,256]{1,0:T(8,128)} async-done(((f32[32,1024]{1,0:T(8,128)}), f32[32,256]{1,0:T(8,128)}) %reduce-scatter.11.cloned.1.call-update) | async-done | bytes 32784 | tf_op jit(solution)/shard_map/reduce_scatter | solution.py:36
  188.7 64.9 %reduce-scatter.9.cloned.1.call-done = f32[32,256]{1,0:T(8,128)} async-done(((f32[32,2048]{1,0:T(8,128)}), f32[32,256]{1,0:T(8,128)}) %reduce-scatter.9.cloned.1.call-update) | async-done | bytes 32784 | tf_op jit(solution)/shard_map/reduce_scatter | solution.py:32
  253.6 1.4 subtract_convert_fusion
  (31 shorter events, 2.5 us)
Async XLA Ops:
  7.2 35.3 %copy-start = (bf16[16,256,256]{2,1,0:T(8,128)(2,1)S(1)}, bf16[16,256,256]{2,1,0:T(8,128)(2,1)}, u32[]{:S(2)}) copy-start(bf16[16,256,256]{2,1,0:T(8,128)(2,1)} %param.10) | copy-start | bytes 6291460
  7.2 35.8 %copy-start.3 = (s32[16]{0:T(128)S(1)}, s32[16]{0:T(128)}, u32[]{:S(2)}) copy-start(s32[16]{0:T(128)} %param.12) | copy-start | bytes 196
  7.2 57.8 %reduce-scatter.7.cloned.1.call-start = ((), (), s32[]{:S(2)}) async-start(), calls=%async_computation.5 | async-start | bytes 163840 | tf_op jit(solution)/shard_map/reduce_scatter | solution.py:36
  42.5 1.9 copy-start.2
  43.7 7.4 %copy-start.4 = (s32[16]{0:T(128)S(1)}, s32[16]{0:T(128)}, u32[]{:S(2)}) copy-start(s32[16]{0:T(128)} %param.11) | copy-start | bytes 196
  44.4 86.0 %reduce-scatter.5.cloned.1.call-start = ((), (), s32[]{:S(2)}) async-start(), calls=%async_computation.4 | async-start | bytes 294912 | tf_op jit(solution)/shard_map/reduce_scatter | solution.py:32
  52.5 136.2 %reduce-scatter.11.cloned.1.call-start = ((), (), s32[]{:S(2)}) async-start(), calls=%async_computation.7 | async-start | bytes 163840 | tf_op jit(solution)/shard_map/reduce_scatter | solution.py:36
  131.2 37.4 %copy-start.1 = (bf16[32,256]{1,0:T(8,128)(2,1)}, bf16[32,256]{1,0:T(8,128)(2,1)S(1)}, u32[]{:S(2)}) copy-start(bf16[32,256]{1,0:T(8,128)(2,1)S(1)} %add_convert_fusion) | copy-start | bytes 49156
  170.0 83.6 %reduce-scatter.9.cloned.1.call-start = ((), (), s32[]{:S(2)}) async-start(), calls=%async_computation.6 | async-start | bytes 294912 | tf_op jit(solution)/shard_map/reduce_scatter | solution.py:32
Sparse Core Ops, SparseCore 0:
  44.5 20.4 reduce-scatter.6
  68.7 61.6 reduce-scatter.4
  170.1 18.5 reduce-scatter.10
  191.9 61.6 reduce-scatter.8
where the time goes:
time: 262 us
  waiting for transfers between devices  159 us (61%)
  blocking collectives  73.5 us (28%)
  between operations  14.6 us (6%)
  local copies, waits for them, and re-layouts  5.23 us (2%)
  matrix products  5.03 us (2%)
  other arithmetic  3.65 us (1%)
    reduce_scatter x2, waiting for transfers between devices, sum_rows(): return lax.psum_scatter(direct, 'col', scatter_dimension=1, tiled=True)  130 us
    all_gather x2, blocking collectives, gather_rowset(): return lax.all_gather(vec, 'col', axis=1, tiled=True)  63 us
    reduce_scatter x2, waiting for transfers between devices, sum_cols(): return lax.psum_scatter(mirror, 'row', scatter_dimension=1, tiled=True)  29 us
    all_gather x2, blocking collectives, both_halves(): colset = lax.all_gather(vec, 'row', axis=1, tiled=True)  10.5 us
  transfers between devices with their start and end apart: 4, of which 4 were waited for; matrix products, arithmetic and copies ran while one was open for 2% of the time, Pallas kernels for 0%

commit v1 on v0

v1 whole, which is shorter than its diff:
```python
import functools

import jax
import jax.numpy as jnp
from jax import lax
from jax.experimental import pallas as pl
from jax.experimental.pallas import tpu as pltpu
from jax.sharding import PartitionSpec as P


def digits_of(count):
    out, stride, rest, prime = [], 1, count, 2
    while rest > 1:
        while rest % prime:
            prime += 1
        out.append((stride, prime))
        stride, rest = stride * prime, rest // prime
    return out


def moved(index, stride, radix, step):
    digit = index // stride % radix
    return index + ((digit + step) % radix - digit) * stride


def send(value, axis, count, stride, radix, step):
    pairs = [(i, moved(i, stride, radix, step)) for i in range(count)]
    return lax.ppermute(value, axis, pairs)


def gather(block, axis, count):
    pieces = [block[None]]
    for stride, radix in reversed(digits_of(count)):
        held = pieces[0] if len(pieces) == 1 else jnp.concatenate(pieces, 0)
        for step in range(1, radix):
            pieces.append(send(held, axis, count, stride, radix, -step))
    return pieces


def slots_of(count):
    slots = [()]
    for _, radix in reversed(digits_of(count)):
        slots = [(step,) + rest for step in range(radix) for rest in slots]
    return slots


def slot_index(me, count, steps):
    for (stride, radix), step in zip(digits_of(count), steps):
        if step:
            me = moved(me, stride, radix, step)
    return me


def sizes_of(count):
    sizes, held = [1], 1
    for _, radix in reversed(digits_of(count)):
        sizes += [held] * (radix - 1)
        held *= radix
    return sizes


def scatter(pieces, axis, count):
    for stride, radix in digits_of(count):
        keep = pieces[: len(pieces) - (radix - 1)]
        sent = pieces[len(keep) :]
        got = [send(value, axis, count, stride, radix, step + 1) for step, value in enumerate(sent)]
        at, pieces = 0, []
        for value in keep:
            size = value.shape[0]
            for other in got:
                value = value + other[at : at + size]
            at += size
            pieces.append(value)
    return pieces[0][0]


def kernel(me_ref, take_ref, put_ref, live_ref, *refs, n_in, counts, axes, direct):
    pieces, tiles_ref, outs = refs[:n_in], refs[n_in], refs[n_in + 1 : -2]
    vec, acc = refs[-2:]
    count_in, count_out = counts
    me_in, me_out = me_ref[0], me_ref[1]
    slots = iter(slots_of(count_in))
    for piece in pieces:
        for i in range(piece.shape[0]):
            vec[slot_index(me_in, count_in, next(slots))] = piece[i]
    acc[...] = jnp.zeros_like(acc)
    dims = (((1,), (1,)), ((), ())) if direct else (((1,), (0,)), ((), ()))
    live = live_ref[0]
    for t in range(tiles_ref.shape[0]):
        x = vec[take_ref[t]]
        y = lax.dot_general(x, tiles_ref[t], dims, preferred_element_type=jnp.float32)
        acc[put_ref[t]] += jnp.where(t < live, y, 0.0)
    slots = iter(slots_of(count_out))
    for out in outs:
        for i in range(out.shape[0]):
            out[i] = acc[slot_index(me_out, count_out, next(slots))]


def half(me, pieces, tiles, take, put, live, counts, direct):
    width, size = pieces[0].shape[1:]
    smem = pl.BlockSpec(memory_space=pltpu.SMEM)
    vmem = pl.BlockSpec(memory_space=pltpu.VMEM)
    sizes = sizes_of(counts[1])
    return pl.pallas_call(
        functools.partial(kernel, n_in=len(pieces), counts=counts, axes=None, direct=direct),
        out_shape=[jax.ShapeDtypeStruct((n, width, size), jnp.float32) for n in sizes],
        in_specs=[smem] * 4 + [vmem] * (len(pieces) + 1),
        out_specs=[vmem] * len(sizes),
        scratch_shapes=[
            pltpu.VMEM((counts[0], width, size), jnp.bfloat16),
            pltpu.VMEM((counts[1], width, size), jnp.float32),
        ],
        name="direct" if direct else "mirror",
    )(me, take, put, live, *pieces, tiles)


def local(rows, cols, vectors, tiles, tile_rows, tile_cols, tile_live):
    r, c = lax.axis_index("row"), lax.axis_index("col")
    me_direct = jnp.stack([r, c]).astype(jnp.int32)
    me_mirror = jnp.stack([c, r]).astype(jnp.int32)

    def apply(vec):
        colset = gather(vec, "row", rows)
        rowset = gather(vec, "col", cols)
        direct = half(me_direct, colset, tiles, tile_cols, tile_rows, tile_live, (rows, cols), True)
        mirror = half(me_mirror, rowset, tiles, tile_rows, tile_cols, tile_live, (cols, rows), False)
        return scatter(list(direct), "col", cols) + scatter(list(mirror), "row", rows)

    first = apply(vectors).astype(jnp.bfloat16)
    second = 2.0 * apply(first) - vectors.astype(jnp.float32)
    return first, second.astype(jnp.bfloat16)


def solution(mesh):
    both = ("row", "col")
    placed = (P(None, both), P(both, None, None), P(both), P(both), P(both))
    return jax.shard_map(
        functools.partial(local, mesh.shape["row"], mesh.shape["col"]),
        mesh=mesh,
        in_specs=placed,
        out_specs=(P(None, both), P(None, both)),
        check_vma=False,
    )
```

time: 262 us -> 70.9 us (0.27)
  waiting for transfers between devices: 159 us -> 28.4 us
  blocking collectives: 73.5 us -> 0 us
  starting transfers between devices: 0.16 us -> 19.5 us
  between operations: 14.6 us -> 1.44 us
  Pallas kernels: 0 us -> 11.9 us
  matrix products: 5.03 us -> 0 us
  other arithmetic: 3.65 us -> 6.4 us
  local copies, waits for them, and re-layouts: 5.23 us -> 2.55 us
    reduce_scatter x4 -> x0, waiting for transfers between devices: 159 us -> none  [the longest x2 130 us: sum_rows(): return lax.psum_scatter(direct, 'col', scatter_dimension=1, tiled=True)]
    all_gather x4 -> x0, blocking collectives: 73.5 us -> none  [the longest x2 63 us: gather_rowset(): return lax.all_gather(vec, 'col', axis=1, tiled=True)]
    ppermute x0 -> x20, waiting for transfers between devices: none -> 28.4 us  [send(): return lax.ppermute(value, axis, pairs)]
    ppermute x0 -> x20, starting transfers between devices: none -> 19.5 us  [send(): return lax.ppermute(value, axis, pairs)]
    pallas_call x0 -> x4, Pallas kernels: none -> 11.9 us  [half(): pl.pallas_call(functools.partial(kernel, n_in=len(pieces), counts=counts,...]
    dot_general x8 -> x0, matrix products: 5.03 us -> none  [the longest x2 1.43 us: half_direct(): jnp.einsum('ktj,tij->kti', picked, tiles, preferred_element_type=jnp.floa...]
  transfers between devices with their start and end apart: 4 -> 20, of which waited for: 4 -> 15; matrix products, arithmetic and copies ran while one was open for 2% -> 5% of each run, Pallas kernels for 0% -> 17%
where the time goes in v1:
time: 70.9 us; the launch traced here: 70.2 us
  waiting for transfers between devices  28.4 us (40%)
  starting transfers between devices  19.5 us (28%)
  Pallas kernels  11.9 us (17%)
  other arithmetic  6.4 us (9%)
  local copies, waits for them, and re-layouts  2.55 us (4%)
  between operations  1.44 us (2%)
    ppermute x20, waiting for transfers between devices, send(): return lax.ppermute(value, axis, pairs)  28.4 us
    ppermute x20, starting transfers between devices, send(): return lax.ppermute(value, axis, pairs)  19.5 us
    pallas_call x4, Pallas kernels, half(): pl.pallas_call(functools.partial(kernel, n_in=len(pieces), counts=counts,...  11.9 us
    unnamed x38, local copies, waits for them, and re-layouts  2.55 us
    add x6, other arithmetic, scatter(): value = value + other[at:at + size]  1.57 us
    concatenate x4, other arithmetic, gather(): held = pieces[0] if len(pieces) == 1 else jnp.concatenate(pieces, 0)  1.48 us
  transfers between devices with their start and end apart: 20, of which 15 were waited for; matrix products, arithmetic and copies ran while one was open for 5% of the time, Pallas kernels for 17%

profile of v1, /device:TPU:0, one launch (start us, length us, event | category | flops | bytes accessed | tf_op | source)
XLA Modules:
  0.0 70.2 jit_solution(6265475148975066844)
XLA Ops:
  0.6 4.1 %collective-permute-start.5 = (bf16[1,32,256]{2,1,0:T(8,128)(2,1)}, bf16[1,32,256]{2,1,0:T(8,128)(2,1)S(1)}, u32[]{:S(2)}, u32[]{:S(2)}) collective-permute-start(bf16[1,32,256]{2,1,0:T(8,128)(2,1)} %bitcast.10), channel_id=1, source_target_pairs={{0,4},{1,5},{2,6},{3,7},{4,0},{5,1},{6,2},{7,3},{8,12},{9,13},{10,... | collective-permute-start | bytes 49160 | tf_op jit(solution)/shard_map/ppermute | solution.py:28
  4.7 1.5 %collective-permute-start = (bf16[1,32,256]{2,1,0:T(8,128)(2,1)}, bf16[1,32,256]{2,1,0:T(8,128)(2,1)S(1)}, u32[]{:S(2)}, u32[]{:S(2)}) collective-permute-start(bf16[1,32,256]{2,1,0:T(8,128)(2,1)} %bitcast.11), channel_id=1, source_target_pairs={{0,16},{8,24},{16,0},{24,8},{1,17},{9,25},{17,1},{25,9},{2,18},{10... | collective-permute-start | bytes 49160 | tf_op jit(solution)/shard_map/ppermute | solution.py:28
  6.7 2.0 %collective-permute-done.refs_1_ = bf16[1,32,256]{2,1,0:T(8,128)(2,1)S(1)} collective-permute-done((bf16[1,32,256]{2,1,0:T(8,128)(2,1)}, bf16[1,32,256]{2,1,0:T(8,128)(2,1)S(1)}, u32[]{:S(2)}, u32[]{:S(2)}) %collective-permute-start) | collective-permute-done | bytes 16416 | tf_op jit(solution)/shard_map/ppermute | solution.py:28
  9.4 1.6 %collective-permute-start.6 = (bf16[2,32,256]{2,1,0:T(8,128)(2,1)S(1)}, bf16[2,32,256]{2,1,0:T(8,128)(2,1)S(1)}, u32[]{:S(2)}, u32[]{:S(2)}) collective-permute-start(bf16[2,32,256]{2,1,0:T(8,128)(2,1)S(1)} %get-tuple-element.33), channel_id=1, source_target_pairs={{0,2},{1,3},{2,0},{3,1},{4,6},{5,7},{6,4},{7,5},{8,10},{9,11},{10,... | collective-permute-start | bytes 98312 | tf_op jit(solution)/shard_map/ppermute | solution.py:28
  12.9 3.1 %direct.2 = (f32[1,32,256]{2,1,0:T(8,128)}, f32[1,32,256]{2,1,0:T(8,128)}, f32[2,32,256]{2,1,0:T(8,128)}, f32[4,32,256]{2,1,0:T(8,128)}) custom-call(s32[2]{0:T(128)} %pad_add_fusion.me_ref, s32[16]{0:T(128)} %put_ref.7, s32[16]{0:T(128)} %take_ref.7, s32[1]{0:T(128)S(6)} %copy.7.live_ref, bf16[1,32,256]{2,1,0:T(8,128)(2,1)} %bitcast.13, ...), custom_call_target="tpu_custom_call" | custom-call | tf_op jit(solution)/shard_map/direct/pallas_call | solution.py:104
  16.0 1.6 %collective-permute-start.2 = (f32[4,32,256]{2,1,0:T(8,128)}, f32[4,32,256]{2,1,0:T(8,128)S(1)}, u32[]{:S(2)}, u32[]{:S(2)}) collective-permute-start(f32[4,32,256]{2,1,0:T(8,128)} %get-tuple-element.17), channel_id=1, source_target_pairs={{0,1},{1,0},{2,3},{3,2},{4,5},{5,4},{6,7},{7,6},{8,9},{9,8},{10,11... | collective-permute-start | bytes 393224 | tf_op jit(solution)/shard_map/ppermute | solution.py:28
  18.8 4.5 %collective-permute-done.7.refs_3_ = bf16[4,32,256]{2,1,0:T(8,128)(2,1)S(1)} collective-permute-done((bf16[4,32,256]{2,1,0:T(8,128)(2,1)S(1)}, bf16[4,32,256]{2,1,0:T(8,128)(2,1)S(1)}, u32[]{:S(2)}, u32[]{:S(2)}) %collective-permute-start.7) | collective-permute-done | bytes 65568 | tf_op jit(solution)/shard_map/ppermute | solution.py:28
  23.9 2.9 %mirror.2 = (f32[1,32,256]{2,1,0:T(8,128)}, f32[1,32,256]{2,1,0:T(8,128)}, f32[2,32,256]{2,1,0:T(8,128)}) custom-call(s32[2]{0:T(128)} %pad_add_fusion.1.me_ref, s32[16]{0:T(128)} %take_ref.7, s32[16]{0:T(128)} %put_ref.7, s32[1]{0:T(128)S(6)} %copy.7.live_ref, bf16[1,32,256]{2,1,0:T(8,128)(2,1)} %bitcast.14, bf16[1,32,256]{2,1,0:T(8,128)(2,1)} %copy-done.3, ...), custom_call_target="tpu_custom_call" | custom-call | tf_op jit(solution)/shard_map/mirror/pallas_call | solution.py:104
  27.4 0.9 %collective-permute-done.8 = f32[2,32,256]{2,1,0:T(8,128)S(1)} collective-permute-done((f32[2,32,256]{2,1,0:T(8,128)}, f32[2,32,256]{2,1,0:T(8,128)S(1)}, u32[]{:S(2)}, u32[]{:S(2)}) %collective-permute-start.8) | collective-permute-done | bytes 65568 | tf_op jit(solution)/shard_map/ppermute | solution.py:28
  29.0 1.5 %collective-permute-start.9 = (f32[1,32,256]{2,1,0:T(8,128)S(1)}, f32[1,32,256]{2,1,0:T(8,128)S(1)}, u32[]{:S(2)}, u32[]{:S(2)}) collective-permute-start(f32[1,32,256]{2,1,0:T(8,128)S(1)} %slice_add_fusion.8), channel_id=1, source_target_pairs={{0,16},{8,24},{16,0},{24,8},{1,17},{9,25},{17,1},{25,9},{2,18},{10... | collective-permute-start | bytes 98312 | tf_op jit(solution)/shard_map/ppermute | solution.py:28
  31.4 1.0 %collective-permute-start.4 = (f32[1,32,256]{2,1,0:T(8,128)S(1)}, f32[1,32,256]{2,1,0:T(8,128)S(1)}, u32[]{:S(2)}, u32[]{:S(2)}) collective-permute-start(f32[1,32,256]{2,1,0:T(8,128)S(1)} %slice_add_fusion.10), channel_id=1, source_target_pairs={{0,4},{1,5},{2,6},{3,7},{4,0},{5,1},{6,2},{7,3},{8,12},{9,13},{10,... | collective-permute-start | bytes 98312 | tf_op jit(solution)/shard_map/ppermute | solution.py:28
  33.0 3.6 %collective-permute-done.4 = f32[1,32,256]{2,1,0:T(8,128)S(1)} collective-permute-done((f32[1,32,256]{2,1,0:T(8,128)S(1)}, f32[1,32,256]{2,1,0:T(8,128)S(1)}, u32[]{:S(2)}, u32[]{:S(2)}) %collective-permute-start.4) | collective-permute-done | bytes 32800 | tf_op jit(solution)/shard_map/ppermute | solution.py:28
  37.3 1.6 %collective-permute-start.10 = (bf16[1,32,256]{2,1,0:T(8,128)(2,1)S(1)}, bf16[1,32,256]{2,1,0:T(8,128)(2,1)S(1)}, u32[]{:S(2)}, u32[]{:S(2)}) collective-permute-start(bf16[1,32,256]{2,1,0:T(8,128)(2,1)S(1)} %fusion.9.refs_0_), channel_id=1, source_target_pairs={{0,16},{8,24},{16,0},{24,8},{1,17},{9,25},{17,1},{25,9},{2,18},{10... | collective-permute-start | bytes 49160 | tf_op jit(solution)/shard_map/ppermute | solution.py:28
  39.6 1.5 %collective-permute-done.10.refs_1_ = bf16[1,32,256]{2,1,0:T(8,128)(2,1)S(1)} collective-permute-done((bf16[1,32,256]{2,1,0:T(8,128)(2,1)S(1)}, bf16[1,32,256]{2,1,0:T(8,128)(2,1)S(1)}, u32[]{:S(2)}, u32[]{:S(2)}) %collective-permute-start.10) | collective-permute-done | bytes 16416 | tf_op jit(solution)/shard_map/ppermute | solution.py:28
  41.1 2.4 %collective-permute-done.15.refs_1_ = bf16[1,32,256]{2,1,0:T(8,128)(2,1)S(1)} collective-permute-done((bf16[1,32,256]{2,1,0:T(8,128)(2,1)S(1)}, bf16[1,32,256]{2,1,0:T(8,128)(2,1)S(1)}, u32[]{:S(2)}, u32[]{:S(2)}) %collective-permute-start.15) | collective-permute-done | bytes 16416 | tf_op jit(solution)/shard_map/ppermute | solution.py:28
  43.9 0.9 %collective-permute-done.11.refs_2_ = bf16[2,32,256]{2,1,0:T(8,128)(2,1)S(1)} collective-permute-done((bf16[2,32,256]{2,1,0:T(8,128)(2,1)S(1)}, bf16[2,32,256]{2,1,0:T(8,128)(2,1)S(1)}, u32[]{:S(2)}, u32[]{:S(2)}) %collective-permute-start.11) | collective-permute-done | bytes 32800 | tf_op jit(solution)/shard_map/ppermute | solution.py:28
  45.4 3.1 %direct.3 = (f32[1,32,256]{2,1,0:T(8,128)}, f32[1,32,256]{2,1,0:T(8,128)}, f32[2,32,256]{2,1,0:T(8,128)}, f32[4,32,256]{2,1,0:T(8,128)}) custom-call(s32[2]{0:T(128)} %pad_add_fusion.me_ref, s32[16]{0:T(128)} %put_ref.7, s32[16]{0:T(128)} %take_ref.7, s32[1]{0:T(128)S(6)} %copy.7.live_ref, bf16[1,32,256]{2,1,0:T(8,128)(2,1)} %copy-done.2, ...), custom_call_target="tpu_custom_call" | custom-call | tf_op jit(solution)/shard_map/direct/pallas_call | solution.py:104
  48.5 1.6 %collective-permute-start.12 = (f32[4,32,256]{2,1,0:T(8,128)}, f32[4,32,256]{2,1,0:T(8,128)S(1)}, u32[]{:S(2)}, u32[]{:S(2)}) collective-permute-start(f32[4,32,256]{2,1,0:T(8,128)} %get-tuple-element.24), channel_id=1, source_target_pairs={{0,1},{1,0},{2,3},{3,2},{4,5},{5,4},{6,7},{7,6},{8,9},{9,8},{10,11... | collective-permute-start | bytes 393224 | tf_op jit(solution)/shard_map/ppermute | solution.py:28
  51.4 4.4 %collective-permute-done.17.refs_3_ = bf16[4,32,256]{2,1,0:T(8,128)(2,1)S(1)} collective-permute-done((bf16[4,32,256]{2,1,0:T(8,128)(2,1)S(1)}, bf16[4,32,256]{2,1,0:T(8,128)(2,1)S(1)}, u32[]{:S(2)}, u32[]{:S(2)}) %collective-permute-start.17) | collective-permute-done | bytes 65568 | tf_op jit(solution)/shard_map/ppermute | solution.py:28
  56.4 2.9 %mirror.3 = (f32[1,32,256]{2,1,0:T(8,128)}, f32[1,32,256]{2,1,0:T(8,128)}, f32[2,32,256]{2,1,0:T(8,128)}) custom-call(s32[2]{0:T(128)} %pad_add_fusion.1.me_ref, s32[16]{0:T(128)} %take_ref.7, s32[16]{0:T(128)} %put_ref.7, s32[1]{0:T(128)S(6)} %copy.7.live_ref, bf16[1,32,256]{2,1,0:T(8,128)(2,1)} %copy-done.2, bf16[1,32,256]{2,1,0:T(8,128)(2,1)} %copy-done.4, ...), custom_call_target="tpu_custom_call" | custom-call | tf_op jit(solution)/shard_map/mirror/pallas_call | solution.py:104
  59.3 1.0 %collective-permute-start.13 = (f32[2,32,256]{2,1,0:T(8,128)S(1)}, f32[2,32,256]{2,1,0:T(8,128)S(1)}, u32[]{:S(2)}, u32[]{:S(2)}) collective-permute-start(f32[2,32,256]{2,1,0:T(8,128)S(1)} %slice_add_fusion), channel_id=1, source_target_pairs={{0,2},{1,3},{2,0},{3,1},{4,6},{5,7},{6,4},{7,5},{8,10},{9,11},{10,... | collective-permute-start | bytes 196616 | tf_op jit(solution)/shard_map/ppermute | solution.py:28
  62.1 1.8 %collective-permute-done.13 = f32[2,32,256]{2,1,0:T(8,128)S(1)} collective-permute-done((f32[2,32,256]{2,1,0:T(8,128)S(1)}, f32[2,32,256]{2,1,0:T(8,128)S(1)}, u32[]{:S(2)}, u32[]{:S(2)}) %collective-permute-start.13) | collective-permute-done | bytes 65568 | tf_op jit(solution)/shard_map/ppermute | solution.py:28
  65.4 3.4 %collective-permute-done.14 = f32[1,32,256]{2,1,0:T(8,128)S(1)} collective-permute-done((f32[1,32,256]{2,1,0:T(8,128)S(1)}, f32[1,32,256]{2,1,0:T(8,128)S(1)}, u32[]{:S(2)}, u32[]{:S(2)}) %collective-permute-start.14) | collective-permute-done | bytes 32800 | tf_op jit(solution)/shard_map/ppermute | solution.py:28
  68.8 1.4 %fusion.5 = bf16[32,256]{1,0:T(8,128)(2,1)} fusion(f32[1,32,256]{2,1,0:T(8,128)S(1)} %collective-permute-done.19, f32[1,32,256]{2,1,0:T(8,128)} %get-tuple-element.27, f32[2,32,256]{2,1,0:T(8,128)S(1)} %collective-permute-done.18, f32[1,32,256]{2,1,0:T(8,128)S(1)} %collective-permute-done.14, f32[2,32,256]{2,1,0:T(8,128)S(1)} %collective-permute-done.13, ...), kind=kLoop, calls=%fused_computation.15 | loop fusion | flops 81920 | bytes 262144 | tf_op jit(solution)/shard_map/convert_element_type | solution.py:131
  (72 shorter events, 14.6 us)
Async XLA Ops:
  0.6 17.0 %copy-start = (bf16[32,256]{1,0:T(8,128)(2,1)S(1)}, bf16[32,256]{1,0:T(8,128)(2,1)}, u32[]{:S(2)}) copy-start(bf16[32,256]{1,0:T(8,128)(2,1)} %param.5) | copy-start | bytes 49156
  0.6 6.0 %collective-permute-start.5 = (bf16[1,32,256]{2,1,0:T(8,128)(2,1)}, bf16[1,32,256]{2,1,0:T(8,128)(2,1)S(1)}, u32[]{:S(2)}, u32[]{:S(2)}) collective-permute-start(bf16[1,32,256]{2,1,0:T(8,128)(2,1)} %bitcast.10), channel_id=1, source_target_pairs={{0,4},{1,5},{2,6},{3,7},{4,0},{5,1},{6,2},{7,3},{8,12},{9,13},{10,... | collective-permute-start | bytes 49160 | tf_op jit(solution)/shard_map/ppermute | solution.py:28
  4.7 3.9 %collective-permute-start = (bf16[1,32,256]{2,1,0:T(8,128)(2,1)}, bf16[1,32,256]{2,1,0:T(8,128)(2,1)S(1)}, u32[]{:S(2)}, u32[]{:S(2)}) collective-permute-start(bf16[1,32,256]{2,1,0:T(8,128)(2,1)} %bitcast.11), channel_id=1, source_target_pairs={{0,16},{8,24},{16,0},{24,8},{1,17},{9,25},{17,1},{25,9},{2,18},{10... | collective-permute-start | bytes 49160 | tf_op jit(solution)/shard_map/ppermute | solution.py:28
  9.4 2.9 %collective-permute-start.1 = (bf16[2,32,256]{2,1,0:T(8,128)(2,1)S(1)}, bf16[2,32,256]{2,1,0:T(8,128)(2,1)S(1)}, u32[]{:S(2)}, u32[]{:S(2)}) collective-permute-start(bf16[2,32,256]{2,1,0:T(8,128)(2,1)S(1)} %get-tuple-element.32), channel_id=1, source_target_pairs={{0,8},{8,0},{16,24},{24,16},{1,9},{9,1},{17,25},{25,17},{2,10},{10... | collective-permute-start | bytes 98312 | tf_op jit(solution)/shard_map/ppermute | solution.py:28
  9.4 8.2 %collective-permute-start.6 = (bf16[2,32,256]{2,1,0:T(8,128)(2,1)S(1)}, bf16[2,32,256]{2,1,0:T(8,128)(2,1)S(1)}, u32[]{:S(2)}, u32[]{:S(2)}) collective-permute-start(bf16[2,32,256]{2,1,0:T(8,128)(2,1)S(1)} %get-tuple-element.33), channel_id=1, source_target_pairs={{0,2},{1,3},{2,0},{3,1},{4,6},{5,7},{6,4},{7,5},{8,10},{9,11},{10,... | collective-permute-start | bytes 98312 | tf_op jit(solution)/shard_map/ppermute | solution.py:28
  16.0 20.5 %copy-start.15 = (f32[1,32,256]{2,1,0:T(8,128)S(1)}, f32[1,32,256]{2,1,0:T(8,128)}, u32[]{:S(2)}) copy-start(f32[1,32,256]{2,1,0:T(8,128)} %get-tuple-element.16) | copy-start | bytes 98308
  16.0 10.8 %collective-permute-start.2 = (f32[4,32,256]{2,1,0:T(8,128)}, f32[4,32,256]{2,1,0:T(8,128)S(1)}, u32[]{:S(2)}, u32[]{:S(2)}) collective-permute-start(f32[4,32,256]{2,1,0:T(8,128)} %get-tuple-element.17), channel_id=1, source_target_pairs={{0,1},{1,0},{2,3},{3,2},{4,5},{5,4},{6,7},{7,6},{8,9},{9,8},{10,11... | collective-permute-start | bytes 393224 | tf_op jit(solution)/shard_map/ppermute | solution.py:28
  17.7 5.6 %collective-permute-start.7 = (bf16[4,32,256]{2,1,0:T(8,128)(2,1)S(1)}, bf16[4,32,256]{2,1,0:T(8,128)(2,1)S(1)}, u32[]{:S(2)}, u32[]{:S(2)}) collective-permute-start(bf16[4,32,256]{2,1,0:T(8,128)(2,1)S(1)} %pad_maximum_fusion), channel_id=1, source_target_pairs={{0,1},{1,0},{2,3},{3,2},{4,5},{5,4},{6,7},{7,6},{8,9},{9,8},{10,11... | collective-permute-start | bytes 196616 | tf_op jit(solution)/shard_map/ppermute | solution.py:28
  26.8 1.5 %collective-permute-start.8 = (f32[2,32,256]{2,1,0:T(8,128)}, f32[2,32,256]{2,1,0:T(8,128)S(1)}, u32[]{:S(2)}, u32[]{:S(2)}) collective-permute-start(f32[2,32,256]{2,1,0:T(8,128)} %get-tuple-element.21), channel_id=1, source_target_pairs={{0,8},{8,0},{16,24},{24,16},{1,9},{9,1},{17,25},{25,17},{2,10},{10... | collective-permute-start | bytes 196616 | tf_op jit(solution)/shard_map/ppermute | solution.py:28
  26.8 4.6 %collective-permute-start.3 = (f32[2,32,256]{2,1,0:T(8,128)S(1)}, f32[2,32,256]{2,1,0:T(8,128)S(1)}, u32[]{:S(2)}, u32[]{:S(2)}) collective-permute-start(f32[2,32,256]{2,1,0:T(8,128)S(1)} %slice_add_fusion.1), channel_id=1, source_target_pairs={{0,2},{1,3},{2,0},{3,1},{4,6},{5,7},{6,4},{7,5},{8,10},{9,11},{10,... | collective-permute-start | bytes 196616 | tf_op jit(solution)/shard_map/ppermute | solution.py:28
  29.0 3.9 %collective-permute-start.9 = (f32[1,32,256]{2,1,0:T(8,128)S(1)}, f32[1,32,256]{2,1,0:T(8,128)S(1)}, u32[]{:S(2)}, u32[]{:S(2)}) collective-permute-start(f32[1,32,256]{2,1,0:T(8,128)S(1)} %slice_add_fusion.8), channel_id=1, source_target_pairs={{0,16},{8,24},{16,0},{24,8},{1,17},{9,25},{17,1},{25,9},{2,18},{10... | collective-permute-start | bytes 98312 | tf_op jit(solution)/shard_map/ppermute | solution.py:28
  31.4 5.1 %collective-permute-start.4 = (f32[1,32,256]{2,1,0:T(8,128)S(1)}, f32[1,32,256]{2,1,0:T(8,128)S(1)}, u32[]{:S(2)}, u32[]{:S(2)}) collective-permute-start(f32[1,32,256]{2,1,0:T(8,128)S(1)} %slice_add_fusion.10), channel_id=1, source_target_pairs={{0,4},{1,5},{2,6},{3,7},{4,0},{5,1},{6,2},{7,3},{8,12},{9,13},{10,... | collective-permute-start | bytes 98312 | tf_op jit(solution)/shard_map/ppermute | solution.py:28
  37.3 3.8 %collective-permute-start.10 = (bf16[1,32,256]{2,1,0:T(8,128)(2,1)S(1)}, bf16[1,32,256]{2,1,0:T(8,128)(2,1)S(1)}, u32[]{:S(2)}, u32[]{:S(2)}) collective-permute-start(bf16[1,32,256]{2,1,0:T(8,128)(2,1)S(1)} %fusion.9.refs_0_), channel_id=1, source_target_pairs={{0,16},{8,24},{16,0},{24,8},{1,17},{9,25},{17,1},{25,9},{2,18},{10... | collective-permute-start | bytes 49160 | tf_op jit(solution)/shard_map/ppermute | solution.py:28
  38.9 4.6 %collective-permute-start.15 = (bf16[1,32,256]{2,1,0:T(8,128)(2,1)S(1)}, bf16[1,32,256]{2,1,0:T(8,128)(2,1)S(1)}, u32[]{:S(2)}, u32[]{:S(2)}) collective-permute-start(bf16[1,32,256]{2,1,0:T(8,128)(2,1)S(1)} %fusion.9.refs_0_), channel_id=1, source_target_pairs={{0,4},{1,5},{2,6},{3,7},{4,0},{5,1},{6,2},{7,3},{8,12},{9,13},{10,... | collective-permute-start | bytes 49160 | tf_op jit(solution)/shard_map/ppermute | solution.py:28
  43.5 1.3 %collective-permute-start.11 = (bf16[2,32,256]{2,1,0:T(8,128)(2,1)S(1)}, bf16[2,32,256]{2,1,0:T(8,128)(2,1)S(1)}, u32[]{:S(2)}, u32[]{:S(2)}) collective-permute-start(bf16[2,32,256]{2,1,0:T(8,128)(2,1)S(1)} %get-tuple-element.30), channel_id=1, source_target_pairs={{0,8},{8,0},{16,24},{24,16},{1,9},{9,1},{17,25},{25,17},{2,10},{10... | collective-permute-start | bytes 98312 | tf_op jit(solution)/shard_map/ppermute | solution.py:28
  43.6 25.2 %copy-start.1 = (bf16[32,256]{1,0:T(8,128)(2,1)S(1)}, bf16[32,256]{1,0:T(8,128)(2,1)}, u32[]{:S(2)}) copy-start(bf16[32,256]{1,0:T(8,128)(2,1)} %param.5) | copy-start | bytes 49156
  43.6 6.5 %collective-permute-start.16 = (bf16[2,32,256]{2,1,0:T(8,128)(2,1)S(1)}, bf16[2,32,256]{2,1,0:T(8,128)(2,1)S(1)}, u32[]{:S(2)}, u32[]{:S(2)}) collective-permute-start(bf16[2,32,256]{2,1,0:T(8,128)(2,1)S(1)} %get-tuple-element.31), channel_id=1, source_target_pairs={{0,2},{1,3},{2,0},{3,1},{4,6},{5,7},{6,4},{7,5},{8,10},{9,11},{10,... | collective-permute-start | bytes 98312 | tf_op jit(solution)/shard_map/ppermute | solution.py:28
  48.5 20.3 %copy-start.18 = (f32[1,32,256]{2,1,0:T(8,128)S(1)}, f32[1,32,256]{2,1,0:T(8,128)}, u32[]{:S(2)}) copy-start(f32[1,32,256]{2,1,0:T(8,128)} %get-tuple-element.23) | copy-start | bytes 98308
  48.5 10.8 %collective-permute-start.12 = (f32[4,32,256]{2,1,0:T(8,128)}, f32[4,32,256]{2,1,0:T(8,128)S(1)}, u32[]{:S(2)}, u32[]{:S(2)}) collective-permute-start(f32[4,32,256]{2,1,0:T(8,128)} %get-tuple-element.24), channel_id=1, source_target_pairs={{0,1},{1,0},{2,3},{3,2},{4,5},{5,4},{6,7},{7,6},{8,9},{9,8},{10,11... | collective-permute-start | bytes 393224 | tf_op jit(solution)/shard_map/ppermute | solution.py:28
  50.9 4.9 %collective-permute-start.17 = (bf16[4,32,256]{2,1,0:T(8,128)(2,1)S(1)}, bf16[4,32,256]{2,1,0:T(8,128)(2,1)S(1)}, u32[]{:S(2)}, u32[]{:S(2)}) collective-permute-start(bf16[4,32,256]{2,1,0:T(8,128)(2,1)S(1)} %pad_maximum_fusion.1), channel_id=1, source_target_pairs={{0,1},{1,0},{2,3},{3,2},{4,5},{5,4},{6,7},{7,6},{8,9},{9,8},{10,11... | collective-permute-start | bytes 196616 | tf_op jit(solution)/shard_map/ppermute | solution.py:28
  59.3 1.5 %collective-permute-start.18 = (f32[2,32,256]{2,1,0:T(8,128)}, f32[2,32,256]{2,1,0:T(8,128)S(1)}, u32[]{:S(2)}, u32[]{:S(2)}) collective-permute-start(f32[2,32,256]{2,1,0:T(8,128)} %get-tuple-element.28), channel_id=1, source_target_pairs={{0,8},{8,0},{16,24},{24,16},{1,9},{9,1},{17,25},{25,17},{2,10},{10... | collective-permute-start | bytes 196616 | tf_op jit(solution)/shard_map/ppermute | solution.py:28
  59.3 4.6 %collective-permute-start.13 = (f32[2,32,256]{2,1,0:T(8,128)S(1)}, f32[2,32,256]{2,1,0:T(8,128)S(1)}, u32[]{:S(2)}, u32[]{:S(2)}) collective-permute-start(f32[2,32,256]{2,1,0:T(8,128)S(1)} %slice_add_fusion), channel_id=1, source_target_pairs={{0,2},{1,3},{2,0},{3,1},{4,6},{5,7},{6,4},{7,5},{8,10},{9,11},{10,... | collective-permute-start | bytes 196616 | tf_op jit(solution)/shard_map/ppermute | solution.py:28
  61.5 3.9 %collective-permute-start.19 = (f32[1,32,256]{2,1,0:T(8,128)S(1)}, f32[1,32,256]{2,1,0:T(8,128)S(1)}, u32[]{:S(2)}, u32[]{:S(2)}) collective-permute-start(f32[1,32,256]{2,1,0:T(8,128)S(1)} %slice_add_fusion.2), channel_id=1, source_target_pairs={{0,16},{8,24},{16,0},{24,8},{1,17},{9,25},{17,1},{25,9},{2,18},{10... | collective-permute-start | bytes 98312 | tf_op jit(solution)/shard_map/ppermute | solution.py:28
  63.9 4.9 %collective-permute-start.14 = (f32[1,32,256]{2,1,0:T(8,128)S(1)}, f32[1,32,256]{2,1,0:T(8,128)S(1)}, u32[]{:S(2)}, u32[]{:S(2)}) collective-permute-start(f32[1,32,256]{2,1,0:T(8,128)S(1)} %slice_add_fusion.4), channel_id=1, source_target_pairs={{0,4},{1,5},{2,6},{3,7},{4,0},{5,1},{6,2},{7,3},{8,12},{9,13},{10,... | collective-permute-start | bytes 98312 | tf_op jit(solution)/shard_map/ppermute | solution.py:28
  (15 other events, 109.8 us)

commit v2 on v1

v2 whole, which is shorter than its diff:
```python
import functools

import jax
import jax.numpy as jnp
from jax import lax
from jax.experimental import pallas as pl
from jax.experimental.pallas import tpu as pltpu
from jax.sharding import PartitionSpec as P

SMEM = pl.BlockSpec(memory_space=pltpu.SMEM)
VMEM = pl.BlockSpec(memory_space=pltpu.VMEM)
HBM = pl.BlockSpec(memory_space=pltpu.HBM)


def digits_of(count, wide):
    out, stride, rest = [], 1, count
    for radix in wide:
        if rest % radix == 0:
            out.append((stride, radix))
            stride, rest = stride * radix, rest // radix
    prime = 2
    while rest > 1:
        while rest % prime:
            prime += 1
        out.append((stride, prime))
        stride, rest = stride * prime, rest // prime
    return out


def moved(index, stride, radix, step):
    if radix & (radix - 1) == 0 and stride & (stride - 1) == 0:
        return index ^ (abs(step) * stride)
    digit = index // stride % radix
    return index + ((digit + step) % radix - digit) * stride


def send(value, axis, count, stride, radix, step):
    pairs = [(i, moved(i, stride, radix, step)) for i in range(count)]
    return lax.ppermute(value, axis, pairs)


def gather(block, kept, axis, count, digits):
    pieces = [kept[None]]
    for stride, radix in reversed(digits):
        held = block[None] if len(pieces) == 1 else jnp.concatenate(pieces, 0)
        for step in range(1, radix):
            pieces.append(send(held, axis, count, stride, radix, -step))
    return pieces


def slots_of(digits):
    slots = [()]
    for _, radix in reversed(digits):
        slots = [(step,) + rest for step in range(radix) for rest in slots]
    return slots


def slot_index(me, digits, steps):
    for (stride, radix), step in zip(digits, steps):
        if step:
            me = moved(me, stride, radix, step)
    return me


def sizes_of(digits):
    sizes, held = [1], 1
    for _, radix in reversed(digits):
        sizes += [held] * (radix - 1)
        held *= radix
    return sizes


def scatter(pieces, axis, count, digits):
    for stride, radix in digits:
        keep = pieces[: len(pieces) - (radix - 1)]
        sent = pieces[len(keep) :]
        got = [send(value, axis, count, stride, radix, step + 1) for step, value in enumerate(sent)]
        at, pieces = 0, []
        for value in keep:
            size = value.shape[0]
            for other in got:
                value = value + other[at : at + size]
            at += size
            pieces.append(value)
    return pieces[0][0]


def fetch_kernel(tiles_hbm, vec_hbm, tiles_ref, vec_ref, sems):
    pairs = ((tiles_hbm, tiles_ref), (vec_hbm, vec_ref))
    copies = [pltpu.make_async_copy(a, b, sems.at[i]) for i, (a, b) in enumerate(pairs)]
    for copy in copies:
        copy.start()
    for copy in copies:
        copy.wait()


def fetch(*arrays):
    return pl.pallas_call(
        fetch_kernel,
        out_shape=[jax.ShapeDtypeStruct(a.shape, a.dtype) for a in arrays],
        in_specs=[HBM] * 2,
        out_specs=[VMEM] * 2,
        scratch_shapes=[pltpu.SemaphoreType.DMA((2,))],
        compiler_params=pltpu.CompilerParams(vmem_limit_bytes=16 * 2**20),
        cost_estimate=pl.CostEstimate(flops=0, bytes_accessed=8 * 2**20, transcendentals=0),
        name="fetch",
    )(*[pltpu.with_memory_space_constraint(a, pltpu.HBM) for a in arrays])


def kernel(index_ref, *refs, n_in, plans, direct):
    pieces, tiles_ref, outs = refs[:n_in], refs[n_in], refs[n_in + 1 : -2]
    vec, acc = refs[-2:]
    slots = tiles_ref.shape[0]
    me_r, me_c = lax.axis_index("row"), lax.axis_index("col")
    me_in, me_out = (me_r, me_c) if direct else (me_c, me_r)
    where = iter(slots_of(plans[0]))
    for piece in pieces:
        for i in range(piece.shape[0]):
            vec[slot_index(me_in, plans[0], next(where))] = piece[i]
    acc[...] = jnp.zeros_like(acc)
    dims = (((1,), (1,)), ((), ())) if direct else (((1,), (0,)), ((), ()))
    live = index_ref[2 * slots]
    for t in range(slots):
        row, col = index_ref[t], index_ref[slots + t]
        take, put = (col, row) if direct else (row, col)
        y = lax.dot_general(vec[take], tiles_ref[t], dims, preferred_element_type=jnp.float32)
        acc[put] += jnp.where(t < live, y, 0.0)
    where = iter(slots_of(plans[1]))
    for out in outs:
        for i in range(out.shape[0]):
            out[i] = acc[slot_index(me_out, plans[1], next(where))]


def half(index, pieces, tiles, plans, direct):
    width, size = pieces[0].shape[1:]
    sizes = sizes_of(plans[1])
    count_in, count_out = (sum(sizes_of(plan)) for plan in plans)
    flops = 2 * width * tiles.size
    return pl.pallas_call(
        functools.partial(kernel, n_in=len(pieces), plans=plans, direct=direct),
        out_shape=[jax.ShapeDtypeStruct((n, width, size), jnp.float32) for n in sizes],
        in_specs=[SMEM] + [VMEM] * (len(pieces) + 1),
        out_specs=[VMEM] * len(sizes),
        scratch_shapes=[
            pltpu.VMEM((count_in, width, size), jnp.bfloat16),
            pltpu.VMEM((count_out, width, size), jnp.float32),
        ],
        compiler_params=pltpu.CompilerParams(vmem_limit_bytes=16 * 2**20),
        name="direct" if direct else "mirror",
    )(index, *pieces, tiles)


def local(rows, cols, vectors, tiles, tile_rows, tile_cols, tile_live):
    row_plan, col_plan = digits_of(rows, (4,)), digits_of(cols, ())
    index = jnp.concatenate([tile_rows, tile_cols, tile_live])
    held, vectors_held = fetch(tiles, vectors)

    def apply(vec, kept):
        colset = gather(vec, kept, "row", rows, row_plan)
        rowset = gather(vec, kept, "col", cols, col_plan)
        direct = half(index, colset, held, (row_plan, col_plan), True)
        mirror = half(index, rowset, held, (col_plan, row_plan), False)
        return scatter(list(direct), "col", cols, col_plan) + scatter(list(mirror), "row", rows, row_plan)

    first = apply(vectors, vectors_held).astype(jnp.bfloat16)
    second = 2.0 * apply(first, first) - vectors_held.astype(jnp.float32)
    return first, second.astype(jnp.bfloat16)


def solution(mesh):
    both = ("row", "col")
    placed = (P(None, both), P(both, None, None), P(both), P(both), P(both))
    return jax.shard_map(
        functools.partial(local, mesh.shape["row"], mesh.shape["col"]),
        mesh=mesh,
        in_specs=placed,
        out_specs=(P(None, both), P(None, both)),
        check_vma=False,
    )
```

time: 70.9 us -> 50.2 us (0.71)
  waiting for transfers between devices: 28.4 us -> 15.9 us
  starting transfers between devices: 19.5 us -> 25.6 us
  Pallas kernels: 11.9 us -> 6.27 us
  other arithmetic: 6.4 us -> 0.79 us
  local copies, waits for them, and re-layouts: 2.55 us -> 0.02 us
    ppermute x20 -> x24, waiting for transfers between devices: 28.4 us -> 15.9 us  [send(): return lax.ppermute(value, axis, pairs)]
    ppermute x20 -> x24, starting transfers between devices: 19.5 us -> 25.6 us  [send(): return lax.ppermute(value, axis, pairs)]
    pallas_call x4 -> x5, Pallas kernels: 11.9 us -> 6.27 us  [the longest x4 4.66 us: half(): pl.pallas_call(functools.partial(kernel, n_in=len(pieces), plans=plans, d...]
    unnamed x38 -> x6, local copies, waits for them, and re-layouts: 2.55 us -> 0.02 us
    add x6 -> x4, other arithmetic: 1.57 us -> 0.03 us  [scatter(): value = value + other[at:at + size]]
    concatenate x4 -> x5, other arithmetic: 1.48 us -> 0.11 us  [the longest x1 0.08 us: local(): index = jnp.concatenate([tile_rows, tile_cols, tile_live])]
    another operation x2 -> x0, other arithmetic: 1.18 us -> none  [the longest x1 0.61 us: local(): me_mirror = jnp.stack([c, r]).astype(jnp.int32)]
    convert_element_type x1, other arithmetic: 0.78 us -> 0.02 us  [local(): first = apply(vectors, vectors_held).astype(jnp.bfloat16)]
  transfers between devices with their start and end apart: 20 -> 24, of which waited for: 15 -> 9; matrix products, arithmetic and copies ran while one was open for 5% -> 0% of each run, Pallas kernels for 17% -> 13%
where the time goes in v2:
time: 50.2 us; the launch traced here: 50 us
  starting transfers between devices  25.6 us (51%)
  waiting for transfers between devices  15.9 us (32%)
  Pallas kernels  6.27 us (12%)
  between operations  1.42 us (3%)
  other arithmetic  0.79 us (2%)
    ppermute x24, starting transfers between devices, send(): return lax.ppermute(value, axis, pairs)  25.6 us
    ppermute x24, waiting for transfers between devices, send(): return lax.ppermute(value, axis, pairs)  15.9 us
    pallas_call x4, Pallas kernels, half(): pl.pallas_call(functools.partial(kernel, n_in=len(pieces), plans=plans, d...  4.66 us
    pallas_call x1, Pallas kernels, fetch(): pl.pallas_call(fetch_kernel, out_shape=[jax.ShapeDtypeStruct(a.shape, a.d...  1.61 us
  transfers between devices with their start and end apart: 24, of which 9 were waited for; matrix products, arithmetic and copies ran while one was open for 0% of the time, Pallas kernels for 13%

profile of v2, /device:TPU:0, one launch (start us, length us, event | category | flops | bytes accessed | tf_op | source)
XLA Modules:
  0.0 50.0 jit_solution(3415999843810261769)
XLA Ops:
  0.7 4.1 %collective-permute-start.6 = (bf16[1,32,256]{2,1,0:T(8,128)(2,1)}, bf16[1,32,256]{2,1,0:T(8,128)(2,1)S(1)}, u32[]{:S(2)}, u32[]{:S(2)}) collective-permute-start(bf16[1,32,256]{2,1,0:T(8,128)(2,1)} %bitcast.14), channel_id=1, source_target_pairs={{0,4},{1,5},{2,6},{3,7},{4,0},{5,1},{6,2},{7,3},{8,12},{9,13},{10,... | collective-permute-start | bytes 49160 | tf_op jit(solution)/shard_map/ppermute | solution.py:39
  4.8 1.5 %collective-permute-start.1 = (bf16[1,32,256]{2,1,0:T(8,128)(2,1)}, bf16[1,32,256]{2,1,0:T(8,128)(2,1)S(1)}, u32[]{:S(2)}, u32[]{:S(2)}) collective-permute-start(bf16[1,32,256]{2,1,0:T(8,128)(2,1)} %bitcast.16), channel_id=1, source_target_pairs={{0,16},{8,24},{16,0},{24,8},{1,17},{9,25},{17,1},{25,9},{2,18},{10... | collective-permute-start | bytes 49160 | tf_op jit(solution)/shard_map/ppermute | solution.py:39
  6.6 1.6 %fetch.1 = (bf16[16,256,256]{2,1,0:T(8,128)(2,1)S(1)}, bf16[32,256]{1,0:T(8,128)(2,1)S(1)}) custom-call(bf16[16,256,256]{2,1,0:T(8,128)(2,1)} %tiles_hbm.1, bf16[32,256]{1,0:T(8,128)(2,1)} %vec_hbm.1), custom_call_target="tpu_custom_call" | custom-call | bytes 8388608 | tf_op jit(solution)/shard_map/fetch/pallas_call | solution.py:98
  8.9 1.6 %collective-permute-start.7 = (bf16[2,32,256]{2,1,0:T(8,128)(2,1)S(1)}, bf16[2,32,256]{2,1,0:T(8,128)(2,1)S(1)}, u32[]{:S(2)}, u32[]{:S(2)}) collective-permute-start(bf16[2,32,256]{2,1,0:T(8,128)(2,1)S(1)} %pad_maximum_fusion.2), channel_id=1, source_target_pairs={{0,2},{1,3},{2,0},{3,1},{4,6},{5,7},{6,4},{7,5},{8,10},{9,11},{10,... | collective-permute-start | bytes 98312 | tf_op jit(solution)/shard_map/ppermute | solution.py:39
  10.6 1.3 %direct.2 = (f32[1,32,256]{2,1,0:T(8,128)S(1)}, f32[1,32,256]{2,1,0:T(8,128)S(1)}, f32[2,32,256]{2,1,0:T(8,128)S(1)}, f32[4,32,256]{2,1,0:T(8,128)S(1)}) custom-call(s32[33]{0:T(128)S(1)} %pad_add_fusion.index_ref, bf16[1,32,256]{2,1,0:T(8,128)(2,1)S(1)} %bitcast.10, bf16[1,32,256]{2,1,0:T(8,128)(2,1)S(1)} %collective-permute-done.refs_1_, ...), custom_call_target="tpu_custom_call" | custom-call | tf_op jit(solution)/shard_map/direct/pallas_call | solution.py:139
  11.9 1.6 %collective-permute-start.3 = (f32[4,32,256]{2,1,0:T(8,128)S(1)}, f32[4,32,256]{2,1,0:T(8,128)S(1)}, u32[]{:S(2)}, u32[]{:S(2)}) collective-permute-start(f32[4,32,256]{2,1,0:T(8,128)S(1)} %get-tuple-element.23), channel_id=1, source_target_pairs={{0,1},{1,0},{2,3},{3,2},{4,5},{5,4},{6,7},{7,6},{8,9},{9,8},{10,11... | collective-permute-start | bytes 393224 | tf_op jit(solution)/shard_map/ppermute | solution.py:39
  13.5 0.9 %collective-permute-start.8 = (bf16[4,32,256]{2,1,0:T(8,128)(2,1)S(1)}, bf16[4,32,256]{2,1,0:T(8,128)(2,1)S(1)}, u32[]{:S(2)}, u32[]{:S(2)}) collective-permute-start(bf16[4,32,256]{2,1,0:T(8,128)(2,1)S(1)} %pad_maximum_fusion), channel_id=1, source_target_pairs={{0,1},{1,0},{2,3},{3,2},{4,5},{5,4},{6,7},{7,6},{8,9},{9,8},{10,11... | collective-permute-start | bytes 196616 | tf_op jit(solution)/shard_map/ppermute | solution.py:39
  14.5 3.6 %collective-permute-done.3 = f32[4,32,256]{2,1,0:T(8,128)S(1)} collective-permute-done((f32[4,32,256]{2,1,0:T(8,128)S(1)}, f32[4,32,256]{2,1,0:T(8,128)S(1)}, u32[]{:S(2)}, u32[]{:S(2)}) %collective-permute-start.3) | collective-permute-done | bytes 131104 | tf_op jit(solution)/shard_map/ppermute | solution.py:39
  19.0 1.0 %mirror.2 = (f32[1,32,256]{2,1,0:T(8,128)S(1)}, f32[1,32,256]{2,1,0:T(8,128)S(1)}, f32[1,32,256]{2,1,0:T(8,128)S(1)}, f32[1,32,256]{2,1,0:T(8,128)S(1)}) custom-call(s32[33]{0:T(128)S(1)} %pad_add_fusion.index_ref, bf16[1,32,256]{2,1,0:T(8,128)(2,1)S(1)} %bitcast.12, bf16[1,32,256]{2,1,0:T(8,128)(2,1)S(1)} %collective-permute-done.6.refs_1_, ...), custom_call_target="tpu_custom_call" | custom-call | tf_op jit(solution)/shard_map/mirror/pallas_call | solution.py:139
  20.0 1.4 %collective-permute-start.10 = (f32[1,32,256]{2,1,0:T(8,128)S(1)}, f32[1,32,256]{2,1,0:T(8,128)S(1)}, u32[]{:S(2)}, u32[]{:S(2)}) collective-permute-start(f32[1,32,256]{2,1,0:T(8,128)S(1)} %get-tuple-element.28), channel_id=1, source_target_pairs={{0,16},{8,24},{16,0},{24,8},{1,17},{9,25},{17,1},{25,9},{2,18},{10... | collective-permute-start | bytes 98312 | tf_op jit(solution)/shard_map/ppermute | solution.py:39
  22.9 1.1 %collective-permute-done.10 = f32[1,32,256]{2,1,0:T(8,128)S(1)} collective-permute-done((f32[1,32,256]{2,1,0:T(8,128)S(1)}, f32[1,32,256]{2,1,0:T(8,128)S(1)}, u32[]{:S(2)}, u32[]{:S(2)}) %collective-permute-start.10) | collective-permute-done | bytes 32800 | tf_op jit(solution)/shard_map/ppermute | solution.py:39
  24.8 2.6 %collective-permute-done.5 = f32[1,32,256]{2,1,0:T(8,128)S(1)} collective-permute-done((f32[1,32,256]{2,1,0:T(8,128)S(1)}, f32[1,32,256]{2,1,0:T(8,128)S(1)}, u32[]{:S(2)}, u32[]{:S(2)}) %collective-permute-start.5) | collective-permute-done | bytes 32800 | tf_op jit(solution)/shard_map/ppermute | solution.py:39
  27.8 1.5 %collective-permute-start.13 = (bf16[1,32,256]{2,1,0:T(8,128)(2,1)S(1)}, bf16[1,32,256]{2,1,0:T(8,128)(2,1)S(1)}, u32[]{:S(2)}, u32[]{:S(2)}) collective-permute-start(bf16[1,32,256]{2,1,0:T(8,128)(2,1)S(1)} %fusion.8.refs_0_), channel_id=1, source_target_pairs={{0,16},{8,24},{16,0},{24,8},{1,17},{9,25},{17,1},{25,9},{2,18},{10... | collective-permute-start | bytes 49160 | tf_op jit(solution)/shard_map/ppermute | solution.py:39
  29.6 2.4 %collective-permute-done.18.refs_1_ = bf16[1,32,256]{2,1,0:T(8,128)(2,1)S(1)} collective-permute-done((bf16[1,32,256]{2,1,0:T(8,128)(2,1)S(1)}, bf16[1,32,256]{2,1,0:T(8,128)(2,1)S(1)}, u32[]{:S(2)}, u32[]{:S(2)}) %collective-permute-start.18) | collective-permute-done | bytes 16416 | tf_op jit(solution)/shard_map/ppermute | solution.py:39
  32.1 1.0 %collective-permute-start.19 = (bf16[2,32,256]{2,1,0:T(8,128)(2,1)S(1)}, bf16[2,32,256]{2,1,0:T(8,128)(2,1)S(1)}, u32[]{:S(2)}, u32[]{:S(2)}) collective-permute-start(bf16[2,32,256]{2,1,0:T(8,128)(2,1)S(1)} %pad_maximum_fusion.3), channel_id=1, source_target_pairs={{0,2},{1,3},{2,0},{3,1},{4,6},{5,7},{6,4},{7,5},{8,10},{9,11},{10,... | collective-permute-start | bytes 98312 | tf_op jit(solution)/shard_map/ppermute | solution.py:39
  33.1 1.3 %direct.3 = (f32[1,32,256]{2,1,0:T(8,128)S(1)}, f32[1,32,256]{2,1,0:T(8,128)S(1)}, f32[2,32,256]{2,1,0:T(8,128)S(1)}, f32[4,32,256]{2,1,0:T(8,128)S(1)}) custom-call(s32[33]{0:T(128)S(1)} %pad_add_fusion.index_ref, bf16[1,32,256]{2,1,0:T(8,128)(2,1)S(1)} %fusion.8.refs_0_, bf16[1,32,256]{2,1,0:T(8,128)(2,1)S(1)} %collective-permute-done.12.refs_1_, ...), custom_call_target="tpu_custom_call" | custom-call | tf_op jit(solution)/shard_map/direct/pallas_call | solution.py:139
  34.4 1.6 %collective-permute-start.15 = (f32[4,32,256]{2,1,0:T(8,128)S(1)}, f32[4,32,256]{2,1,0:T(8,128)S(1)}, u32[]{:S(2)}, u32[]{:S(2)}) collective-permute-start(f32[4,32,256]{2,1,0:T(8,128)S(1)} %get-tuple-element.31), channel_id=1, source_target_pairs={{0,1},{1,0},{2,3},{3,2},{4,5},{5,4},{6,7},{7,6},{8,9},{9,8},{10,11... | collective-permute-start | bytes 393224 | tf_op jit(solution)/shard_map/ppermute | solution.py:39
  36.0 1.6 %collective-permute-start.20 = (bf16[4,32,256]{2,1,0:T(8,128)(2,1)S(1)}, bf16[4,32,256]{2,1,0:T(8,128)(2,1)S(1)}, u32[]{:S(2)}, u32[]{:S(2)}) collective-permute-start(bf16[4,32,256]{2,1,0:T(8,128)(2,1)S(1)} %pad_maximum_fusion.1), channel_id=1, source_target_pairs={{0,1},{1,0},{2,3},{3,2},{4,5},{5,4},{6,7},{7,6},{8,9},{9,8},{10,11... | collective-permute-start | bytes 196616 | tf_op jit(solution)/shard_map/ppermute | solution.py:39
  37.6 2.5 %collective-permute-done.15 = f32[4,32,256]{2,1,0:T(8,128)S(1)} collective-permute-done((f32[4,32,256]{2,1,0:T(8,128)S(1)}, f32[4,32,256]{2,1,0:T(8,128)S(1)}, u32[]{:S(2)}, u32[]{:S(2)}) %collective-permute-start.15) | collective-permute-done | bytes 131104 | tf_op jit(solution)/shard_map/ppermute | solution.py:39
  40.2 1.1 %collective-permute-start.16 = (f32[2,32,256]{2,1,0:T(8,128)S(1)}, f32[2,32,256]{2,1,0:T(8,128)S(1)}, u32[]{:S(2)}, u32[]{:S(2)}) collective-permute-start(f32[2,32,256]{2,1,0:T(8,128)S(1)} %slice_add_fusion), channel_id=1, source_target_pairs={{0,2},{1,3},{2,0},{3,1},{4,6},{5,7},{6,4},{7,5},{8,10},{9,11},{10,... | collective-permute-start | bytes 196616 | tf_op jit(solution)/shard_map/ppermute | solution.py:39
  41.2 1.0 %mirror.3 = (f32[1,32,256]{2,1,0:T(8,128)S(1)}, f32[1,32,256]{2,1,0:T(8,128)S(1)}, f32[1,32,256]{2,1,0:T(8,128)S(1)}, f32[1,32,256]{2,1,0:T(8,128)S(1)}) custom-call(s32[33]{0:T(128)S(1)} %pad_add_fusion.index_ref, bf16[1,32,256]{2,1,0:T(8,128)(2,1)S(1)} %fusion.8.refs_0_, bf16[1,32,256]{2,1,0:T(8,128)(2,1)S(1)} %collective-permute-done.18.refs_1_, ...), custom_call_target="tpu_custom_call" | custom-call | tf_op jit(solution)/shard_map/mirror/pallas_call | solution.py:139
  43.3 1.0 %collective-permute-start.23 = (f32[1,32,256]{2,1,0:T(8,128)S(1)}, f32[1,32,256]{2,1,0:T(8,128)S(1)}, u32[]{:S(2)}, u32[]{:S(2)}) collective-permute-start(f32[1,32,256]{2,1,0:T(8,128)S(1)} %get-tuple-element.37), channel_id=1, source_target_pairs={{0,24},{8,16},{16,8},{24,0},{1,25},{9,17},{17,9},{25,1},{2,26},{10... | collective-permute-start | bytes 98312 | tf_op jit(solution)/shard_map/ppermute | solution.py:39
  44.5 2.7 %collective-permute-start.17 = (f32[1,32,256]{2,1,0:T(8,128)S(1)}, f32[1,32,256]{2,1,0:T(8,128)S(1)}, u32[]{:S(2)}, u32[]{:S(2)}) collective-permute-start(f32[1,32,256]{2,1,0:T(8,128)S(1)} %slice_add_fusion.2), channel_id=1, source_target_pairs={{0,4},{1,5},{2,6},{3,7},{4,0},{5,1},{6,2},{7,3},{8,12},{9,13},{10,... | collective-permute-start | bytes 98312 | tf_op jit(solution)/shard_map/ppermute | solution.py:39
  47.2 2.2 %collective-permute-done.17 = f32[1,32,256]{2,1,0:T(8,128)S(1)} collective-permute-done((f32[1,32,256]{2,1,0:T(8,128)S(1)}, f32[1,32,256]{2,1,0:T(8,128)S(1)}, u32[]{:S(2)}, u32[]{:S(2)}) %collective-permute-start.17) | collective-permute-done | bytes 32800 | tf_op jit(solution)/shard_map/ppermute | solution.py:39
  (46 shorter events, 6.3 us)
Async XLA Ops:
  0.7 8.2 %collective-permute-start.6 = (bf16[1,32,256]{2,1,0:T(8,128)(2,1)}, bf16[1,32,256]{2,1,0:T(8,128)(2,1)S(1)}, u32[]{:S(2)}, u32[]{:S(2)}) collective-permute-start(bf16[1,32,256]{2,1,0:T(8,128)(2,1)} %bitcast.14), channel_id=1, source_target_pairs={{0,4},{1,5},{2,6},{3,7},{4,0},{5,1},{6,2},{7,3},{8,12},{9,13},{10,... | collective-permute-start | bytes 49160 | tf_op jit(solution)/shard_map/ppermute | solution.py:39
  4.8 5.9 %collective-permute-start = (bf16[1,32,256]{2,1,0:T(8,128)(2,1)}, bf16[1,32,256]{2,1,0:T(8,128)(2,1)S(1)}, u32[]{:S(2)}, u32[]{:S(2)}) collective-permute-start(bf16[1,32,256]{2,1,0:T(8,128)(2,1)} %bitcast.15), channel_id=1, source_target_pairs={{0,8},{8,0},{16,24},{24,16},{1,9},{9,1},{17,25},{25,17},{2,10},{10... | collective-permute-start | bytes 49160 | tf_op jit(solution)/shard_map/ppermute | solution.py:39
  4.8 5.9 %collective-permute-start.1 = (bf16[1,32,256]{2,1,0:T(8,128)(2,1)}, bf16[1,32,256]{2,1,0:T(8,128)(2,1)S(1)}, u32[]{:S(2)}, u32[]{:S(2)}) collective-permute-start(bf16[1,32,256]{2,1,0:T(8,128)(2,1)} %bitcast.16), channel_id=1, source_target_pairs={{0,16},{8,24},{16,0},{24,8},{1,17},{9,25},{17,1},{25,9},{2,18},{10... | collective-permute-start | bytes 49160 | tf_op jit(solution)/shard_map/ppermute | solution.py:39
  6.2 4.4 %collective-permute-start.2 = (bf16[1,32,256]{2,1,0:T(8,128)(2,1)}, bf16[1,32,256]{2,1,0:T(8,128)(2,1)S(1)}, u32[]{:S(2)}, u32[]{:S(2)}) collective-permute-start(bf16[1,32,256]{2,1,0:T(8,128)(2,1)} %bitcast.17), channel_id=1, source_target_pairs={{0,24},{8,16},{16,8},{24,0},{1,25},{9,17},{17,9},{25,1},{2,26},{10... | collective-permute-start | bytes 49160 | tf_op jit(solution)/shard_map/ppermute | solution.py:39
  8.9 4.6 %collective-permute-start.7 = (bf16[2,32,256]{2,1,0:T(8,128)(2,1)S(1)}, bf16[2,32,256]{2,1,0:T(8,128)(2,1)S(1)}, u32[]{:S(2)}, u32[]{:S(2)}) collective-permute-start(bf16[2,32,256]{2,1,0:T(8,128)(2,1)S(1)} %pad_maximum_fusion.2), channel_id=1, source_target_pairs={{0,2},{1,3},{2,0},{3,1},{4,6},{5,7},{6,4},{7,5},{8,10},{9,11},{10,... | collective-permute-start | bytes 98312 | tf_op jit(solution)/shard_map/ppermute | solution.py:39
  11.9 6.2 %collective-permute-start.3 = (f32[4,32,256]{2,1,0:T(8,128)S(1)}, f32[4,32,256]{2,1,0:T(8,128)S(1)}, u32[]{:S(2)}, u32[]{:S(2)}) collective-permute-start(f32[4,32,256]{2,1,0:T(8,128)S(1)} %get-tuple-element.23), channel_id=1, source_target_pairs={{0,1},{1,0},{2,3},{3,2},{4,5},{5,4},{6,7},{7,6},{8,9},{9,8},{10,11... | collective-permute-start | bytes 393224 | tf_op jit(solution)/shard_map/ppermute | solution.py:39
  13.5 5.4 %collective-permute-start.8 = (bf16[4,32,256]{2,1,0:T(8,128)(2,1)S(1)}, bf16[4,32,256]{2,1,0:T(8,128)(2,1)S(1)}, u32[]{:S(2)}, u32[]{:S(2)}) collective-permute-start(bf16[4,32,256]{2,1,0:T(8,128)(2,1)S(1)} %pad_maximum_fusion), channel_id=1, source_target_pairs={{0,1},{1,0},{2,3},{3,2},{4,5},{5,4},{6,7},{7,6},{8,9},{9,8},{10,11... | collective-permute-start | bytes 196616 | tf_op jit(solution)/shard_map/ppermute | solution.py:39
  18.1 4.3 %collective-permute-start.4 = (f32[2,32,256]{2,1,0:T(8,128)S(1)}, f32[2,32,256]{2,1,0:T(8,128)S(1)}, u32[]{:S(2)}, u32[]{:S(2)}) collective-permute-start(f32[2,32,256]{2,1,0:T(8,128)S(1)} %slice_add_fusion.1), channel_id=1, source_target_pairs={{0,2},{1,3},{2,0},{3,1},{4,6},{5,7},{6,4},{7,5},{8,10},{9,11},{10,... | collective-permute-start | bytes 196616 | tf_op jit(solution)/shard_map/ppermute | solution.py:39
  20.0 4.0 %collective-permute-start.10 = (f32[1,32,256]{2,1,0:T(8,128)S(1)}, f32[1,32,256]{2,1,0:T(8,128)S(1)}, u32[]{:S(2)}, u32[]{:S(2)}) collective-permute-start(f32[1,32,256]{2,1,0:T(8,128)S(1)} %get-tuple-element.28), channel_id=1, source_target_pairs={{0,16},{8,24},{16,0},{24,8},{1,17},{9,25},{17,1},{25,9},{2,18},{10... | collective-permute-start | bytes 98312 | tf_op jit(solution)/shard_map/ppermute | solution.py:39
  21.4 3.3 %collective-permute-start.11 = (f32[1,32,256]{2,1,0:T(8,128)S(1)}, f32[1,32,256]{2,1,0:T(8,128)S(1)}, u32[]{:S(2)}, u32[]{:S(2)}) collective-permute-start(f32[1,32,256]{2,1,0:T(8,128)S(1)} %get-tuple-element.29), channel_id=1, source_target_pairs={{0,24},{8,16},{16,8},{24,0},{1,25},{9,17},{17,9},{25,1},{2,26},{10... | collective-permute-start | bytes 98312 | tf_op jit(solution)/shard_map/ppermute | solution.py:39
  21.4 3.3 %collective-permute-start.9 = (f32[1,32,256]{2,1,0:T(8,128)S(1)}, f32[1,32,256]{2,1,0:T(8,128)S(1)}, u32[]{:S(2)}, u32[]{:S(2)}) collective-permute-start(f32[1,32,256]{2,1,0:T(8,128)S(1)} %get-tuple-element.27), channel_id=1, source_target_pairs={{0,8},{8,0},{16,24},{24,16},{1,9},{9,1},{17,25},{25,17},{2,10},{10... | collective-permute-start | bytes 98312 | tf_op jit(solution)/shard_map/ppermute | solution.py:39
  22.5 4.9 %collective-permute-start.5 = (f32[1,32,256]{2,1,0:T(8,128)S(1)}, f32[1,32,256]{2,1,0:T(8,128)S(1)}, u32[]{:S(2)}, u32[]{:S(2)}) collective-permute-start(f32[1,32,256]{2,1,0:T(8,128)S(1)} %slice_add_fusion.6), channel_id=1, source_target_pairs={{0,4},{1,5},{2,6},{3,7},{4,0},{5,1},{6,2},{7,3},{8,12},{9,13},{10,... | collective-permute-start | bytes 98312 | tf_op jit(solution)/shard_map/ppermute | solution.py:39
  27.4 4.7 %collective-permute-start.18 = (bf16[1,32,256]{2,1,0:T(8,128)(2,1)S(1)}, bf16[1,32,256]{2,1,0:T(8,128)(2,1)S(1)}, u32[]{:S(2)}, u32[]{:S(2)}) collective-permute-start(bf16[1,32,256]{2,1,0:T(8,128)(2,1)S(1)} %fusion.8.refs_0_), channel_id=1, source_target_pairs={{0,4},{1,5},{2,6},{3,7},{4,0},{5,1},{6,2},{7,3},{8,12},{9,13},{10,... | collective-permute-start | bytes 49160 | tf_op jit(solution)/shard_map/ppermute | solution.py:39
  27.8 5.3 %collective-permute-start.12 = (bf16[1,32,256]{2,1,0:T(8,128)(2,1)S(1)}, bf16[1,32,256]{2,1,0:T(8,128)(2,1)S(1)}, u32[]{:S(2)}, u32[]{:S(2)}) collective-permute-start(bf16[1,32,256]{2,1,0:T(8,128)(2,1)S(1)} %fusion.8.refs_0_), channel_id=1, source_target_pairs={{0,8},{8,0},{16,24},{24,16},{1,9},{9,1},{17,25},{25,17},{2,10},{10... | collective-permute-start | bytes 49160 | tf_op jit(solution)/shard_map/ppermute | solution.py:39
  27.8 5.3 %collective-permute-start.13 = (bf16[1,32,256]{2,1,0:T(8,128)(2,1)S(1)}, bf16[1,32,256]{2,1,0:T(8,128)(2,1)S(1)}, u32[]{:S(2)}, u32[]{:S(2)}) collective-permute-start(bf16[1,32,256]{2,1,0:T(8,128)(2,1)S(1)} %fusion.8.refs_0_), channel_id=1, source_target_pairs={{0,16},{8,24},{16,0},{24,8},{1,17},{9,25},{17,1},{25,9},{2,18},{10... | collective-permute-start | bytes 49160 | tf_op jit(solution)/shard_map/ppermute | solution.py:39
  29.3 3.9 %collective-permute-start.14 = (bf16[1,32,256]{2,1,0:T(8,128)(2,1)S(1)}, bf16[1,32,256]{2,1,0:T(8,128)(2,1)S(1)}, u32[]{:S(2)}, u32[]{:S(2)}) collective-permute-start(bf16[1,32,256]{2,1,0:T(8,128)(2,1)S(1)} %fusion.8.refs_0_), channel_id=1, source_target_pairs={{0,24},{8,16},{16,8},{24,0},{1,25},{9,17},{17,9},{25,1},{2,26},{10... | collective-permute-start | bytes 49160 | tf_op jit(solution)/shard_map/ppermute | solution.py:39
  32.1 3.9 %collective-permute-start.19 = (bf16[2,32,256]{2,1,0:T(8,128)(2,1)S(1)}, bf16[2,32,256]{2,1,0:T(8,128)(2,1)S(1)}, u32[]{:S(2)}, u32[]{:S(2)}) collective-permute-start(bf16[2,32,256]{2,1,0:T(8,128)(2,1)S(1)} %pad_maximum_fusion.3), channel_id=1, source_target_pairs={{0,2},{1,3},{2,0},{3,1},{4,6},{5,7},{6,4},{7,5},{8,10},{9,11},{10,... | collective-permute-start | bytes 98312 | tf_op jit(solution)/shard_map/ppermute | solution.py:39
  34.4 5.7 %collective-permute-start.15 = (f32[4,32,256]{2,1,0:T(8,128)S(1)}, f32[4,32,256]{2,1,0:T(8,128)S(1)}, u32[]{:S(2)}, u32[]{:S(2)}) collective-permute-start(f32[4,32,256]{2,1,0:T(8,128)S(1)} %get-tuple-element.31), channel_id=1, source_target_pairs={{0,1},{1,0},{2,3},{3,2},{4,5},{5,4},{6,7},{7,6},{8,9},{9,8},{10,11... | collective-permute-start | bytes 393224 | tf_op jit(solution)/shard_map/ppermute | solution.py:39
  36.0 5.2 %collective-permute-start.20 = (bf16[4,32,256]{2,1,0:T(8,128)(2,1)S(1)}, bf16[4,32,256]{2,1,0:T(8,128)(2,1)S(1)}, u32[]{:S(2)}, u32[]{:S(2)}) collective-permute-start(bf16[4,32,256]{2,1,0:T(8,128)(2,1)S(1)} %pad_maximum_fusion.1), channel_id=1, source_target_pairs={{0,1},{1,0},{2,3},{3,2},{4,5},{5,4},{6,7},{7,6},{8,9},{9,8},{10,11... | collective-permute-start | bytes 196616 | tf_op jit(solution)/shard_map/ppermute | solution.py:39
  40.2 4.3 %collective-permute-start.16 = (f32[2,32,256]{2,1,0:T(8,128)S(1)}, f32[2,32,256]{2,1,0:T(8,128)S(1)}, u32[]{:S(2)}, u32[]{:S(2)}) collective-permute-start(f32[2,32,256]{2,1,0:T(8,128)S(1)} %slice_add_fusion), channel_id=1, source_target_pairs={{0,2},{1,3},{2,0},{3,1},{4,6},{5,7},{6,4},{7,5},{8,10},{9,11},{10,... | collective-permute-start | bytes 196616 | tf_op jit(solution)/shard_map/ppermute | solution.py:39
  42.3 4.9 %collective-permute-start.21 = (f32[1,32,256]{2,1,0:T(8,128)S(1)}, f32[1,32,256]{2,1,0:T(8,128)S(1)}, u32[]{:S(2)}, u32[]{:S(2)}) collective-permute-start(f32[1,32,256]{2,1,0:T(8,128)S(1)} %get-tuple-element.35), channel_id=1, source_target_pairs={{0,8},{8,0},{16,24},{24,16},{1,9},{9,1},{17,25},{25,17},{2,10},{10... | collective-permute-start | bytes 98312 | tf_op jit(solution)/shard_map/ppermute | solution.py:39
  42.4 4.8 %collective-permute-start.22 = (f32[1,32,256]{2,1,0:T(8,128)S(1)}, f32[1,32,256]{2,1,0:T(8,128)S(1)}, u32[]{:S(2)}, u32[]{:S(2)}) collective-permute-start(f32[1,32,256]{2,1,0:T(8,128)S(1)} %get-tuple-element.36), channel_id=1, source_target_pairs={{0,16},{8,24},{16,0},{24,8},{1,17},{9,25},{17,1},{25,9},{2,18},{10... | collective-permute-start | bytes 98312 | tf_op jit(solution)/shard_map/ppermute | solution.py:39
  43.3 3.9 %collective-permute-start.23 = (f32[1,32,256]{2,1,0:T(8,128)S(1)}, f32[1,32,256]{2,1,0:T(8,128)S(1)}, u32[]{:S(2)}, u32[]{:S(2)}) collective-permute-start(f32[1,32,256]{2,1,0:T(8,128)S(1)} %get-tuple-element.37), channel_id=1, source_target_pairs={{0,24},{8,16},{16,8},{24,0},{1,25},{9,17},{17,9},{25,1},{2,26},{10... | collective-permute-start | bytes 98312 | tf_op jit(solution)/shard_map/ppermute | solution.py:39
  44.5 4.9 %collective-permute-start.17 = (f32[1,32,256]{2,1,0:T(8,128)S(1)}, f32[1,32,256]{2,1,0:T(8,128)S(1)}, u32[]{:S(2)}, u32[]{:S(2)}) collective-permute-start(f32[1,32,256]{2,1,0:T(8,128)S(1)} %slice_add_fusion.2), channel_id=1, source_target_pairs={{0,4},{1,5},{2,6},{3,7},{4,0},{5,1},{6,2},{7,3},{8,12},{9,13},{10,... | collective-permute-start | bytes 98312 | tf_op jit(solution)/shard_map/ppermute | solution.py:39
  (3 other events, 34.7 us)

commit v3 on v2

v3 whole, which is shorter than its diff:
```python
import functools
import math

import jax
import jax.numpy as jnp
from jax import lax
from jax.experimental import pallas as pl
from jax.experimental.pallas import tpu as pltpu
from jax.sharding import PartitionSpec as P

SMEM = pl.BlockSpec(memory_space=pltpu.SMEM)
VMEM = pl.BlockSpec(memory_space=pltpu.VMEM)
HBM = pl.BlockSpec(memory_space=pltpu.HBM)
PARAMS = pltpu.CompilerParams(vmem_limit_bytes=16 * 2**20)


def digits_of(count, wide):
    out, stride, rest, prime = [], 1, count, 2
    while rest > 1:
        while rest % prime:
            prime += 1
        radix = 4 if wide > 0 and rest % 4 == 0 else prime
        wide -= 1
        out.append((stride, radix))
        stride, rest = stride * radix, rest // radix
    return out


def moved(index, stride, radix, step):
    if radix & (radix - 1) == 0 and stride & (stride - 1) == 0:
        return index ^ (abs(step) * stride)
    digit = index // stride % radix
    return index + ((digit + step) % radix - digit) * stride


def send(value, axis, count, stride, radix, step):
    pairs = [(i, moved(i, stride, radix, step)) for i in range(count)]
    return lax.ppermute(value, axis, pairs)


def after(value, *others):
    return lax.optimization_barrier((value, *others))[0]


def gather(block, kept, axis, count, digits):
    pieces = [kept[None]]
    for stride, radix in reversed(digits):
        held = block[None] if len(pieces) == 1 else jnp.concatenate(pieces, 0)
        for step in range(1, radix):
            pieces.append(send(held, axis, count, stride, radix, -step))
    return pieces


def slots_of(digits):
    slots = [()]
    for _, radix in reversed(digits):
        slots = [(step,) + rest for step in range(radix) for rest in slots]
    return slots


def slot_index(me, digits, steps):
    for (stride, radix), step in zip(digits, steps):
        if step:
            me = moved(me, stride, radix, step)
    return me


def sizes_of(digits):
    sizes, held = [1], 1
    for _, radix in reversed(digits):
        sizes += [held] * (radix - 1)
        held *= radix
    return sizes


def scatter(pieces, axis, count, digits):
    for stride, radix in digits:
        keep = pieces[: len(pieces) - (radix - 1)]
        sent = pieces[len(keep) :]
        got = [send(value, axis, count, stride, radix, step + 1) for step, value in enumerate(sent)]
        at, pieces = 0, []
        for value in keep:
            size = value.shape[0]
            for other in got[::-1]:
                value = value + other[at : at + size]
            at += size
            pieces.append(value)
    return pieces[0][0]


def fetch_kernel(tiles_hbm, vec_hbm, tiles_ref, vec_ref, sems):
    pairs = ((tiles_hbm, tiles_ref), (vec_hbm, vec_ref))
    copies = [pltpu.make_async_copy(a, b, sems.at[i]) for i, (a, b) in enumerate(pairs)]
    for copy in copies:
        copy.start()
    for copy in copies:
        copy.wait()


def fetch(*arrays):
    return pl.pallas_call(
        fetch_kernel,
        out_shape=[jax.ShapeDtypeStruct(a.shape, a.dtype) for a in arrays],
        in_specs=[HBM] * 2,
        out_specs=[VMEM] * 2,
        scratch_shapes=[pltpu.SemaphoreType.DMA((2,))],
        compiler_params=PARAMS,
        cost_estimate=pl.CostEstimate(flops=0, bytes_accessed=8 * 2**20, transcendentals=0),
        name="fetch",
    )(*[pltpu.with_memory_space_constraint(a, pltpu.HBM) for a in arrays])


def products(index_ref, tiles_ref, vec, acc, direct):
    dims = (((1,), (1,)), ((), ())) if direct else (((1,), (0,)), ((), ()))
    slots = tiles_ref.shape[0]
    live = index_ref[2 * slots]
    acc[...] = jnp.zeros_like(acc)
    for t in range(slots):
        row, col = index_ref[t], index_ref[slots + t]
        take, put = (col, row) if direct else (row, col)
        y = lax.dot_general(vec[take], tiles_ref[t], dims, preferred_element_type=jnp.float32)
        acc[put] += jnp.where(t < live, y, 0.0)


def direct_half(index, colset, own, tiles, rows, cols):
    width, size = own[0].shape[1:]
    radix = cols[0][1]
    held = sum(piece.shape[0] for piece in own)
    n_row, n_own = len(colset), len(own)

    def body(index_ref, *refs):
        ins, tiles_ref = refs[: n_row + n_own], refs[n_row + n_own]
        keep_ref, *outs, vec, acc = refs[n_row + n_own + 1 :]
        me_r, me_c = lax.axis_index("row"), lax.axis_index("col")
        where = iter(slots_of(rows))
        for piece in ins[:n_row]:
            for i in range(piece.shape[0]):
                vec[slot_index(me_r, rows, next(where))] = piece[i]
        products(index_ref, tiles_ref, vec, acc, True)
        slots = slots_of(cols)
        for i in range(held):
            keep_ref[i] = acc[slot_index(me_c, cols, slots[i])]
        for step, out in enumerate(outs, 1):
            for i in range(held):
                value = acc[slot_index(me_c, cols, slots[step * held + i])]
                high = value.astype(jnp.bfloat16)
                out[i] = high
                out[held + i] = (value - high.astype(jnp.float32)).astype(jnp.bfloat16)
            at = 2 * held
            for piece in ins[n_row:]:
                for i in range(piece.shape[0]):
                    out[at] = piece[i]
                    at += 1

    return pl.pallas_call(
        body,
        out_shape=[jax.ShapeDtypeStruct((held, width, size), jnp.float32)]
        + [jax.ShapeDtypeStruct((3 * held, width, size), jnp.bfloat16)] * (radix - 1),
        in_specs=[SMEM] + [VMEM] * (n_row + n_own + 1),
        out_specs=[VMEM] * radix,
        scratch_shapes=[
            pltpu.VMEM((math.prod(r for _, r in rows), width, size), jnp.bfloat16),
            pltpu.VMEM((math.prod(r for _, r in cols), width, size), jnp.float32),
        ],
        compiler_params=PARAMS,
        name="direct",
    )(index, *colset, *own, tiles)


def mirror_half(index, own, got, tiles, rows, cols):
    width, size = own[0].shape[1:]
    held = sum(piece.shape[0] for piece in own)
    n_own, n_got = len(own), len(got)
    sizes = sizes_of(rows)

    def body(index_ref, *refs):
        ins, tiles_ref = refs[: n_own + n_got], refs[n_own + n_got]
        *outs, vec, acc = refs[n_own + n_got + 1 :]
        me_r, me_c = lax.axis_index("row"), lax.axis_index("col")
        where = iter(slots_of(cols))
        for piece in ins[:n_own]:
            for i in range(piece.shape[0]):
                vec[slot_index(me_c, cols, next(where))] = piece[i]
        for piece in ins[n_own:]:
            for i in range(held):
                vec[slot_index(me_c, cols, next(where))] = piece[2 * held + i]
        products(index_ref, tiles_ref, vec, acc, False)
        where = iter(slots_of(rows))
        for out in outs:
            for i in range(out.shape[0]):
                out[i] = acc[slot_index(me_r, rows, next(where))]

    return pl.pallas_call(
        body,
        out_shape=[jax.ShapeDtypeStruct((n, width, size), jnp.float32) for n in sizes],
        in_specs=[SMEM] + [VMEM] * (n_own + n_got + 1),
        out_specs=[VMEM] * len(sizes),
        scratch_shapes=[
            pltpu.VMEM((math.prod(r for _, r in cols), width, size), jnp.bfloat16),
            pltpu.VMEM((math.prod(r for _, r in rows), width, size), jnp.float32),
        ],
        compiler_params=PARAMS,
        name="mirror",
    )(index, *own, *got, tiles)


def local(n_rows, n_cols, vectors, tiles, tile_rows, tile_cols, tile_live):
    rows, cols = digits_of(n_rows, 99), digits_of(n_cols, 1)
    inner, outer = cols[0], cols[1:]
    index = jnp.concatenate([tile_rows, tile_cols, tile_live])
    tiles, kept = fetch(tiles, vectors)

    def apply(vec, kept):
        colset = gather(vec, kept, "row", n_rows, rows)
        own = gather(vec, kept, "col", n_cols, outer)
        keep, *packed = direct_half(index, colset, own, tiles, rows, cols)
        got = [send(value, "col", n_cols, *inner, step) for step, value in enumerate(packed, 1)]
        held, at, pieces = keep.shape[0], 0, []
        for size in sizes_of(outer):
            value = keep[at : at + size]
            for other in got[::-1]:
                high, low = other[at : at + size], other[held + at : held + at + size]
                value = value + (high.astype(jnp.float32) + low.astype(jnp.float32))
            at += size
            pieces.append(value)
        if False:
            got[-1] = after(got[-1], pieces[-1])
        mirror = mirror_half(index, own, got, tiles, rows, cols)
        return scatter(pieces, "col", n_cols, outer) + scatter(list(mirror), "row", n_rows, rows)

    first = apply(vectors, kept).astype(jnp.bfloat16)
    second = 2.0 * apply(first, first) - kept.astype(jnp.float32)
    return first, second.astype(jnp.bfloat16)


def solution(mesh):
    both = ("row", "col")
    placed = (P(None, both), P(both, None, None), P(both), P(both), P(both))
    return jax.shard_map(
        functools.partial(local, mesh.shape["row"], mesh.shape["col"]),
        mesh=mesh,
        in_specs=placed,
        out_specs=(P(None, both), P(None, both)),
        check_vma=False,
    )
```

time: 50.2 us -> 47.7 us (0.950)
  starting transfers between devices: 25.6 us -> 22.3 us
  other arithmetic: 0.79 us -> 1.46 us
    ppermute x24 -> x22, starting transfers between devices: 25.6 us -> 22.3 us  [send(): return lax.ppermute(value, axis, pairs)]
    concatenate x1, other arithmetic: 0.08 us -> 0.75 us  [local(): index = jnp.concatenate([tile_rows, tile_cols, tile_live])]
    ppermute x24 -> x22, waiting for transfers between devices: 15.9 us -> 16 us  [send(): return lax.ppermute(value, axis, pairs)]
  transfers between devices with their start and end apart: 24 -> 22, of which waited for: 9 -> 14; matrix products, arithmetic and copies ran while one was open for 0% -> 2% of each run, Pallas kernels for 13% -> 8%
where the time goes in v3:
time: 47.7 us; the launch traced here: 47.5 us
  starting transfers between devices  22.3 us (47%)
  waiting for transfers between devices  16 us (34%)
  Pallas kernels  6.3 us (13%)
  other arithmetic  1.46 us (3%)
  between operations  1.41 us (3%)
    ppermute x22, starting transfers between devices, send(): return lax.ppermute(value, axis, pairs)  22.3 us
    ppermute x22, waiting for transfers between devices, send(): return lax.ppermute(value, axis, pairs)  16 us
    pallas_call x2, Pallas kernels, direct_half(): pl.pallas_call(body, out_shape=[jax.ShapeDtypeStruct((held, width, size),...  2.62 us
    pallas_call x2, Pallas kernels, mirror_half(): pl.pallas_call(body, out_shape=[jax.ShapeDtypeStruct((n, width, size), jn...  2.06 us
    pallas_call x1, Pallas kernels, fetch(): pl.pallas_call(fetch_kernel, out_shape=[jax.ShapeDtypeStruct(a.shape, a.d...  1.61 us
  transfers between devices with their start and end apart: 22, of which 14 were waited for; matrix products, arithmetic and copies ran while one was open for 2% of the time, Pallas kernels for 8%

profile of v3, /device:TPU:0, one launch (start us, length us, event | category | flops | bytes accessed | tf_op | source)
XLA Modules:
  0.0 47.5 jit_solution(9875519682753300835)
XLA Ops:
  0.6 4.1 %collective-permute-start.3 = (bf16[1,32,256]{2,1,0:T(8,128)(2,1)}, bf16[1,32,256]{2,1,0:T(8,128)(2,1)S(1)}, u32[]{:S(2)}, u32[]{:S(2)}) collective-permute-start(bf16[1,32,256]{2,1,0:T(8,128)(2,1)} %bitcast.11), channel_id=1, source_target_pairs={{0,4},{1,5},{2,6},{3,7},{4,0},{5,1},{6,2},{7,3},{8,12},{9,13},{10,... | collective-permute-start | bytes 49160 | tf_op jit(solution)/shard_map/ppermute | solution.py:38
  5.4 0.9 %collective-permute-start.1 = (bf16[1,32,256]{2,1,0:T(8,128)(2,1)}, bf16[1,32,256]{2,1,0:T(8,128)(2,1)S(1)}, u32[]{:S(2)}, u32[]{:S(2)}) collective-permute-start(bf16[1,32,256]{2,1,0:T(8,128)(2,1)} %bitcast.13), channel_id=1, source_target_pairs={{0,16},{8,24},{16,0},{24,8},{1,17},{9,25},{17,1},{25,9},{2,18},{10... | collective-permute-start | bytes 49160 | tf_op jit(solution)/shard_map/ppermute | solution.py:38
  7.2 0.7 %pad_add_fusion.index_ref = s32[33]{0:T(128)S(1)} fusion(s32[1]{0:T(128)S(6)} %copy.7, s32[16]{0:T(128)} %param.8, s32[16]{0:T(128)} %param.7), kind=kLoop, calls=%fused_computation.5 | loop fusion | flops 66 | bytes 264 | tf_op jit(solution)/shard_map/concatenate | solution.py:210
  8.0 1.6 %fetch.1 = (bf16[16,256,256]{2,1,0:T(8,128)(2,1)S(1)}, bf16[32,256]{1,0:T(8,128)(2,1)S(1)}) custom-call(bf16[16,256,256]{2,1,0:T(8,128)(2,1)} %tiles_hbm.1, bf16[32,256]{1,0:T(8,128)(2,1)} %vec_hbm.1), custom_call_target="tpu_custom_call" | custom-call | bytes 8388608 | tf_op jit(solution)/shard_map/fetch/pallas_call | solution.py:101
  9.7 1.3 %direct.2 = (f32[2,32,256]{2,1,0:T(8,128)S(1)}, bf16[6,32,256]{2,1,0:T(8,128)(2,1)S(1)}, bf16[6,32,256]{2,1,0:T(8,128)(2,1)S(1)}, bf16[6,32,256]{2,1,0:T(8,128)(2,1)S(1)}) custom-call(s32[33]{0:T(128)S(1)} %pad_add_fusion.index_ref, bf16[1,32,256]{2,1,0:T(8,128)(2,1)S(1)} %bitcast.7, bf16[1,32,256]{2,1,0:T(8,128)(2,1)S(1)} %collective-permute-done.refs_1_, ...), custom_call_target="tpu_custom_call" | custom-call | tf_op jit(solution)/shard_map/direct/pallas_call | solution.py:155
  11.0 2.6 %collective-permute-start.4 = (bf16[6,32,256]{2,1,0:T(8,128)(2,1)S(1)}, bf16[6,32,256]{2,1,0:T(8,128)(2,1)S(1)}, u32[]{:S(2)}, u32[]{:S(2)}) collective-permute-start(bf16[6,32,256]{2,1,0:T(8,128)(2,1)S(1)} %get-tuple-element.23), channel_id=1, source_target_pairs={{0,3},{1,2},{2,1},{3,0},{4,7},{5,6},{6,5},{7,4},{8,11},{9,10},{10,... | collective-permute-start | bytes 294920 | tf_op jit(solution)/shard_map/ppermute | solution.py:38
  14.5 3.0 %collective-permute-done.4.refs_4_ = bf16[6,32,256]{2,1,0:T(8,128)(2,1)S(1)} collective-permute-done((bf16[6,32,256]{2,1,0:T(8,128)(2,1)S(1)}, bf16[6,32,256]{2,1,0:T(8,128)(2,1)S(1)}, u32[]{:S(2)}, u32[]{:S(2)}) %collective-permute-start.4) | collective-permute-done | bytes 98336 | tf_op jit(solution)/shard_map/ppermute | solution.py:38
  17.6 1.4 %collective-permute-done.5.refs_3_ = bf16[6,32,256]{2,1,0:T(8,128)(2,1)S(1)} collective-permute-done((bf16[6,32,256]{2,1,0:T(8,128)(2,1)S(1)}, bf16[6,32,256]{2,1,0:T(8,128)(2,1)S(1)}, u32[]{:S(2)}, u32[]{:S(2)}) %collective-permute-start.5) | collective-permute-done | bytes 98336 | tf_op jit(solution)/shard_map/ppermute | solution.py:38
  19.4 1.0 %mirror.2 = (f32[1,32,256]{2,1,0:T(8,128)S(1)}, f32[1,32,256]{2,1,0:T(8,128)S(1)}, f32[1,32,256]{2,1,0:T(8,128)S(1)}, f32[1,32,256]{2,1,0:T(8,128)S(1)}) custom-call(s32[33]{0:T(128)S(1)} %pad_add_fusion.index_ref, bf16[1,32,256]{2,1,0:T(8,128)(2,1)S(1)} %bitcast.9, bf16[1,32,256]{2,1,0:T(8,128)(2,1)S(1)} %collective-permute-done.3.refs_5_.refs_1_, ...), custom_call_target="tpu_custom_call" | custom-call | tf_op jit(solution)/shard_map/mirror/pallas_call | solution.py:193
  20.5 1.4 %collective-permute-start.9 = (f32[1,32,256]{2,1,0:T(8,128)S(1)}, f32[1,32,256]{2,1,0:T(8,128)S(1)}, u32[]{:S(2)}, u32[]{:S(2)}) collective-permute-start(f32[1,32,256]{2,1,0:T(8,128)S(1)} %get-tuple-element.28), channel_id=1, source_target_pairs={{0,16},{8,24},{16,0},{24,8},{1,17},{9,25},{17,1},{25,9},{2,18},{10... | collective-permute-start | bytes 98312 | tf_op jit(solution)/shard_map/ppermute | solution.py:38
  22.4 1.5 %collective-permute-done.7 = f32[1,32,256]{2,1,0:T(8,128)S(1)} collective-permute-done((f32[1,32,256]{2,1,0:T(8,128)S(1)}, f32[1,32,256]{2,1,0:T(8,128)S(1)}, u32[]{:S(2)}, u32[]{:S(2)}) %collective-permute-start.7) | collective-permute-done | bytes 32800 | tf_op jit(solution)/shard_map/ppermute | solution.py:38
  24.6 2.7 %collective-permute-start.14 = (bf16[1,32,256]{2,1,0:T(8,128)(2,1)S(1)}, bf16[1,32,256]{2,1,0:T(8,128)(2,1)S(1)}, u32[]{:S(2)}, u32[]{:S(2)}) collective-permute-start(bf16[1,32,256]{2,1,0:T(8,128)(2,1)S(1)} %add_convert_fusion.refs_0_.refs_4_), channel_id=1, source_target_pairs={{0,4},{1,5},{2,6},{3,7},{4,0},{5,1},{6,2},{7,3},{8,12},{9,13},{10,... | collective-permute-start | bytes 49160 | tf_op jit(solution)/shard_map/ppermute | solution.py:38
  27.9 1.0 %collective-permute-start.12 = (bf16[1,32,256]{2,1,0:T(8,128)(2,1)S(1)}, bf16[1,32,256]{2,1,0:T(8,128)(2,1)S(1)}, u32[]{:S(2)}, u32[]{:S(2)}) collective-permute-start(bf16[1,32,256]{2,1,0:T(8,128)(2,1)S(1)} %add_convert_fusion.refs_0_.refs_4_), channel_id=1, source_target_pairs={{0,16},{8,24},{16,0},{24,8},{1,17},{9,25},{17,1},{25,9},{2,18},{10... | collective-permute-start | bytes 49160 | tf_op jit(solution)/shard_map/ppermute | solution.py:38
  29.3 1.2 %collective-permute-done.13.refs_3_ = bf16[1,32,256]{2,1,0:T(8,128)(2,1)S(1)} collective-permute-done((bf16[1,32,256]{2,1,0:T(8,128)(2,1)S(1)}, bf16[1,32,256]{2,1,0:T(8,128)(2,1)S(1)}, u32[]{:S(2)}, u32[]{:S(2)}) %collective-permute-start.13) | collective-permute-done | bytes 16416 | tf_op jit(solution)/shard_map/ppermute | solution.py:38
  30.4 1.3 %collective-permute-done.12.refs_2_ = bf16[1,32,256]{2,1,0:T(8,128)(2,1)S(1)} collective-permute-done((bf16[1,32,256]{2,1,0:T(8,128)(2,1)S(1)}, bf16[1,32,256]{2,1,0:T(8,128)(2,1)S(1)}, u32[]{:S(2)}, u32[]{:S(2)}) %collective-permute-start.12) | collective-permute-done | bytes 16416 | tf_op jit(solution)/shard_map/ppermute | solution.py:38
  31.7 1.3 %direct.3 = (f32[2,32,256]{2,1,0:T(8,128)S(1)}, bf16[6,32,256]{2,1,0:T(8,128)(2,1)S(1)}, bf16[6,32,256]{2,1,0:T(8,128)(2,1)S(1)}, bf16[6,32,256]{2,1,0:T(8,128)(2,1)S(1)}) custom-call(s32[33]{0:T(128)S(1)} %pad_add_fusion.index_ref, bf16[1,32,256]{2,1,0:T(8,128)(2,1)S(1)} %add_convert_fusion.refs_0_.refs_4_, ...), custom_call_target="tpu_custom_call" | custom-call | tf_op jit(solution)/shard_map/direct/pallas_call | solution.py:155
  33.1 2.5 %collective-permute-start.15 = (bf16[6,32,256]{2,1,0:T(8,128)(2,1)S(1)}, bf16[6,32,256]{2,1,0:T(8,128)(2,1)S(1)}, u32[]{:S(2)}, u32[]{:S(2)}) collective-permute-start(bf16[6,32,256]{2,1,0:T(8,128)(2,1)S(1)} %get-tuple-element.31), channel_id=1, source_target_pairs={{0,3},{1,2},{2,1},{3,0},{4,7},{5,6},{6,5},{7,4},{8,11},{9,10},{10,... | collective-permute-start | bytes 294920 | tf_op jit(solution)/shard_map/ppermute | solution.py:38
  36.6 3.0 %collective-permute-done.15.refs_4_ = bf16[6,32,256]{2,1,0:T(8,128)(2,1)S(1)} collective-permute-done((bf16[6,32,256]{2,1,0:T(8,128)(2,1)S(1)}, bf16[6,32,256]{2,1,0:T(8,128)(2,1)S(1)}, u32[]{:S(2)}, u32[]{:S(2)}) %collective-permute-start.15) | collective-permute-done | bytes 98336 | tf_op jit(solution)/shard_map/ppermute | solution.py:38
  39.6 1.3 %collective-permute-done.16.refs_3_ = bf16[6,32,256]{2,1,0:T(8,128)(2,1)S(1)} collective-permute-done((bf16[6,32,256]{2,1,0:T(8,128)(2,1)S(1)}, bf16[6,32,256]{2,1,0:T(8,128)(2,1)S(1)}, u32[]{:S(2)}, u32[]{:S(2)}) %collective-permute-start.16) | collective-permute-done | bytes 98336 | tf_op jit(solution)/shard_map/ppermute | solution.py:38
  41.5 1.0 %mirror.3 = (f32[1,32,256]{2,1,0:T(8,128)S(1)}, f32[1,32,256]{2,1,0:T(8,128)S(1)}, f32[1,32,256]{2,1,0:T(8,128)S(1)}, f32[1,32,256]{2,1,0:T(8,128)S(1)}) custom-call(s32[33]{0:T(128)S(1)} %pad_add_fusion.index_ref, bf16[1,32,256]{2,1,0:T(8,128)(2,1)S(1)} %add_convert_fusion.refs_0_.refs_4_, bf16[1,32,256]{2,1,0:T(8,128)(2,1)S(1)} %collective-permute-done.14.refs_5_.refs_1_, ...), custom_call_target="tpu_custom_call" | custom-call | tf_op jit(solution)/shard_map/mirror/pallas_call | solution.py:193
  42.6 1.1 %collective-permute-start.20 = (f32[1,32,256]{2,1,0:T(8,128)S(1)}, f32[1,32,256]{2,1,0:T(8,128)S(1)}, u32[]{:S(2)}, u32[]{:S(2)}) collective-permute-start(f32[1,32,256]{2,1,0:T(8,128)S(1)} %get-tuple-element.36), channel_id=1, source_target_pairs={{0,16},{8,24},{16,0},{24,8},{1,17},{9,25},{17,1},{25,9},{2,18},{10... | collective-permute-start | bytes 98312 | tf_op jit(solution)/shard_map/ppermute | solution.py:38
  43.7 0.8 %collective-permute-start.21 = (f32[1,32,256]{2,1,0:T(8,128)S(1)}, f32[1,32,256]{2,1,0:T(8,128)S(1)}, u32[]{:S(2)}, u32[]{:S(2)}) collective-permute-start(f32[1,32,256]{2,1,0:T(8,128)S(1)} %get-tuple-element.37), channel_id=1, source_target_pairs={{0,8},{8,0},{16,24},{24,16},{1,9},{9,1},{17,25},{25,17},{2,10},{10... | collective-permute-start | bytes 98312 | tf_op jit(solution)/shard_map/ppermute | solution.py:38
  44.5 1.4 %collective-permute-done.18 = f32[1,32,256]{2,1,0:T(8,128)S(1)} collective-permute-done((f32[1,32,256]{2,1,0:T(8,128)S(1)}, f32[1,32,256]{2,1,0:T(8,128)S(1)}, u32[]{:S(2)}, u32[]{:S(2)}) %collective-permute-start.18) | collective-permute-done | bytes 32800 | tf_op jit(solution)/shard_map/ppermute | solution.py:38
  45.9 0.9 %collective-permute-done.20 = f32[1,32,256]{2,1,0:T(8,128)S(1)} collective-permute-done((f32[1,32,256]{2,1,0:T(8,128)S(1)}, f32[1,32,256]{2,1,0:T(8,128)S(1)}, u32[]{:S(2)}, u32[]{:S(2)}) %collective-permute-start.20) | collective-permute-done | bytes 32800 | tf_op jit(solution)/shard_map/ppermute | solution.py:38
  (32 shorter events, 7.0 us)
Async XLA Ops:
  0.6 9.0 %collective-permute-start.3 = (bf16[1,32,256]{2,1,0:T(8,128)(2,1)}, bf16[1,32,256]{2,1,0:T(8,128)(2,1)S(1)}, u32[]{:S(2)}, u32[]{:S(2)}) collective-permute-start(bf16[1,32,256]{2,1,0:T(8,128)(2,1)} %bitcast.11), channel_id=1, source_target_pairs={{0,4},{1,5},{2,6},{3,7},{4,0},{5,1},{6,2},{7,3},{8,12},{9,13},{10,... | collective-permute-start | bytes 49160 | tf_op jit(solution)/shard_map/ppermute | solution.py:38
  4.7 4.9 %collective-permute-start.2 = (bf16[1,32,256]{2,1,0:T(8,128)(2,1)}, bf16[1,32,256]{2,1,0:T(8,128)(2,1)S(1)}, u32[]{:S(2)}, u32[]{:S(2)}) collective-permute-start(bf16[1,32,256]{2,1,0:T(8,128)(2,1)} %bitcast.12), channel_id=1, source_target_pairs={{0,24},{8,16},{16,8},{24,0},{1,25},{9,17},{17,9},{25,1},{2,26},{10... | collective-permute-start | bytes 49160 | tf_op jit(solution)/shard_map/ppermute | solution.py:38
  5.4 4.3 %collective-permute-start.1 = (bf16[1,32,256]{2,1,0:T(8,128)(2,1)}, bf16[1,32,256]{2,1,0:T(8,128)(2,1)S(1)}, u32[]{:S(2)}, u32[]{:S(2)}) collective-permute-start(bf16[1,32,256]{2,1,0:T(8,128)(2,1)} %bitcast.13), channel_id=1, source_target_pairs={{0,16},{8,24},{16,0},{24,8},{1,17},{9,25},{17,1},{25,9},{2,18},{10... | collective-permute-start | bytes 49160 | tf_op jit(solution)/shard_map/ppermute | solution.py:38
  6.3 3.4 %collective-permute-start = (bf16[1,32,256]{2,1,0:T(8,128)(2,1)}, bf16[1,32,256]{2,1,0:T(8,128)(2,1)S(1)}, u32[]{:S(2)}, u32[]{:S(2)}) collective-permute-start(bf16[1,32,256]{2,1,0:T(8,128)(2,1)} %bitcast.14), channel_id=1, source_target_pairs={{0,8},{8,0},{16,24},{24,16},{1,9},{9,1},{17,25},{25,17},{2,10},{10... | collective-permute-start | bytes 49160 | tf_op jit(solution)/shard_map/ppermute | solution.py:38
  11.0 6.6 %collective-permute-start.4 = (bf16[6,32,256]{2,1,0:T(8,128)(2,1)S(1)}, bf16[6,32,256]{2,1,0:T(8,128)(2,1)S(1)}, u32[]{:S(2)}, u32[]{:S(2)}) collective-permute-start(bf16[6,32,256]{2,1,0:T(8,128)(2,1)S(1)} %get-tuple-element.23), channel_id=1, source_target_pairs={{0,3},{1,2},{2,1},{3,0},{4,7},{5,6},{6,5},{7,4},{8,11},{9,10},{10,... | collective-permute-start | bytes 294920 | tf_op jit(solution)/shard_map/ppermute | solution.py:38
  13.6 5.4 %collective-permute-start.5 = (bf16[6,32,256]{2,1,0:T(8,128)(2,1)S(1)}, bf16[6,32,256]{2,1,0:T(8,128)(2,1)S(1)}, u32[]{:S(2)}, u32[]{:S(2)}) collective-permute-start(bf16[6,32,256]{2,1,0:T(8,128)(2,1)S(1)} %get-tuple-element.24), channel_id=1, source_target_pairs={{0,2},{1,3},{2,0},{3,1},{4,6},{5,7},{6,4},{7,5},{8,10},{9,11},{10,... | collective-permute-start | bytes 294920 | tf_op jit(solution)/shard_map/ppermute | solution.py:38
  14.0 5.0 %collective-permute-start.6 = (bf16[6,32,256]{2,1,0:T(8,128)(2,1)S(1)}, bf16[6,32,256]{2,1,0:T(8,128)(2,1)S(1)}, u32[]{:S(2)}, u32[]{:S(2)}) collective-permute-start(bf16[6,32,256]{2,1,0:T(8,128)(2,1)S(1)} %get-tuple-element.25), channel_id=1, source_target_pairs={{0,1},{1,0},{2,3},{3,2},{4,5},{5,4},{6,7},{7,6},{8,9},{9,8},{10,11... | collective-permute-start | bytes 294920 | tf_op jit(solution)/shard_map/ppermute | solution.py:38
  19.0 4.9 %collective-permute-start.7 = (f32[1,32,256]{2,1,0:T(8,128)S(1)}, f32[1,32,256]{2,1,0:T(8,128)S(1)}, u32[]{:S(2)}, u32[]{:S(2)}) collective-permute-start(f32[1,32,256]{2,1,0:T(8,128)S(1)} %add_add_fusion.1), channel_id=1, source_target_pairs={{0,4},{1,5},{2,6},{3,7},{4,0},{5,1},{6,2},{7,3},{8,12},{9,13},{10,... | collective-permute-start | bytes 98312 | tf_op jit(solution)/shard_map/ppermute | solution.py:38
  20.4 3.7 %collective-permute-start.8 = (f32[1,32,256]{2,1,0:T(8,128)S(1)}, f32[1,32,256]{2,1,0:T(8,128)S(1)}, u32[]{:S(2)}, u32[]{:S(2)}) collective-permute-start(f32[1,32,256]{2,1,0:T(8,128)S(1)} %get-tuple-element.27), channel_id=1, source_target_pairs={{0,24},{8,16},{16,8},{24,0},{1,25},{9,17},{17,9},{25,1},{2,26},{10... | collective-permute-start | bytes 98312 | tf_op jit(solution)/shard_map/ppermute | solution.py:38
  20.5 4.0 %collective-permute-start.9 = (f32[1,32,256]{2,1,0:T(8,128)S(1)}, f32[1,32,256]{2,1,0:T(8,128)S(1)}, u32[]{:S(2)}, u32[]{:S(2)}) collective-permute-start(f32[1,32,256]{2,1,0:T(8,128)S(1)} %get-tuple-element.28), channel_id=1, source_target_pairs={{0,16},{8,24},{16,0},{24,8},{1,17},{9,25},{17,1},{25,9},{2,18},{10... | collective-permute-start | bytes 98312 | tf_op jit(solution)/shard_map/ppermute | solution.py:38
  22.0 2.5 %collective-permute-start.10 = (f32[1,32,256]{2,1,0:T(8,128)S(1)}, f32[1,32,256]{2,1,0:T(8,128)S(1)}, u32[]{:S(2)}, u32[]{:S(2)}) collective-permute-start(f32[1,32,256]{2,1,0:T(8,128)S(1)} %get-tuple-element.29), channel_id=1, source_target_pairs={{0,8},{8,0},{16,24},{24,16},{1,9},{9,1},{17,25},{25,17},{2,10},{10... | collective-permute-start | bytes 98312 | tf_op jit(solution)/shard_map/ppermute | solution.py:38
  24.5 18.0 %copy-start = (bf16[1,32,256]{2,1,0:T(8,128)(2,1)}, bf16[1,32,256]{2,1,0:T(8,128)(2,1)S(1)}, u32[]{:S(2)}) copy-start(bf16[1,32,256]{2,1,0:T(8,128)(2,1)S(1)} %add_convert_fusion.refs_0_.refs_4_) | copy-start | bytes 49156
  24.6 4.7 %collective-permute-start.14 = (bf16[1,32,256]{2,1,0:T(8,128)(2,1)S(1)}, bf16[1,32,256]{2,1,0:T(8,128)(2,1)S(1)}, u32[]{:S(2)}, u32[]{:S(2)}) collective-permute-start(bf16[1,32,256]{2,1,0:T(8,128)(2,1)S(1)} %add_convert_fusion.refs_0_.refs_4_), channel_id=1, source_target_pairs={{0,4},{1,5},{2,6},{3,7},{4,0},{5,1},{6,2},{7,3},{8,12},{9,13},{10,... | collective-permute-start | bytes 49160 | tf_op jit(solution)/shard_map/ppermute | solution.py:38
  27.2 3.2 %collective-permute-start.13 = (bf16[1,32,256]{2,1,0:T(8,128)(2,1)S(1)}, bf16[1,32,256]{2,1,0:T(8,128)(2,1)S(1)}, u32[]{:S(2)}, u32[]{:S(2)}) collective-permute-start(bf16[1,32,256]{2,1,0:T(8,128)(2,1)S(1)} %add_convert_fusion.refs_0_.refs_4_), channel_id=1, source_target_pairs={{0,24},{8,16},{16,8},{24,0},{1,25},{9,17},{17,9},{25,1},{2,26},{10... | collective-permute-start | bytes 49160 | tf_op jit(solution)/shard_map/ppermute | solution.py:38
  27.9 3.9 %collective-permute-start.12 = (bf16[1,32,256]{2,1,0:T(8,128)(2,1)S(1)}, bf16[1,32,256]{2,1,0:T(8,128)(2,1)S(1)}, u32[]{:S(2)}, u32[]{:S(2)}) collective-permute-start(bf16[1,32,256]{2,1,0:T(8,128)(2,1)S(1)} %add_convert_fusion.refs_0_.refs_4_), channel_id=1, source_target_pairs={{0,16},{8,24},{16,0},{24,8},{1,17},{9,25},{17,1},{25,9},{2,18},{10... | collective-permute-start | bytes 49160 | tf_op jit(solution)/shard_map/ppermute | solution.py:38
  28.8 2.9 %collective-permute-start.11 = (bf16[1,32,256]{2,1,0:T(8,128)(2,1)S(1)}, bf16[1,32,256]{2,1,0:T(8,128)(2,1)S(1)}, u32[]{:S(2)}, u32[]{:S(2)}) collective-permute-start(bf16[1,32,256]{2,1,0:T(8,128)(2,1)S(1)} %add_convert_fusion.refs_0_.refs_4_), channel_id=1, source_target_pairs={{0,8},{8,0},{16,24},{24,16},{1,9},{9,1},{17,25},{25,17},{2,10},{10... | collective-permute-start | bytes 49160 | tf_op jit(solution)/shard_map/ppermute | solution.py:38
  33.1 6.5 %collective-permute-start.15 = (bf16[6,32,256]{2,1,0:T(8,128)(2,1)S(1)}, bf16[6,32,256]{2,1,0:T(8,128)(2,1)S(1)}, u32[]{:S(2)}, u32[]{:S(2)}) collective-permute-start(bf16[6,32,256]{2,1,0:T(8,128)(2,1)S(1)} %get-tuple-element.31), channel_id=1, source_target_pairs={{0,3},{1,2},{2,1},{3,0},{4,7},{5,6},{6,5},{7,4},{8,11},{9,10},{10,... | collective-permute-start | bytes 294920 | tf_op jit(solution)/shard_map/ppermute | solution.py:38
  35.6 5.3 %collective-permute-start.16 = (bf16[6,32,256]{2,1,0:T(8,128)(2,1)S(1)}, bf16[6,32,256]{2,1,0:T(8,128)(2,1)S(1)}, u32[]{:S(2)}, u32[]{:S(2)}) collective-permute-start(bf16[6,32,256]{2,1,0:T(8,128)(2,1)S(1)} %get-tuple-element.32), channel_id=1, source_target_pairs={{0,2},{1,3},{2,0},{3,1},{4,6},{5,7},{6,4},{7,5},{8,10},{9,11},{10,... | collective-permute-start | bytes 294920 | tf_op jit(solution)/shard_map/ppermute | solution.py:38
  36.0 4.9 %collective-permute-start.17 = (bf16[6,32,256]{2,1,0:T(8,128)(2,1)S(1)}, bf16[6,32,256]{2,1,0:T(8,128)(2,1)S(1)}, u32[]{:S(2)}, u32[]{:S(2)}) collective-permute-start(bf16[6,32,256]{2,1,0:T(8,128)(2,1)S(1)} %get-tuple-element.33), channel_id=1, source_target_pairs={{0,1},{1,0},{2,3},{3,2},{4,5},{5,4},{6,7},{7,6},{8,9},{9,8},{10,11... | collective-permute-start | bytes 294920 | tf_op jit(solution)/shard_map/ppermute | solution.py:38
  41.0 4.9 %collective-permute-start.18 = (f32[1,32,256]{2,1,0:T(8,128)S(1)}, f32[1,32,256]{2,1,0:T(8,128)S(1)}, u32[]{:S(2)}, u32[]{:S(2)}) collective-permute-start(f32[1,32,256]{2,1,0:T(8,128)S(1)} %add_add_fusion), channel_id=1, source_target_pairs={{0,4},{1,5},{2,6},{3,7},{4,0},{5,1},{6,2},{7,3},{8,12},{9,13},{10,... | collective-permute-start | bytes 98312 | tf_op jit(solution)/shard_map/ppermute | solution.py:38
  42.5 3.4 %collective-permute-start.19 = (f32[1,32,256]{2,1,0:T(8,128)S(1)}, f32[1,32,256]{2,1,0:T(8,128)S(1)}, u32[]{:S(2)}, u32[]{:S(2)}) collective-permute-start(f32[1,32,256]{2,1,0:T(8,128)S(1)} %get-tuple-element.35), channel_id=1, source_target_pairs={{0,24},{8,16},{16,8},{24,0},{1,25},{9,17},{17,9},{25,1},{2,26},{10... | collective-permute-start | bytes 98312 | tf_op jit(solution)/shard_map/ppermute | solution.py:38
  42.6 4.2 %collective-permute-start.20 = (f32[1,32,256]{2,1,0:T(8,128)S(1)}, f32[1,32,256]{2,1,0:T(8,128)S(1)}, u32[]{:S(2)}, u32[]{:S(2)}) collective-permute-start(f32[1,32,256]{2,1,0:T(8,128)S(1)} %get-tuple-element.36), channel_id=1, source_target_pairs={{0,16},{8,24},{16,0},{24,8},{1,17},{9,25},{17,1},{25,9},{2,18},{10... | collective-permute-start | bytes 98312 | tf_op jit(solution)/shard_map/ppermute | solution.py:38
  43.7 3.2 %collective-permute-start.21 = (f32[1,32,256]{2,1,0:T(8,128)S(1)}, f32[1,32,256]{2,1,0:T(8,128)S(1)}, u32[]{:S(2)}, u32[]{:S(2)}) collective-permute-start(f32[1,32,256]{2,1,0:T(8,128)S(1)} %get-tuple-element.37), channel_id=1, source_target_pairs={{0,8},{8,0},{16,24},{24,16},{1,9},{9,1},{17,25},{25,17},{2,10},{10... | collective-permute-start | bytes 98312 | tf_op jit(solution)/shard_map/ppermute | solution.py:38

commit v4 on v3

--- a/solution.py
+++ b/solution.py
@@ -8,7 +8,6 @@
 from jax.experimental.pallas import tpu as pltpu
 from jax.sharding import PartitionSpec as P
 
-SMEM = pl.BlockSpec(memory_space=pltpu.SMEM)
 VMEM = pl.BlockSpec(memory_space=pltpu.VMEM)
 HBM = pl.BlockSpec(memory_space=pltpu.HBM)
 PARAMS = pltpu.CompilerParams(vmem_limit_bytes=16 * 2**20)
@@ -36,10 +35,6 @@
 def send(value, axis, count, stride, radix, step):
     pairs = [(i, moved(i, stride, radix, step)) for i in range(count)]
     return lax.ppermute(value, axis, pairs)
-
-
-def after(value, *others):
-    return lax.optimization_barrier((value, *others))[0]
 
 
 def gather(block, kept, axis, count, digits):
@@ -110,25 +105,24 @@
     )(*[pltpu.with_memory_space_constraint(a, pltpu.HBM) for a in arrays])
 
 
-def products(index_ref, tiles_ref, vec, acc, direct):
+def products(code_ref, tiles_ref, vec, acc, direct):
     dims = (((1,), (1,)), ((), ())) if direct else (((1,), (0,)), ((), ()))
-    slots = tiles_ref.shape[0]
-    live = index_ref[2 * slots]
     acc[...] = jnp.zeros_like(acc)
-    for t in range(slots):
-        row, col = index_ref[t], index_ref[slots + t]
+    for t in range(tiles_ref.shape[0]):
+        code = code_ref[t, 0]
+        row, col, used = code & 4095, (code >> 12) & 4095, code >> 24
         take, put = (col, row) if direct else (row, col)
         y = lax.dot_general(vec[take], tiles_ref[t], dims, preferred_element_type=jnp.float32)
-        acc[put] += jnp.where(t < live, y, 0.0)
-
-
-def direct_half(index, colset, own, tiles, rows, cols):
+        acc[put] += jnp.where(used > 0, y, 0.0)
+
+
+def direct_half(codes, colset, own, tiles, rows, cols):
     width, size = own[0].shape[1:]
     radix = cols[0][1]
     held = sum(piece.shape[0] for piece in own)
     n_row, n_own = len(colset), len(own)
 
-    def body(index_ref, *refs):
+    def body(code_ref, *refs):
         ins, tiles_ref = refs[: n_row + n_own], refs[n_row + n_own]
         keep_ref, *outs, vec, acc = refs[n_row + n_own + 1 :]
         me_r, me_c = lax.axis_index("row"), lax.axis_index("col")
@@ -136,7 +130,7 @@
         for piece in ins[:n_row]:
             for i in range(piece.shape[0]):
                 vec[slot_index(me_r, rows, next(where))] = piece[i]
-        products(index_ref, tiles_ref, vec, acc, True)
+        products(code_ref, tiles_ref, vec, acc, True)
         slots = slots_of(cols)
         for i in range(held):
             keep_ref[i] = acc[slot_index(me_c, cols, slots[i])]
@@ -156,7 +150,7 @@
         body,
         out_shape=[jax.ShapeDtypeStruct((held, width, size), jnp.float32)]
         + [jax.ShapeDtypeStruct((3 * held, width, size), jnp.bfloat16)] * (radix - 1),
-        in_specs=[SMEM] + [VMEM] * (n_row + n_own + 1),
+        in_specs=[VMEM] * (n_row + n_own + 2),
         out_specs=[VMEM] * radix,
         scratch_shapes=[
             pltpu.VMEM((math.prod(r for _, r in rows), width, size), jnp.bfloat16),
@@ -164,16 +158,16 @@
         ],
         compiler_params=PARAMS,
         name="direct",
-    )(index, *colset, *own, tiles)
-
-
-def mirror_half(index, own, got, tiles, rows, cols):
+    )(codes, *colset, *own, tiles)
+
+
+def mirror_half(codes, own, got, tiles, rows, cols):
     width, size = own[0].shape[1:]
     held = sum(piece.shape[0] for piece in own)
     n_own, n_got = len(own), len(got)
     sizes = sizes_of(rows)
 
-    def body(index_ref, *refs):
+    def body(code_ref, *refs):
         ins, tiles_ref = refs[: n_own + n_got], refs[n_own + n_got]
         *outs, vec, acc = refs[n_own + n_got + 1 :]
         me_r, me_c = lax.axis_index("row"), lax.axis_index("col")
@@ -184,7 +178,7 @@
         for piece in ins[n_own:]:
             for i in range(held):
                 vec[slot_index(me_c, cols, next(where))] = piece[2 * held + i]
-        products(index_ref, tiles_ref, vec, acc, False)
+        products(code_ref, tiles_ref, vec, acc, False)
         where = iter(slots_of(rows))
         for out in outs:
             for i in range(out.shape[0]):
@@ -193,7 +187,7 @@
     return pl.pallas_call(
         body,
         out_shape=[jax.ShapeDtypeStruct((n, width, size), jnp.float32) for n in sizes],
-        in_specs=[SMEM] + [VMEM] * (n_own + n_got + 1),
+        in_specs=[VMEM] * (n_own + n_got + 2),
         out_specs=[VMEM] * len(sizes),
         scratch_shapes=[
             pltpu.VMEM((math.prod(r for _, r in cols), width, size), jnp.bfloat16),
@@ -201,19 +195,20 @@
         ],
         compiler_params=PARAMS,
         name="mirror",
-    )(index, *own, *got, tiles)
+    )(codes, *own, *got, tiles)
 
 
 def local(n_rows, n_cols, vectors, tiles, tile_rows, tile_cols, tile_live):
     rows, cols = digits_of(n_rows, 99), digits_of(n_cols, 1)
     inner, outer = cols[0], cols[1:]
-    index = jnp.concatenate([tile_rows, tile_cols, tile_live])
+    used = (jnp.arange(tile_rows.shape[0], dtype=jnp.int32) < tile_live[0]).astype(jnp.int32)
+    codes = jnp.broadcast_to((tile_rows + tile_cols * 4096 + used * 4096**2)[:, None], (tile_rows.shape[0], 128))
     tiles, kept = fetch(tiles, vectors)
 
     def apply(vec, kept):
         colset = gather(vec, kept, "row", n_rows, rows)
         own = gather(vec, kept, "col", n_cols, outer)
-        keep, *packed = direct_half(index, colset, own, tiles, rows, cols)
+        keep, *packed = direct_half(codes, colset, own, tiles, rows, cols)
         got = [send(value, "col", n_cols, *inner, step) for step, value in enumerate(packed, 1)]
         held, at, pieces = keep.shape[0], 0, []
         for size in sizes_of(outer):
@@ -223,9 +218,7 @@
                 value = value + (high.astype(jnp.float32) + low.astype(jnp.float32))
             at += size
             pieces.append(value)
-        if False:
-            got[-1] = after(got[-1], pieces[-1])
-        mirror = mirror_half(index, own, got, tiles, rows, cols)
+        mirror = mirror_half(codes, own, got, tiles, rows, cols)
         return scatter(pieces, "col", n_cols, outer) + scatter(list(mirror), "row", n_rows, rows)
 
     first = apply(vectors, kept).astype(jnp.bfloat16)

time: 47.7 us -> 45.6 us (0.956)
  Pallas kernels: 6.3 us -> 4.2 us
    pallas_call x2, Pallas kernels: 2.06 us -> 1.01 us  [mirror_half(): pl.pallas_call(body, out_shape=[jax.ShapeDtypeStruct((n, width, size), jn...]
    pallas_call x2, Pallas kernels: 2.62 us -> 1.58 us  [direct_half(): pl.pallas_call(body, out_shape=[jax.ShapeDtypeStruct((held, width, size),...]
    concatenate x1 -> x0, other arithmetic: 0.75 us -> none  [local(): index = jnp.concatenate([tile_rows, tile_cols, tile_live])]
    add x0 -> x1, other arithmetic: none -> 0.68 us  [local(): tile_rows + tile_cols * 4096 + used * 4096 ** 2]
  transfers between devices with their start and end apart: 22 -> 22, of which waited for: 14 -> 12; matrix products, arithmetic and copies ran while one was open for 2% -> 1% of each run, Pallas kernels for 8% -> 6%
where the time goes in v4:
time: 45.6 us; the launch traced here: 45.5 us
  starting transfers between devices  22.4 us (49%)
  waiting for transfers between devices  16 us (35%)
  Pallas kernels  4.2 us (9%)
  between operations  1.41 us (3%)
  other arithmetic  1.39 us (3%)
    ppermute x22, starting transfers between devices, send(): return lax.ppermute(value, axis, pairs)  22.4 us
    ppermute x22, waiting for transfers between devices, send(): return lax.ppermute(value, axis, pairs)  16 us
    pallas_call x1, Pallas kernels, fetch(): pl.pallas_call(fetch_kernel, out_shape=[jax.ShapeDtypeStruct(a.shape, a.d...  1.61 us
    pallas_call x2, Pallas kernels, direct_half(): pl.pallas_call(body, out_shape=[jax.ShapeDtypeStruct((held, width, size),...  1.58 us
    pallas_call x2, Pallas kernels, mirror_half(): pl.pallas_call(body, out_shape=[jax.ShapeDtypeStruct((n, width, size), jn...  1.01 us
  transfers between devices with their start and end apart: 22, of which 12 were waited for; matrix products, arithmetic and copies ran while one was open for 1% of the time, Pallas kernels for 6%

profile of v4, /device:TPU:0, one launch (start us, length us, event | category | flops | bytes accessed | tf_op | source)
XLA Modules:
  0.0 45.5 jit_solution(15419564293186812370)
XLA Ops:
  0.6 4.1 %collective-permute-start.3 = (bf16[1,32,256]{2,1,0:T(8,128)(2,1)}, bf16[1,32,256]{2,1,0:T(8,128)(2,1)S(1)}, u32[]{:S(2)}, u32[]{:S(2)}) collective-permute-start(bf16[1,32,256]{2,1,0:T(8,128)(2,1)} %bitcast.13), channel_id=1, source_target_pairs={{0,4},{1,5},{2,6},{3,7},{4,0},{5,1},{6,2},{7,3},{8,12},{9,13},{10,... | collective-permute-start | bytes 49160 | tf_op jit(solution)/shard_map/ppermute | solution.py:37
  4.7 0.7 %collective-permute-start.2 = (bf16[1,32,256]{2,1,0:T(8,128)(2,1)}, bf16[1,32,256]{2,1,0:T(8,128)(2,1)S(1)}, u32[]{:S(2)}, u32[]{:S(2)}) collective-permute-start(bf16[1,32,256]{2,1,0:T(8,128)(2,1)} %bitcast.14), channel_id=1, source_target_pairs={{0,24},{8,16},{16,8},{24,0},{1,25},{9,17},{17,9},{25,1},{2,26},{10... | collective-permute-start | bytes 49160 | tf_op jit(solution)/shard_map/ppermute | solution.py:37
  5.4 0.9 %collective-permute-start.1 = (bf16[1,32,256]{2,1,0:T(8,128)(2,1)}, bf16[1,32,256]{2,1,0:T(8,128)(2,1)S(1)}, u32[]{:S(2)}, u32[]{:S(2)}) collective-permute-start(bf16[1,32,256]{2,1,0:T(8,128)(2,1)} %bitcast.15), channel_id=1, source_target_pairs={{0,16},{8,24},{16,0},{24,8},{1,17},{9,25},{17,1},{25,9},{2,18},{10... | collective-permute-start | bytes 49160 | tf_op jit(solution)/shard_map/ppermute | solution.py:37
  7.2 0.7 %fusion.1 = s32[16]{0:T(128)S(1)} fusion(s32[16]{0:T(128)} %param.7, s32[16]{0:T(128)} %param.8, s32[]{:T(128)} %bitcast.8), kind=kLoop, calls=%fused_computation.6 | loop fusion | flops 80 | bytes 196 | tf_op jit(solution)/shard_map/add | solution.py:205
  7.9 1.6 %fetch.1 = (bf16[16,256,256]{2,1,0:T(8,128)(2,1)S(1)}, bf16[32,256]{1,0:T(8,128)(2,1)S(1)}) custom-call(bf16[16,256,256]{2,1,0:T(8,128)(2,1)} %tiles_hbm.1, bf16[32,256]{1,0:T(8,128)(2,1)} %vec_hbm.1), custom_call_target="tpu_custom_call" | custom-call | bytes 8388608 | tf_op jit(solution)/shard_map/fetch/pallas_call | solution.py:96
  9.7 0.8 %direct.2 = (f32[2,32,256]{2,1,0:T(8,128)S(1)}, bf16[6,32,256]{2,1,0:T(8,128)(2,1)S(1)}, bf16[6,32,256]{2,1,0:T(8,128)(2,1)S(1)}, bf16[6,32,256]{2,1,0:T(8,128)(2,1)S(1)}) custom-call(s32[16,128]{1,0:T(8,128)S(1)} %broadcast_in_dim.6.code_ref, bf16[1,32,256]{2,1,0:T(8,128)(2,1)S(1)} %bitcast.9, bf16[1,32,256]{2,1,0:T(8,128)(2,1)S(1)} %collective-permute-done.refs_1_, ...), custom_call_target="tpu_custom_call" | custom-call | tf_op jit(solution)/shard_map/direct/pallas_call | solution.py:149
  10.4 2.6 %collective-permute-start.4 = (bf16[6,32,256]{2,1,0:T(8,128)(2,1)S(1)}, bf16[6,32,256]{2,1,0:T(8,128)(2,1)S(1)}, u32[]{:S(2)}, u32[]{:S(2)}) collective-permute-start(bf16[6,32,256]{2,1,0:T(8,128)(2,1)S(1)} %get-tuple-element.23), channel_id=1, source_target_pairs={{0,3},{1,2},{2,1},{3,0},{4,7},{5,6},{6,5},{7,4},{8,11},{9,10},{10,... | collective-permute-start | bytes 294920 | tf_op jit(solution)/shard_map/ppermute | solution.py:37
  14.0 3.0 %collective-permute-done.4.refs_4_ = bf16[6,32,256]{2,1,0:T(8,128)(2,1)S(1)} collective-permute-done((bf16[6,32,256]{2,1,0:T(8,128)(2,1)S(1)}, bf16[6,32,256]{2,1,0:T(8,128)(2,1)S(1)}, u32[]{:S(2)}, u32[]{:S(2)}) %collective-permute-start.4) | collective-permute-done | bytes 98336 | tf_op jit(solution)/shard_map/ppermute | solution.py:37
  17.1 1.4 %collective-permute-done.5.refs_3_ = bf16[6,32,256]{2,1,0:T(8,128)(2,1)S(1)} collective-permute-done((bf16[6,32,256]{2,1,0:T(8,128)(2,1)S(1)}, bf16[6,32,256]{2,1,0:T(8,128)(2,1)S(1)}, u32[]{:S(2)}, u32[]{:S(2)}) %collective-permute-start.5) | collective-permute-done | bytes 98336 | tf_op jit(solution)/shard_map/ppermute | solution.py:37
  19.5 1.4 %collective-permute-start.9 = (f32[1,32,256]{2,1,0:T(8,128)S(1)}, f32[1,32,256]{2,1,0:T(8,128)S(1)}, u32[]{:S(2)}, u32[]{:S(2)}) collective-permute-start(f32[1,32,256]{2,1,0:T(8,128)S(1)} %get-tuple-element.28), channel_id=1, source_target_pairs={{0,16},{8,24},{16,0},{24,8},{1,17},{9,25},{17,1},{25,9},{2,18},{10... | collective-permute-start | bytes 98312 | tf_op jit(solution)/shard_map/ppermute | solution.py:37
  21.3 2.1 %collective-permute-done.7 = f32[1,32,256]{2,1,0:T(8,128)S(1)} collective-permute-done((f32[1,32,256]{2,1,0:T(8,128)S(1)}, f32[1,32,256]{2,1,0:T(8,128)S(1)}, u32[]{:S(2)}, u32[]{:S(2)}) %collective-permute-start.7) | collective-permute-done | bytes 32800 | tf_op jit(solution)/shard_map/ppermute | solution.py:37
  23.5 2.7 %collective-permute-start.14 = (bf16[1,32,256]{2,1,0:T(8,128)(2,1)S(1)}, bf16[1,32,256]{2,1,0:T(8,128)(2,1)S(1)}, u32[]{:S(2)}, u32[]{:S(2)}) collective-permute-start(bf16[1,32,256]{2,1,0:T(8,128)(2,1)S(1)} %add_convert_fusion.refs_0_.refs_4_), channel_id=1, source_target_pairs={{0,4},{1,5},{2,6},{3,7},{4,0},{5,1},{6,2},{7,3},{8,12},{9,13},{10,... | collective-permute-start | bytes 49160 | tf_op jit(solution)/shard_map/ppermute | solution.py:37
  26.2 0.6 %collective-permute-start.13 = (bf16[1,32,256]{2,1,0:T(8,128)(2,1)S(1)}, bf16[1,32,256]{2,1,0:T(8,128)(2,1)S(1)}, u32[]{:S(2)}, u32[]{:S(2)}) collective-permute-start(bf16[1,32,256]{2,1,0:T(8,128)(2,1)S(1)} %add_convert_fusion.refs_0_.refs_4_), channel_id=1, source_target_pairs={{0,24},{8,16},{16,8},{24,0},{1,25},{9,17},{17,9},{25,1},{2,26},{10... | collective-permute-start | bytes 49160 | tf_op jit(solution)/shard_map/ppermute | solution.py:37
  26.8 1.0 %collective-permute-start.12 = (bf16[1,32,256]{2,1,0:T(8,128)(2,1)S(1)}, bf16[1,32,256]{2,1,0:T(8,128)(2,1)S(1)}, u32[]{:S(2)}, u32[]{:S(2)}) collective-permute-start(bf16[1,32,256]{2,1,0:T(8,128)(2,1)S(1)} %add_convert_fusion.refs_0_.refs_4_), channel_id=1, source_target_pairs={{0,16},{8,24},{16,0},{24,8},{1,17},{9,25},{17,1},{25,9},{2,18},{10... | collective-permute-start | bytes 49160 | tf_op jit(solution)/shard_map/ppermute | solution.py:37
  28.2 1.2 %collective-permute-done.13.refs_3_ = bf16[1,32,256]{2,1,0:T(8,128)(2,1)S(1)} collective-permute-done((bf16[1,32,256]{2,1,0:T(8,128)(2,1)S(1)}, bf16[1,32,256]{2,1,0:T(8,128)(2,1)S(1)}, u32[]{:S(2)}, u32[]{:S(2)}) %collective-permute-start.13) | collective-permute-done | bytes 16416 | tf_op jit(solution)/shard_map/ppermute | solution.py:37
  29.4 1.3 %collective-permute-done.12.refs_2_ = bf16[1,32,256]{2,1,0:T(8,128)(2,1)S(1)} collective-permute-done((bf16[1,32,256]{2,1,0:T(8,128)(2,1)S(1)}, bf16[1,32,256]{2,1,0:T(8,128)(2,1)S(1)}, u32[]{:S(2)}, u32[]{:S(2)}) %collective-permute-start.12) | collective-permute-done | bytes 16416 | tf_op jit(solution)/shard_map/ppermute | solution.py:37
  30.7 0.8 %direct.3 = (f32[2,32,256]{2,1,0:T(8,128)S(1)}, bf16[6,32,256]{2,1,0:T(8,128)(2,1)S(1)}, bf16[6,32,256]{2,1,0:T(8,128)(2,1)S(1)}, bf16[6,32,256]{2,1,0:T(8,128)(2,1)S(1)}) custom-call(s32[16,128]{1,0:T(8,128)S(1)} %broadcast_in_dim.6.code_ref, bf16[1,32,256]{2,1,0:T(8,128)(2,1)S(1)} %add_convert_fusion.refs_0_.refs_4_, ...), custom_call_target="tpu_custom_call" | custom-call | tf_op jit(solution)/shard_map/direct/pallas_call | solution.py:149
  31.5 2.5 %collective-permute-start.15 = (bf16[6,32,256]{2,1,0:T(8,128)(2,1)S(1)}, bf16[6,32,256]{2,1,0:T(8,128)(2,1)S(1)}, u32[]{:S(2)}, u32[]{:S(2)}) collective-permute-start(bf16[6,32,256]{2,1,0:T(8,128)(2,1)S(1)} %get-tuple-element.31), channel_id=1, source_target_pairs={{0,3},{1,2},{2,1},{3,0},{4,7},{5,6},{6,5},{7,4},{8,11},{9,10},{10,... | collective-permute-start | bytes 294920 | tf_op jit(solution)/shard_map/ppermute | solution.py:37
  35.0 3.0 %collective-permute-done.15.refs_4_ = bf16[6,32,256]{2,1,0:T(8,128)(2,1)S(1)} collective-permute-done((bf16[6,32,256]{2,1,0:T(8,128)(2,1)S(1)}, bf16[6,32,256]{2,1,0:T(8,128)(2,1)S(1)}, u32[]{:S(2)}, u32[]{:S(2)}) %collective-permute-start.15) | collective-permute-done | bytes 98336 | tf_op jit(solution)/shard_map/ppermute | solution.py:37
  38.0 1.3 %collective-permute-done.16.refs_3_ = bf16[6,32,256]{2,1,0:T(8,128)(2,1)S(1)} collective-permute-done((bf16[6,32,256]{2,1,0:T(8,128)(2,1)S(1)}, bf16[6,32,256]{2,1,0:T(8,128)(2,1)S(1)}, u32[]{:S(2)}, u32[]{:S(2)}) %collective-permute-start.16) | collective-permute-done | bytes 98336 | tf_op jit(solution)/shard_map/ppermute | solution.py:37
  40.5 1.1 %collective-permute-start.20 = (f32[1,32,256]{2,1,0:T(8,128)S(1)}, f32[1,32,256]{2,1,0:T(8,128)S(1)}, u32[]{:S(2)}, u32[]{:S(2)}) collective-permute-start(f32[1,32,256]{2,1,0:T(8,128)S(1)} %get-tuple-element.36), channel_id=1, source_target_pairs={{0,16},{8,24},{16,0},{24,8},{1,17},{9,25},{17,1},{25,9},{2,18},{10... | collective-permute-start | bytes 98312 | tf_op jit(solution)/shard_map/ppermute | solution.py:37
  41.6 0.8 %collective-permute-start.21 = (f32[1,32,256]{2,1,0:T(8,128)S(1)}, f32[1,32,256]{2,1,0:T(8,128)S(1)}, u32[]{:S(2)}, u32[]{:S(2)}) collective-permute-start(f32[1,32,256]{2,1,0:T(8,128)S(1)} %get-tuple-element.37), channel_id=1, source_target_pairs={{0,8},{8,0},{16,24},{24,16},{1,9},{9,1},{17,25},{25,17},{2,10},{10... | collective-permute-start | bytes 98312 | tf_op jit(solution)/shard_map/ppermute | solution.py:37
  42.4 1.9 %collective-permute-done.18 = f32[1,32,256]{2,1,0:T(8,128)S(1)} collective-permute-done((f32[1,32,256]{2,1,0:T(8,128)S(1)}, f32[1,32,256]{2,1,0:T(8,128)S(1)}, u32[]{:S(2)}, u32[]{:S(2)}) %collective-permute-start.18) | collective-permute-done | bytes 32800 | tf_op jit(solution)/shard_map/ppermute | solution.py:37
  44.8 0.6 %fusion = bf16[32,256]{1,0:T(8,128)(2,1)} fusion(bf16[32,256]{1,0:T(8,128)(2,1)S(1)} %get-tuple-element.20, f32[1,32,256]{2,1,0:T(8,128)S(1)} %collective-permute-done.21, f32[1,32,256]{2,1,0:T(8,128)S(1)} %collective-permute-done.20, f32[1,32,256]{2,1,0:T(8,128)S(1)} %get-tuple-element.34, f32[1,32,256]{2,1,0:T(8,128)S(1)} %collective-permute-done.19, ...), kind=kLoop, calls=%fused_computation.1 | loop fusion | flops 172032 | bytes 327680 | tf_op jit(solution)/shard_map/convert_element_type | solution.py:226
  (33 shorter events, 6.1 us)
Async XLA Ops:
  0.6 8.9 %collective-permute-start.3 = (bf16[1,32,256]{2,1,0:T(8,128)(2,1)}, bf16[1,32,256]{2,1,0:T(8,128)(2,1)S(1)}, u32[]{:S(2)}, u32[]{:S(2)}) collective-permute-start(bf16[1,32,256]{2,1,0:T(8,128)(2,1)} %bitcast.13), channel_id=1, source_target_pairs={{0,4},{1,5},{2,6},{3,7},{4,0},{5,1},{6,2},{7,3},{8,12},{9,13},{10,... | collective-permute-start | bytes 49160 | tf_op jit(solution)/shard_map/ppermute | solution.py:37
  4.7 4.8 %collective-permute-start.2 = (bf16[1,32,256]{2,1,0:T(8,128)(2,1)}, bf16[1,32,256]{2,1,0:T(8,128)(2,1)S(1)}, u32[]{:S(2)}, u32[]{:S(2)}) collective-permute-start(bf16[1,32,256]{2,1,0:T(8,128)(2,1)} %bitcast.14), channel_id=1, source_target_pairs={{0,24},{8,16},{16,8},{24,0},{1,25},{9,17},{17,9},{25,1},{2,26},{10... | collective-permute-start | bytes 49160 | tf_op jit(solution)/shard_map/ppermute | solution.py:37
  5.4 4.2 %collective-permute-start.1 = (bf16[1,32,256]{2,1,0:T(8,128)(2,1)}, bf16[1,32,256]{2,1,0:T(8,128)(2,1)S(1)}, u32[]{:S(2)}, u32[]{:S(2)}) collective-permute-start(bf16[1,32,256]{2,1,0:T(8,128)(2,1)} %bitcast.15), channel_id=1, source_target_pairs={{0,16},{8,24},{16,0},{24,8},{1,17},{9,25},{17,1},{25,9},{2,18},{10... | collective-permute-start | bytes 49160 | tf_op jit(solution)/shard_map/ppermute | solution.py:37
  6.3 3.3 %collective-permute-start = (bf16[1,32,256]{2,1,0:T(8,128)(2,1)}, bf16[1,32,256]{2,1,0:T(8,128)(2,1)S(1)}, u32[]{:S(2)}, u32[]{:S(2)}) collective-permute-start(bf16[1,32,256]{2,1,0:T(8,128)(2,1)} %bitcast.16), channel_id=1, source_target_pairs={{0,8},{8,0},{16,24},{24,16},{1,9},{9,1},{17,25},{25,17},{2,10},{10... | collective-permute-start | bytes 49160 | tf_op jit(solution)/shard_map/ppermute | solution.py:37
  10.4 6.6 %collective-permute-start.4 = (bf16[6,32,256]{2,1,0:T(8,128)(2,1)S(1)}, bf16[6,32,256]{2,1,0:T(8,128)(2,1)S(1)}, u32[]{:S(2)}, u32[]{:S(2)}) collective-permute-start(bf16[6,32,256]{2,1,0:T(8,128)(2,1)S(1)} %get-tuple-element.23), channel_id=1, source_target_pairs={{0,3},{1,2},{2,1},{3,0},{4,7},{5,6},{6,5},{7,4},{8,11},{9,10},{10,... | collective-permute-start | bytes 294920 | tf_op jit(solution)/shard_map/ppermute | solution.py:37
  13.0 5.4 %collective-permute-start.5 = (bf16[6,32,256]{2,1,0:T(8,128)(2,1)S(1)}, bf16[6,32,256]{2,1,0:T(8,128)(2,1)S(1)}, u32[]{:S(2)}, u32[]{:S(2)}) collective-permute-start(bf16[6,32,256]{2,1,0:T(8,128)(2,1)S(1)} %get-tuple-element.24), channel_id=1, source_target_pairs={{0,2},{1,3},{2,0},{3,1},{4,6},{5,7},{6,4},{7,5},{8,10},{9,11},{10,... | collective-permute-start | bytes 294920 | tf_op jit(solution)/shard_map/ppermute | solution.py:37
  13.5 5.0 %collective-permute-start.6 = (bf16[6,32,256]{2,1,0:T(8,128)(2,1)S(1)}, bf16[6,32,256]{2,1,0:T(8,128)(2,1)S(1)}, u32[]{:S(2)}, u32[]{:S(2)}) collective-permute-start(bf16[6,32,256]{2,1,0:T(8,128)(2,1)S(1)} %get-tuple-element.25), channel_id=1, source_target_pairs={{0,1},{1,0},{2,3},{3,2},{4,5},{5,4},{6,7},{7,6},{8,9},{9,8},{10,11... | collective-permute-start | bytes 294920 | tf_op jit(solution)/shard_map/ppermute | solution.py:37
  18.5 4.9 %collective-permute-start.7 = (f32[1,32,256]{2,1,0:T(8,128)S(1)}, f32[1,32,256]{2,1,0:T(8,128)S(1)}, u32[]{:S(2)}, u32[]{:S(2)}) collective-permute-start(f32[1,32,256]{2,1,0:T(8,128)S(1)} %add_add_fusion.1), channel_id=1, source_target_pairs={{0,4},{1,5},{2,6},{3,7},{4,0},{5,1},{6,2},{7,3},{8,12},{9,13},{10,... | collective-permute-start | bytes 98312 | tf_op jit(solution)/shard_map/ppermute | solution.py:37
  19.4 4.0 %collective-permute-start.8 = (f32[1,32,256]{2,1,0:T(8,128)S(1)}, f32[1,32,256]{2,1,0:T(8,128)S(1)}, u32[]{:S(2)}, u32[]{:S(2)}) collective-permute-start(f32[1,32,256]{2,1,0:T(8,128)S(1)} %get-tuple-element.27), channel_id=1, source_target_pairs={{0,24},{8,16},{16,8},{24,0},{1,25},{9,17},{17,9},{25,1},{2,26},{10... | collective-permute-start | bytes 98312 | tf_op jit(solution)/shard_map/ppermute | solution.py:37
  19.5 4.0 %collective-permute-start.9 = (f32[1,32,256]{2,1,0:T(8,128)S(1)}, f32[1,32,256]{2,1,0:T(8,128)S(1)}, u32[]{:S(2)}, u32[]{:S(2)}) collective-permute-start(f32[1,32,256]{2,1,0:T(8,128)S(1)} %get-tuple-element.28), channel_id=1, source_target_pairs={{0,16},{8,24},{16,0},{24,8},{1,17},{9,25},{17,1},{25,9},{2,18},{10... | collective-permute-start | bytes 98312 | tf_op jit(solution)/shard_map/ppermute | solution.py:37
  20.9 2.5 %collective-permute-start.10 = (f32[1,32,256]{2,1,0:T(8,128)S(1)}, f32[1,32,256]{2,1,0:T(8,128)S(1)}, u32[]{:S(2)}, u32[]{:S(2)}) collective-permute-start(f32[1,32,256]{2,1,0:T(8,128)S(1)} %get-tuple-element.29), channel_id=1, source_target_pairs={{0,8},{8,0},{16,24},{24,16},{1,9},{9,1},{17,25},{25,17},{2,10},{10... | collective-permute-start | bytes 98312 | tf_op jit(solution)/shard_map/ppermute | solution.py:37
  23.5 17.0 %copy-start = (bf16[1,32,256]{2,1,0:T(8,128)(2,1)}, bf16[1,32,256]{2,1,0:T(8,128)(2,1)S(1)}, u32[]{:S(2)}) copy-start(bf16[1,32,256]{2,1,0:T(8,128)(2,1)S(1)} %add_convert_fusion.refs_0_.refs_4_) | copy-start | bytes 49156
  23.5 4.7 %collective-permute-start.14 = (bf16[1,32,256]{2,1,0:T(8,128)(2,1)S(1)}, bf16[1,32,256]{2,1,0:T(8,128)(2,1)S(1)}, u32[]{:S(2)}, u32[]{:S(2)}) collective-permute-start(bf16[1,32,256]{2,1,0:T(8,128)(2,1)S(1)} %add_convert_fusion.refs_0_.refs_4_), channel_id=1, source_target_pairs={{0,4},{1,5},{2,6},{3,7},{4,0},{5,1},{6,2},{7,3},{8,12},{9,13},{10,... | collective-permute-start | bytes 49160 | tf_op jit(solution)/shard_map/ppermute | solution.py:37
  26.2 3.2 %collective-permute-start.13 = (bf16[1,32,256]{2,1,0:T(8,128)(2,1)S(1)}, bf16[1,32,256]{2,1,0:T(8,128)(2,1)S(1)}, u32[]{:S(2)}, u32[]{:S(2)}) collective-permute-start(bf16[1,32,256]{2,1,0:T(8,128)(2,1)S(1)} %add_convert_fusion.refs_0_.refs_4_), channel_id=1, source_target_pairs={{0,24},{8,16},{16,8},{24,0},{1,25},{9,17},{17,9},{25,1},{2,26},{10... | collective-permute-start | bytes 49160 | tf_op jit(solution)/shard_map/ppermute | solution.py:37
  26.8 3.9 %collective-permute-start.12 = (bf16[1,32,256]{2,1,0:T(8,128)(2,1)S(1)}, bf16[1,32,256]{2,1,0:T(8,128)(2,1)S(1)}, u32[]{:S(2)}, u32[]{:S(2)}) collective-permute-start(bf16[1,32,256]{2,1,0:T(8,128)(2,1)S(1)} %add_convert_fusion.refs_0_.refs_4_), channel_id=1, source_target_pairs={{0,16},{8,24},{16,0},{24,8},{1,17},{9,25},{17,1},{25,9},{2,18},{10... | collective-permute-start | bytes 49160 | tf_op jit(solution)/shard_map/ppermute | solution.py:37
  27.8 2.9 %collective-permute-start.11 = (bf16[1,32,256]{2,1,0:T(8,128)(2,1)S(1)}, bf16[1,32,256]{2,1,0:T(8,128)(2,1)S(1)}, u32[]{:S(2)}, u32[]{:S(2)}) collective-permute-start(bf16[1,32,256]{2,1,0:T(8,128)(2,1)S(1)} %add_convert_fusion.refs_0_.refs_4_), channel_id=1, source_target_pairs={{0,8},{8,0},{16,24},{24,16},{1,9},{9,1},{17,25},{25,17},{2,10},{10... | collective-permute-start | bytes 49160 | tf_op jit(solution)/shard_map/ppermute | solution.py:37
  31.5 6.5 %collective-permute-start.15 = (bf16[6,32,256]{2,1,0:T(8,128)(2,1)S(1)}, bf16[6,32,256]{2,1,0:T(8,128)(2,1)S(1)}, u32[]{:S(2)}, u32[]{:S(2)}) collective-permute-start(bf16[6,32,256]{2,1,0:T(8,128)(2,1)S(1)} %get-tuple-element.31), channel_id=1, source_target_pairs={{0,3},{1,2},{2,1},{3,0},{4,7},{5,6},{6,5},{7,4},{8,11},{9,10},{10,... | collective-permute-start | bytes 294920 | tf_op jit(solution)/shard_map/ppermute | solution.py:37
  34.0 5.3 %collective-permute-start.16 = (bf16[6,32,256]{2,1,0:T(8,128)(2,1)S(1)}, bf16[6,32,256]{2,1,0:T(8,128)(2,1)S(1)}, u32[]{:S(2)}, u32[]{:S(2)}) collective-permute-start(bf16[6,32,256]{2,1,0:T(8,128)(2,1)S(1)} %get-tuple-element.32), channel_id=1, source_target_pairs={{0,2},{1,3},{2,0},{3,1},{4,6},{5,7},{6,4},{7,5},{8,10},{9,11},{10,... | collective-permute-start | bytes 294920 | tf_op jit(solution)/shard_map/ppermute | solution.py:37
  34.4 4.9 %collective-permute-start.17 = (bf16[6,32,256]{2,1,0:T(8,128)(2,1)S(1)}, bf16[6,32,256]{2,1,0:T(8,128)(2,1)S(1)}, u32[]{:S(2)}, u32[]{:S(2)}) collective-permute-start(bf16[6,32,256]{2,1,0:T(8,128)(2,1)S(1)} %get-tuple-element.33), channel_id=1, source_target_pairs={{0,1},{1,0},{2,3},{3,2},{4,5},{5,4},{6,7},{7,6},{8,9},{9,8},{10,11... | collective-permute-start | bytes 294920 | tf_op jit(solution)/shard_map/ppermute | solution.py:37
  39.4 4.9 %collective-permute-start.18 = (f32[1,32,256]{2,1,0:T(8,128)S(1)}, f32[1,32,256]{2,1,0:T(8,128)S(1)}, u32[]{:S(2)}, u32[]{:S(2)}) collective-permute-start(f32[1,32,256]{2,1,0:T(8,128)S(1)} %add_add_fusion), channel_id=1, source_target_pairs={{0,4},{1,5},{2,6},{3,7},{4,0},{5,1},{6,2},{7,3},{8,12},{9,13},{10,... | collective-permute-start | bytes 98312 | tf_op jit(solution)/shard_map/ppermute | solution.py:37
  40.5 3.8 %collective-permute-start.19 = (f32[1,32,256]{2,1,0:T(8,128)S(1)}, f32[1,32,256]{2,1,0:T(8,128)S(1)}, u32[]{:S(2)}, u32[]{:S(2)}) collective-permute-start(f32[1,32,256]{2,1,0:T(8,128)S(1)} %get-tuple-element.35), channel_id=1, source_target_pairs={{0,24},{8,16},{16,8},{24,0},{1,25},{9,17},{17,9},{25,1},{2,26},{10... | collective-permute-start | bytes 98312 | tf_op jit(solution)/shard_map/ppermute | solution.py:37
  40.5 4.3 %collective-permute-start.20 = (f32[1,32,256]{2,1,0:T(8,128)S(1)}, f32[1,32,256]{2,1,0:T(8,128)S(1)}, u32[]{:S(2)}, u32[]{:S(2)}) collective-permute-start(f32[1,32,256]{2,1,0:T(8,128)S(1)} %get-tuple-element.36), channel_id=1, source_target_pairs={{0,16},{8,24},{16,0},{24,8},{1,17},{9,25},{17,1},{25,9},{2,18},{10... | collective-permute-start | bytes 98312 | tf_op jit(solution)/shard_map/ppermute | solution.py:37
  41.6 3.2 %collective-permute-start.21 = (f32[1,32,256]{2,1,0:T(8,128)S(1)}, f32[1,32,256]{2,1,0:T(8,128)S(1)}, u32[]{:S(2)}, u32[]{:S(2)}) collective-permute-start(f32[1,32,256]{2,1,0:T(8,128)S(1)} %get-tuple-element.37), channel_id=1, source_target_pairs={{0,8},{8,0},{16,24},{24,16},{1,9},{9,1},{17,25},{25,17},{2,10},{10... | collective-permute-start | bytes 98312 | tf_op jit(solution)/shard_map/ppermute | solution.py:37

commit v5 on v4

--- a/solution.py
+++ b/solution.py
@@ -83,30 +83,65 @@
     return pieces[0][0]
 
 
-def fetch_kernel(tiles_hbm, vec_hbm, tiles_ref, vec_ref, sems):
-    pairs = ((tiles_hbm, tiles_ref), (vec_hbm, vec_ref))
+def fetch_kernel(tiles_hbm, vec_hbm, rows_hbm, cols_hbm, live_ref, tiles_ref, vec_ref, codes_ref, rows_ref, cols_ref, sems):
+    pairs = ((tiles_hbm, tiles_ref), (vec_hbm, vec_ref), (rows_hbm, rows_ref), (cols_hbm, cols_ref))
     copies = [pltpu.make_async_copy(a, b, sems.at[i]) for i, (a, b) in enumerate(pairs)]
     for copy in copies:
         copy.start()
-    for copy in copies:
+    for copy in copies[2:]:
         copy.wait()
-
-
-def fetch(*arrays):
+    slots = rows_ref.shape[0]
+    slot = lax.broadcasted_iota(jnp.int32, (slots, slots), 0)
+    lane = lax.broadcasted_iota(jnp.int32, (slots, slots), 1)
+    code = rows_ref[...] + cols_ref[...] * 4096
+    code = jnp.sum(jnp.where(slot == lane, code[None, :], 0), 1, keepdims=True)
+    used = lax.broadcasted_iota(jnp.int32, (slots, 128), 0) < live_ref[0]
+    codes_ref[...] = code + jnp.where(used, 4096**2, 0)
+    for copy in copies[:2]:
+        copy.wait()
+
+
+def fetch(tiles, vectors, tile_rows, tile_cols, tile_live):
+    slots = tile_rows.shape[0]
+    pinned = [pltpu.with_memory_space_constraint(a, pltpu.HBM) for a in (tiles, vectors, tile_rows, tile_cols)]
     return pl.pallas_call(
         fetch_kernel,
-        out_shape=[jax.ShapeDtypeStruct(a.shape, a.dtype) for a in arrays],
-        in_specs=[HBM] * 2,
-        out_specs=[VMEM] * 2,
-        scratch_shapes=[pltpu.SemaphoreType.DMA((2,))],
+        out_shape=[
+            jax.ShapeDtypeStruct(tiles.shape, tiles.dtype),
+            jax.ShapeDtypeStruct(vectors.shape, vectors.dtype),
+            jax.ShapeDtypeStruct((slots, 128), jnp.int32),
+        ],
+        in_specs=[HBM] * 4 + [pl.BlockSpec(memory_space=pltpu.SMEM)],
+        out_specs=[VMEM] * 3,
+        scratch_shapes=[
+            pltpu.VMEM((slots,), jnp.int32),
+            pltpu.VMEM((slots,), jnp.int32),
+            pltpu.SemaphoreType.DMA((4,)),
+        ],
         compiler_params=PARAMS,
         cost_estimate=pl.CostEstimate(flops=0, bytes_accessed=8 * 2**20, transcendentals=0),
         name="fetch",
-    )(*[pltpu.with_memory_space_constraint(a, pltpu.HBM) for a in arrays])
-
-
-def products(code_ref, tiles_ref, vec, acc, direct):
-    dims = (((1,), (1,)), ((), ())) if direct else (((1,), (0,)), ((), ()))
+    )(*pinned, tile_live)
+
+
+def turn_kernel(tiles_ref, out_ref):
+    for t in range(tiles_ref.shape[0]):
+        out_ref[t] = tiles_ref[t].T
+
+
+def turn(tiles):
+    return pl.pallas_call(
+        turn_kernel,
+        out_shape=jax.ShapeDtypeStruct(tiles.shape, tiles.dtype),
+        in_specs=[VMEM],
+        out_specs=VMEM,
+        compiler_params=PARAMS,
+        name="turn",
+    )(tiles)
+
+
+def products(code_ref, tiles_ref, vec, acc, direct, turned=False):
+    dims = (((1,), (1,)), ((), ())) if direct and not turned else (((1,), (0,)), ((), ()))
     acc[...] = jnp.zeros_like(acc)
     for t in range(tiles_ref.shape[0]):
         code = code_ref[t, 0]
@@ -116,7 +151,7 @@
         acc[put] += jnp.where(used > 0, y, 0.0)
 
 
-def direct_half(codes, colset, own, tiles, rows, cols):
+def direct_half(codes, colset, own, tiles, rows, cols, turned=False):
     width, size = own[0].shape[1:]
     radix = cols[0][1]
     held = sum(piece.shape[0] for piece in own)
@@ -130,7 +165,7 @@
         for piece in ins[:n_row]:
             for i in range(piece.shape[0]):
                 vec[slot_index(me_r, rows, next(where))] = piece[i]
-        products(code_ref, tiles_ref, vec, acc, True)
+        products(code_ref, tiles_ref, vec, acc, True, turned)
         slots = slots_of(cols)
         for i in range(held):
             keep_ref[i] = acc[slot_index(me_c, cols, slots[i])]
@@ -201,14 +236,14 @@
 def local(n_rows, n_cols, vectors, tiles, tile_rows, tile_cols, tile_live):
     rows, cols = digits_of(n_rows, 99), digits_of(n_cols, 1)
     inner, outer = cols[0], cols[1:]
-    used = (jnp.arange(tile_rows.shape[0], dtype=jnp.int32) < tile_live[0]).astype(jnp.int32)
-    codes = jnp.broadcast_to((tile_rows + tile_cols * 4096 + used * 4096**2)[:, None], (tile_rows.shape[0], 128))
-    tiles, kept = fetch(tiles, vectors)
-
-    def apply(vec, kept):
+    tiles, kept, codes = fetch(tiles, vectors, tile_rows, tile_cols, tile_live)
+
+    turned = turn(tiles)
+
+    def apply(vec, kept, again):
         colset = gather(vec, kept, "row", n_rows, rows)
         own = gather(vec, kept, "col", n_cols, outer)
-        keep, *packed = direct_half(codes, colset, own, tiles, rows, cols)
+        keep, *packed = direct_half(codes, colset, own, turned if again else tiles, rows, cols, again)
         got = [send(value, "col", n_cols, *inner, step) for step, value in enumerate(packed, 1)]
         held, at, pieces = keep.shape[0], 0, []
         for size in sizes_of(outer):
@@ -221,8 +256,8 @@
         mirror = mirror_half(codes, own, got, tiles, rows, cols)
         return scatter(pieces, "col", n_cols, outer) + scatter(list(mirror), "row", n_rows, rows)
 
-    first = apply(vectors, kept).astype(jnp.bfloat16)
-    second = 2.0 * apply(first, first) - kept.astype(jnp.float32)
+    first = apply(vectors, kept, False).astype(jnp.bfloat16)
+    second = 2.0 * apply(first, first, True) - kept.astype(jnp.float32)
     return first, second.astype(jnp.bfloat16)
 
 

time: 45.6 us -> 44.8 us (0.982)
  other arithmetic: 1.39 us -> 0.7 us
    add x1 -> x0, other arithmetic: 0.68 us -> none  [local(): tile_rows + tile_cols * 4096 + used * 4096 ** 2]
    pallas_call x1 -> x2, Pallas kernels: 1.61 us -> 2.22 us  [the longest x1 1.63 us: fetch(): pl.pallas_call(fetch_kernel, out_shape=[jax.ShapeDtypeStruct(tiles.shape,...]
  transfers between devices with their start and end apart: 22 -> 22, of which waited for: 12 -> 13; matrix products, arithmetic and copies ran while one was open for 1% -> 0% of each run, Pallas kernels for 6% -> 7%
where the time goes in v5:
time: 44.8 us; the launch traced here: 44.7 us
  starting transfers between devices  22.4 us (50%)
  waiting for transfers between devices  15.6 us (35%)
  Pallas kernels  4.54 us (10%)
  between operations  1.41 us (3%)
  other arithmetic  0.7 us (2%)
    ppermute x22, starting transfers between devices, send(): return lax.ppermute(value, axis, pairs)  22.4 us
    ppermute x22, waiting for transfers between devices, send(): return lax.ppermute(value, axis, pairs)  15.6 us
    pallas_call x1, Pallas kernels, fetch(): pl.pallas_call(fetch_kernel, out_shape=[jax.ShapeDtypeStruct(tiles.shape,...  1.63 us
    pallas_call x2, Pallas kernels, direct_half(): pl.pallas_call(body, out_shape=[jax.ShapeDtypeStruct((held, width, size),...  1.32 us
    pallas_call x2, Pallas kernels, mirror_half(): pl.pallas_call(body, out_shape=[jax.ShapeDtypeStruct((n, width, size), jn...  1.01 us
  transfers between devices with their start and end apart: 22, of which 13 were waited for; matrix products, arithmetic and copies ran while one was open for 0% of the time, Pallas kernels for 7%

profile of v5, /device:TPU:0, one launch (start us, length us, event | category | flops | bytes accessed | tf_op | source)
XLA Modules:
  0.0 44.7 jit_solution(3695460267020723846)
XLA Ops:
  0.6 4.1 %collective-permute-start.3 = (bf16[1,32,256]{2,1,0:T(8,128)(2,1)}, bf16[1,32,256]{2,1,0:T(8,128)(2,1)S(1)}, u32[]{:S(2)}, u32[]{:S(2)}) collective-permute-start(bf16[1,32,256]{2,1,0:T(8,128)(2,1)} %bitcast.11), channel_id=1, source_target_pairs={{0,4},{1,5},{2,6},{3,7},{4,0},{5,1},{6,2},{7,3},{8,12},{9,13},{10,... | collective-permute-start | bytes 49160 | tf_op jit(solution)/shard_map/ppermute | solution.py:37
  4.7 0.7 %collective-permute-start.2 = (bf16[1,32,256]{2,1,0:T(8,128)(2,1)}, bf16[1,32,256]{2,1,0:T(8,128)(2,1)S(1)}, u32[]{:S(2)}, u32[]{:S(2)}) collective-permute-start(bf16[1,32,256]{2,1,0:T(8,128)(2,1)} %bitcast.12), channel_id=1, source_target_pairs={{0,24},{8,16},{16,8},{24,0},{1,25},{9,17},{17,9},{25,1},{2,26},{10... | collective-permute-start | bytes 49160 | tf_op jit(solution)/shard_map/ppermute | solution.py:37
  5.4 0.9 %collective-permute-start.1 = (bf16[1,32,256]{2,1,0:T(8,128)(2,1)}, bf16[1,32,256]{2,1,0:T(8,128)(2,1)S(1)}, u32[]{:S(2)}, u32[]{:S(2)}) collective-permute-start(bf16[1,32,256]{2,1,0:T(8,128)(2,1)} %bitcast.13), channel_id=1, source_target_pairs={{0,16},{8,24},{16,0},{24,8},{1,17},{9,25},{17,1},{25,9},{2,18},{10... | collective-permute-start | bytes 49160 | tf_op jit(solution)/shard_map/ppermute | solution.py:37
  7.2 1.6 %fetch.1 = (bf16[16,256,256]{2,1,0:T(8,128)(2,1)S(1)}, bf16[32,256]{1,0:T(8,128)(2,1)S(1)}, s32[16,128]{1,0:T(8,128)S(1)}) custom-call(bf16[16,256,256]{2,1,0:T(8,128)(2,1)} %tiles_hbm.1, bf16[32,256]{1,0:T(8,128)(2,1)} %vec_hbm.1, s32[16]{0:T(128)} %rows_hbm.1, s32[16]{0:T(128)} %cols_hbm.1, s32[1]{0:T(128)S(6)} %copy.7.live_ref), custom_call_target="tpu_custom_call" | custom-call | bytes 8388608 | tf_op jit(solution)/shard_map/fetch/pallas_call | solution.py:107
  8.9 0.6 %collective-permute-done.1.refs_2_ = bf16[1,32,256]{2,1,0:T(8,128)(2,1)S(1)} collective-permute-done((bf16[1,32,256]{2,1,0:T(8,128)(2,1)}, bf16[1,32,256]{2,1,0:T(8,128)(2,1)S(1)}, u32[]{:S(2)}, u32[]{:S(2)}) %collective-permute-start.1) | collective-permute-done | bytes 16416 | tf_op jit(solution)/shard_map/ppermute | solution.py:37
  9.5 0.8 %direct.2 = (f32[2,32,256]{2,1,0:T(8,128)S(1)}, bf16[6,32,256]{2,1,0:T(8,128)(2,1)S(1)}, bf16[6,32,256]{2,1,0:T(8,128)(2,1)S(1)}, bf16[6,32,256]{2,1,0:T(8,128)(2,1)S(1)}) custom-call(s32[16,128]{1,0:T(8,128)S(1)} %get-tuple-element.21.code_ref, bf16[1,32,256]{2,1,0:T(8,128)(2,1)S(1)} %bitcast.7, bf16[1,32,256]{2,1,0:T(8,128)(2,1)S(1)} %collective-permute-done.refs_1_, ...), custom_call_target="tpu_custom_call" | custom-call | tf_op jit(solution)/shard_map/direct/pallas_call | solution.py:184
  10.3 2.6 %collective-permute-start.4 = (bf16[6,32,256]{2,1,0:T(8,128)(2,1)S(1)}, bf16[6,32,256]{2,1,0:T(8,128)(2,1)S(1)}, u32[]{:S(2)}, u32[]{:S(2)}) collective-permute-start(bf16[6,32,256]{2,1,0:T(8,128)(2,1)S(1)} %get-tuple-element.25), channel_id=1, source_target_pairs={{0,3},{1,2},{2,1},{3,0},{4,7},{5,6},{6,5},{7,4},{8,11},{9,10},{10,... | collective-permute-start | bytes 294920 | tf_op jit(solution)/shard_map/ppermute | solution.py:37
  13.8 3.0 %collective-permute-done.4.refs_4_ = bf16[6,32,256]{2,1,0:T(8,128)(2,1)S(1)} collective-permute-done((bf16[6,32,256]{2,1,0:T(8,128)(2,1)S(1)}, bf16[6,32,256]{2,1,0:T(8,128)(2,1)S(1)}, u32[]{:S(2)}, u32[]{:S(2)}) %collective-permute-start.4) | collective-permute-done | bytes 98336 | tf_op jit(solution)/shard_map/ppermute | solution.py:37
  16.8 1.4 %collective-permute-done.5.refs_3_ = bf16[6,32,256]{2,1,0:T(8,128)(2,1)S(1)} collective-permute-done((bf16[6,32,256]{2,1,0:T(8,128)(2,1)S(1)}, bf16[6,32,256]{2,1,0:T(8,128)(2,1)S(1)}, u32[]{:S(2)}, u32[]{:S(2)}) %collective-permute-start.5) | collective-permute-done | bytes 98336 | tf_op jit(solution)/shard_map/ppermute | solution.py:37
  19.3 1.1 %collective-permute-start.9 = (f32[1,32,256]{2,1,0:T(8,128)S(1)}, f32[1,32,256]{2,1,0:T(8,128)S(1)}, u32[]{:S(2)}, u32[]{:S(2)}) collective-permute-start(f32[1,32,256]{2,1,0:T(8,128)S(1)} %get-tuple-element.30), channel_id=1, source_target_pairs={{0,16},{8,24},{16,0},{24,8},{1,17},{9,25},{17,1},{25,9},{2,18},{10... | collective-permute-start | bytes 98312 | tf_op jit(solution)/shard_map/ppermute | solution.py:37
  20.4 0.7 %collective-permute-start.10 = (f32[1,32,256]{2,1,0:T(8,128)S(1)}, f32[1,32,256]{2,1,0:T(8,128)S(1)}, u32[]{:S(2)}, u32[]{:S(2)}) collective-permute-start(f32[1,32,256]{2,1,0:T(8,128)S(1)} %get-tuple-element.31), channel_id=1, source_target_pairs={{0,8},{8,0},{16,24},{24,16},{1,9},{9,1},{17,25},{25,17},{2,10},{10... | collective-permute-start | bytes 98312 | tf_op jit(solution)/shard_map/ppermute | solution.py:37
  21.2 2.0 %collective-permute-done.7 = f32[1,32,256]{2,1,0:T(8,128)S(1)} collective-permute-done((f32[1,32,256]{2,1,0:T(8,128)S(1)}, f32[1,32,256]{2,1,0:T(8,128)S(1)}, u32[]{:S(2)}, u32[]{:S(2)}) %collective-permute-start.7) | collective-permute-done | bytes 32800 | tf_op jit(solution)/shard_map/ppermute | solution.py:37
  23.6 2.6 %collective-permute-start.14 = (bf16[1,32,256]{2,1,0:T(8,128)(2,1)S(1)}, bf16[1,32,256]{2,1,0:T(8,128)(2,1)S(1)}, u32[]{:S(2)}, u32[]{:S(2)}) collective-permute-start(bf16[1,32,256]{2,1,0:T(8,128)(2,1)S(1)} %add_convert_fusion.refs_0_.refs_4_), channel_id=1, source_target_pairs={{0,4},{1,5},{2,6},{3,7},{4,0},{5,1},{6,2},{7,3},{8,12},{9,13},{10,... | collective-permute-start | bytes 49160 | tf_op jit(solution)/shard_map/ppermute | solution.py:37
  26.3 1.3 %collective-permute-start.12 = (bf16[1,32,256]{2,1,0:T(8,128)(2,1)S(1)}, bf16[1,32,256]{2,1,0:T(8,128)(2,1)S(1)}, u32[]{:S(2)}, u32[]{:S(2)}) collective-permute-start(bf16[1,32,256]{2,1,0:T(8,128)(2,1)S(1)} %add_convert_fusion.refs_0_.refs_4_), channel_id=1, source_target_pairs={{0,16},{8,24},{16,0},{24,8},{1,17},{9,25},{17,1},{25,9},{2,18},{10... | collective-permute-start | bytes 49160 | tf_op jit(solution)/shard_map/ppermute | solution.py:37
  28.1 0.6 %turn.1.refs_6_ = bf16[16,256,256]{2,1,0:T(8,128)(2,1)S(1)} custom-call(bf16[16,256,256]{2,1,0:T(8,128)(2,1)S(1)} %get-tuple-element.23.refs_6_.refs_5_.tiles_ref), custom_call_target="tpu_custom_call" | custom-call | tf_op jit(solution)/shard_map/turn/pallas_call | solution.py:133
  28.7 0.8 %collective-permute-done.13.refs_3_ = bf16[1,32,256]{2,1,0:T(8,128)(2,1)S(1)} collective-permute-done((bf16[1,32,256]{2,1,0:T(8,128)(2,1)S(1)}, bf16[1,32,256]{2,1,0:T(8,128)(2,1)S(1)}, u32[]{:S(2)}, u32[]{:S(2)}) %collective-permute-start.13) | collective-permute-done | bytes 16416 | tf_op jit(solution)/shard_map/ppermute | solution.py:37
  29.5 0.6 %collective-permute-done.12.refs_2_ = bf16[1,32,256]{2,1,0:T(8,128)(2,1)S(1)} collective-permute-done((bf16[1,32,256]{2,1,0:T(8,128)(2,1)S(1)}, bf16[1,32,256]{2,1,0:T(8,128)(2,1)S(1)}, u32[]{:S(2)}, u32[]{:S(2)}) %collective-permute-start.12) | collective-permute-done | bytes 16416 | tf_op jit(solution)/shard_map/ppermute | solution.py:37
  30.6 2.9 %collective-permute-start.15 = (bf16[6,32,256]{2,1,0:T(8,128)(2,1)S(1)}, bf16[6,32,256]{2,1,0:T(8,128)(2,1)S(1)}, u32[]{:S(2)}, u32[]{:S(2)}) collective-permute-start(bf16[6,32,256]{2,1,0:T(8,128)(2,1)S(1)} %get-tuple-element.33), channel_id=1, source_target_pairs={{0,3},{1,2},{2,1},{3,0},{4,7},{5,6},{6,5},{7,4},{8,11},{9,10},{10,... | collective-permute-start | bytes 294920 | tf_op jit(solution)/shard_map/ppermute | solution.py:37
  34.2 3.1 %collective-permute-done.15.refs_4_ = bf16[6,32,256]{2,1,0:T(8,128)(2,1)S(1)} collective-permute-done((bf16[6,32,256]{2,1,0:T(8,128)(2,1)S(1)}, bf16[6,32,256]{2,1,0:T(8,128)(2,1)S(1)}, u32[]{:S(2)}, u32[]{:S(2)}) %collective-permute-start.15) | collective-permute-done | bytes 98336 | tf_op jit(solution)/shard_map/ppermute | solution.py:37
  37.3 1.2 %collective-permute-done.16.refs_3_ = bf16[6,32,256]{2,1,0:T(8,128)(2,1)S(1)} collective-permute-done((bf16[6,32,256]{2,1,0:T(8,128)(2,1)S(1)}, bf16[6,32,256]{2,1,0:T(8,128)(2,1)S(1)}, u32[]{:S(2)}, u32[]{:S(2)}) %collective-permute-start.16) | collective-permute-done | bytes 98336 | tf_op jit(solution)/shard_map/ppermute | solution.py:37
  39.8 1.1 %collective-permute-start.20 = (f32[1,32,256]{2,1,0:T(8,128)S(1)}, f32[1,32,256]{2,1,0:T(8,128)S(1)}, u32[]{:S(2)}, u32[]{:S(2)}) collective-permute-start(f32[1,32,256]{2,1,0:T(8,128)S(1)} %get-tuple-element.38), channel_id=1, source_target_pairs={{0,16},{8,24},{16,0},{24,8},{1,17},{9,25},{17,1},{25,9},{2,18},{10... | collective-permute-start | bytes 98312 | tf_op jit(solution)/shard_map/ppermute | solution.py:37
  40.8 0.8 %collective-permute-start.21 = (f32[1,32,256]{2,1,0:T(8,128)S(1)}, f32[1,32,256]{2,1,0:T(8,128)S(1)}, u32[]{:S(2)}, u32[]{:S(2)}) collective-permute-start(f32[1,32,256]{2,1,0:T(8,128)S(1)} %get-tuple-element.39), channel_id=1, source_target_pairs={{0,8},{8,0},{16,24},{24,16},{1,9},{9,1},{17,25},{25,17},{2,10},{10... | collective-permute-start | bytes 98312 | tf_op jit(solution)/shard_map/ppermute | solution.py:37
  41.6 1.9 %collective-permute-done.18 = f32[1,32,256]{2,1,0:T(8,128)S(1)} collective-permute-done((f32[1,32,256]{2,1,0:T(8,128)S(1)}, f32[1,32,256]{2,1,0:T(8,128)S(1)}, u32[]{:S(2)}, u32[]{:S(2)}) %collective-permute-start.18) | collective-permute-done | bytes 32800 | tf_op jit(solution)/shard_map/ppermute | solution.py:37
  44.0 0.6 %fusion = bf16[32,256]{1,0:T(8,128)(2,1)} fusion(bf16[32,256]{1,0:T(8,128)(2,1)S(1)} %get-tuple-element.22, f32[1,32,256]{2,1,0:T(8,128)S(1)} %collective-permute-done.21, f32[1,32,256]{2,1,0:T(8,128)S(1)} %collective-permute-done.20, f32[1,32,256]{2,1,0:T(8,128)S(1)} %get-tuple-element.36, f32[1,32,256]{2,1,0:T(8,128)S(1)} %collective-permute-done.19, ...), kind=kLoop, calls=%fused_computation.1 | loop fusion | flops 172032 | bytes 327680 | tf_op jit(solution)/shard_map/convert_element_type | solution.py:261
  (32 shorter events, 6.4 us)
Async XLA Ops:
  0.6 8.3 %collective-permute-start.3 = (bf16[1,32,256]{2,1,0:T(8,128)(2,1)}, bf16[1,32,256]{2,1,0:T(8,128)(2,1)S(1)}, u32[]{:S(2)}, u32[]{:S(2)}) collective-permute-start(bf16[1,32,256]{2,1,0:T(8,128)(2,1)} %bitcast.11), channel_id=1, source_target_pairs={{0,4},{1,5},{2,6},{3,7},{4,0},{5,1},{6,2},{7,3},{8,12},{9,13},{10,... | collective-permute-start | bytes 49160 | tf_op jit(solution)/shard_map/ppermute | solution.py:37
  4.7 4.2 %collective-permute-start.2 = (bf16[1,32,256]{2,1,0:T(8,128)(2,1)}, bf16[1,32,256]{2,1,0:T(8,128)(2,1)S(1)}, u32[]{:S(2)}, u32[]{:S(2)}) collective-permute-start(bf16[1,32,256]{2,1,0:T(8,128)(2,1)} %bitcast.12), channel_id=1, source_target_pairs={{0,24},{8,16},{16,8},{24,0},{1,25},{9,17},{17,9},{25,1},{2,26},{10... | collective-permute-start | bytes 49160 | tf_op jit(solution)/shard_map/ppermute | solution.py:37
  5.4 4.1 %collective-permute-start.1 = (bf16[1,32,256]{2,1,0:T(8,128)(2,1)}, bf16[1,32,256]{2,1,0:T(8,128)(2,1)S(1)}, u32[]{:S(2)}, u32[]{:S(2)}) collective-permute-start(bf16[1,32,256]{2,1,0:T(8,128)(2,1)} %bitcast.13), channel_id=1, source_target_pairs={{0,16},{8,24},{16,0},{24,8},{1,17},{9,25},{17,1},{25,9},{2,18},{10... | collective-permute-start | bytes 49160 | tf_op jit(solution)/shard_map/ppermute | solution.py:37
  6.3 3.2 %collective-permute-start = (bf16[1,32,256]{2,1,0:T(8,128)(2,1)}, bf16[1,32,256]{2,1,0:T(8,128)(2,1)S(1)}, u32[]{:S(2)}, u32[]{:S(2)}) collective-permute-start(bf16[1,32,256]{2,1,0:T(8,128)(2,1)} %bitcast.14), channel_id=1, source_target_pairs={{0,8},{8,0},{16,24},{24,16},{1,9},{9,1},{17,25},{25,17},{2,10},{10... | collective-permute-start | bytes 49160 | tf_op jit(solution)/shard_map/ppermute | solution.py:37
  10.3 6.6 %collective-permute-start.4 = (bf16[6,32,256]{2,1,0:T(8,128)(2,1)S(1)}, bf16[6,32,256]{2,1,0:T(8,128)(2,1)S(1)}, u32[]{:S(2)}, u32[]{:S(2)}) collective-permute-start(bf16[6,32,256]{2,1,0:T(8,128)(2,1)S(1)} %get-tuple-element.25), channel_id=1, source_target_pairs={{0,3},{1,2},{2,1},{3,0},{4,7},{5,6},{6,5},{7,4},{8,11},{9,10},{10,... | collective-permute-start | bytes 294920 | tf_op jit(solution)/shard_map/ppermute | solution.py:37
  12.9 5.3 %collective-permute-start.5 = (bf16[6,32,256]{2,1,0:T(8,128)(2,1)S(1)}, bf16[6,32,256]{2,1,0:T(8,128)(2,1)S(1)}, u32[]{:S(2)}, u32[]{:S(2)}) collective-permute-start(bf16[6,32,256]{2,1,0:T(8,128)(2,1)S(1)} %get-tuple-element.26), channel_id=1, source_target_pairs={{0,2},{1,3},{2,0},{3,1},{4,6},{5,7},{6,4},{7,5},{8,10},{9,11},{10,... | collective-permute-start | bytes 294920 | tf_op jit(solution)/shard_map/ppermute | solution.py:37
  13.3 4.9 %collective-permute-start.6 = (bf16[6,32,256]{2,1,0:T(8,128)(2,1)S(1)}, bf16[6,32,256]{2,1,0:T(8,128)(2,1)S(1)}, u32[]{:S(2)}, u32[]{:S(2)}) collective-permute-start(bf16[6,32,256]{2,1,0:T(8,128)(2,1)S(1)} %get-tuple-element.27), channel_id=1, source_target_pairs={{0,1},{1,0},{2,3},{3,2},{4,5},{5,4},{6,7},{7,6},{8,9},{9,8},{10,11... | collective-permute-start | bytes 294920 | tf_op jit(solution)/shard_map/ppermute | solution.py:37
  18.3 4.9 %collective-permute-start.7 = (f32[1,32,256]{2,1,0:T(8,128)S(1)}, f32[1,32,256]{2,1,0:T(8,128)S(1)}, u32[]{:S(2)}, u32[]{:S(2)}) collective-permute-start(f32[1,32,256]{2,1,0:T(8,128)S(1)} %add_add_fusion.1), channel_id=1, source_target_pairs={{0,4},{1,5},{2,6},{3,7},{4,0},{5,1},{6,2},{7,3},{8,12},{9,13},{10,... | collective-permute-start | bytes 98312 | tf_op jit(solution)/shard_map/ppermute | solution.py:37
  19.2 3.9 %collective-permute-start.8 = (f32[1,32,256]{2,1,0:T(8,128)S(1)}, f32[1,32,256]{2,1,0:T(8,128)S(1)}, u32[]{:S(2)}, u32[]{:S(2)}) collective-permute-start(f32[1,32,256]{2,1,0:T(8,128)S(1)} %get-tuple-element.29), channel_id=1, source_target_pairs={{0,24},{8,16},{16,8},{24,0},{1,25},{9,17},{17,9},{25,1},{2,26},{10... | collective-permute-start | bytes 98312 | tf_op jit(solution)/shard_map/ppermute | solution.py:37
  19.3 4.2 %collective-permute-start.9 = (f32[1,32,256]{2,1,0:T(8,128)S(1)}, f32[1,32,256]{2,1,0:T(8,128)S(1)}, u32[]{:S(2)}, u32[]{:S(2)}) collective-permute-start(f32[1,32,256]{2,1,0:T(8,128)S(1)} %get-tuple-element.30), channel_id=1, source_target_pairs={{0,16},{8,24},{16,0},{24,8},{1,17},{9,25},{17,1},{25,9},{2,18},{10... | collective-permute-start | bytes 98312 | tf_op jit(solution)/shard_map/ppermute | solution.py:37
  20.4 3.1 %collective-permute-start.10 = (f32[1,32,256]{2,1,0:T(8,128)S(1)}, f32[1,32,256]{2,1,0:T(8,128)S(1)}, u32[]{:S(2)}, u32[]{:S(2)}) collective-permute-start(f32[1,32,256]{2,1,0:T(8,128)S(1)} %get-tuple-element.31), channel_id=1, source_target_pairs={{0,8},{8,0},{16,24},{24,16},{1,9},{9,1},{17,25},{25,17},{2,10},{10... | collective-permute-start | bytes 98312 | tf_op jit(solution)/shard_map/ppermute | solution.py:37
  23.6 15.6 %copy-start = (bf16[1,32,256]{2,1,0:T(8,128)(2,1)}, bf16[1,32,256]{2,1,0:T(8,128)(2,1)S(1)}, u32[]{:S(2)}) copy-start(bf16[1,32,256]{2,1,0:T(8,128)(2,1)S(1)} %add_convert_fusion.refs_0_.refs_4_) | copy-start | bytes 49156
  23.6 5.1 %collective-permute-start.14 = (bf16[1,32,256]{2,1,0:T(8,128)(2,1)S(1)}, bf16[1,32,256]{2,1,0:T(8,128)(2,1)S(1)}, u32[]{:S(2)}, u32[]{:S(2)}) collective-permute-start(bf16[1,32,256]{2,1,0:T(8,128)(2,1)S(1)} %add_convert_fusion.refs_0_.refs_4_), channel_id=1, source_target_pairs={{0,4},{1,5},{2,6},{3,7},{4,0},{5,1},{6,2},{7,3},{8,12},{9,13},{10,... | collective-permute-start | bytes 49160 | tf_op jit(solution)/shard_map/ppermute | solution.py:37
  26.2 3.3 %collective-permute-start.13 = (bf16[1,32,256]{2,1,0:T(8,128)(2,1)S(1)}, bf16[1,32,256]{2,1,0:T(8,128)(2,1)S(1)}, u32[]{:S(2)}, u32[]{:S(2)}) collective-permute-start(bf16[1,32,256]{2,1,0:T(8,128)(2,1)S(1)} %add_convert_fusion.refs_0_.refs_4_), channel_id=1, source_target_pairs={{0,24},{8,16},{16,8},{24,0},{1,25},{9,17},{17,9},{25,1},{2,26},{10... | collective-permute-start | bytes 49160 | tf_op jit(solution)/shard_map/ppermute | solution.py:37
  26.3 3.7 %collective-permute-start.12 = (bf16[1,32,256]{2,1,0:T(8,128)(2,1)S(1)}, bf16[1,32,256]{2,1,0:T(8,128)(2,1)S(1)}, u32[]{:S(2)}, u32[]{:S(2)}) collective-permute-start(bf16[1,32,256]{2,1,0:T(8,128)(2,1)S(1)} %add_convert_fusion.refs_0_.refs_4_), channel_id=1, source_target_pairs={{0,16},{8,24},{16,0},{24,8},{1,17},{9,25},{17,1},{25,9},{2,18},{10... | collective-permute-start | bytes 49160 | tf_op jit(solution)/shard_map/ppermute | solution.py:37
  27.6 2.5 %collective-permute-start.11 = (bf16[1,32,256]{2,1,0:T(8,128)(2,1)S(1)}, bf16[1,32,256]{2,1,0:T(8,128)(2,1)S(1)}, u32[]{:S(2)}, u32[]{:S(2)}) collective-permute-start(bf16[1,32,256]{2,1,0:T(8,128)(2,1)S(1)} %add_convert_fusion.refs_0_.refs_4_), channel_id=1, source_target_pairs={{0,8},{8,0},{16,24},{24,16},{1,9},{9,1},{17,25},{25,17},{2,10},{10... | collective-permute-start | bytes 49160 | tf_op jit(solution)/shard_map/ppermute | solution.py:37
  30.6 6.7 %collective-permute-start.15 = (bf16[6,32,256]{2,1,0:T(8,128)(2,1)S(1)}, bf16[6,32,256]{2,1,0:T(8,128)(2,1)S(1)}, u32[]{:S(2)}, u32[]{:S(2)}) collective-permute-start(bf16[6,32,256]{2,1,0:T(8,128)(2,1)S(1)} %get-tuple-element.33), channel_id=1, source_target_pairs={{0,3},{1,2},{2,1},{3,0},{4,7},{5,6},{6,5},{7,4},{8,11},{9,10},{10,... | collective-permute-start | bytes 294920 | tf_op jit(solution)/shard_map/ppermute | solution.py:37
  33.5 5.0 %collective-permute-start.16 = (bf16[6,32,256]{2,1,0:T(8,128)(2,1)S(1)}, bf16[6,32,256]{2,1,0:T(8,128)(2,1)S(1)}, u32[]{:S(2)}, u32[]{:S(2)}) collective-permute-start(bf16[6,32,256]{2,1,0:T(8,128)(2,1)S(1)} %get-tuple-element.34), channel_id=1, source_target_pairs={{0,2},{1,3},{2,0},{3,1},{4,6},{5,7},{6,4},{7,5},{8,10},{9,11},{10,... | collective-permute-start | bytes 294920 | tf_op jit(solution)/shard_map/ppermute | solution.py:37
  34.0 4.6 %collective-permute-start.17 = (bf16[6,32,256]{2,1,0:T(8,128)(2,1)S(1)}, bf16[6,32,256]{2,1,0:T(8,128)(2,1)S(1)}, u32[]{:S(2)}, u32[]{:S(2)}) collective-permute-start(bf16[6,32,256]{2,1,0:T(8,128)(2,1)S(1)} %get-tuple-element.35), channel_id=1, source_target_pairs={{0,1},{1,0},{2,3},{3,2},{4,5},{5,4},{6,7},{7,6},{8,9},{9,8},{10,11... | collective-permute-start | bytes 294920 | tf_op jit(solution)/shard_map/ppermute | solution.py:37
  38.6 4.9 %collective-permute-start.18 = (f32[1,32,256]{2,1,0:T(8,128)S(1)}, f32[1,32,256]{2,1,0:T(8,128)S(1)}, u32[]{:S(2)}, u32[]{:S(2)}) collective-permute-start(f32[1,32,256]{2,1,0:T(8,128)S(1)} %add_add_fusion), channel_id=1, source_target_pairs={{0,4},{1,5},{2,6},{3,7},{4,0},{5,1},{6,2},{7,3},{8,12},{9,13},{10,... | collective-permute-start | bytes 98312 | tf_op jit(solution)/shard_map/ppermute | solution.py:37
  39.7 3.8 %collective-permute-start.19 = (f32[1,32,256]{2,1,0:T(8,128)S(1)}, f32[1,32,256]{2,1,0:T(8,128)S(1)}, u32[]{:S(2)}, u32[]{:S(2)}) collective-permute-start(f32[1,32,256]{2,1,0:T(8,128)S(1)} %get-tuple-element.37), channel_id=1, source_target_pairs={{0,24},{8,16},{16,8},{24,0},{1,25},{9,17},{17,9},{25,1},{2,26},{10... | collective-permute-start | bytes 98312 | tf_op jit(solution)/shard_map/ppermute | solution.py:37
  39.8 4.3 %collective-permute-start.20 = (f32[1,32,256]{2,1,0:T(8,128)S(1)}, f32[1,32,256]{2,1,0:T(8,128)S(1)}, u32[]{:S(2)}, u32[]{:S(2)}) collective-permute-start(f32[1,32,256]{2,1,0:T(8,128)S(1)} %get-tuple-element.38), channel_id=1, source_target_pairs={{0,16},{8,24},{16,0},{24,8},{1,17},{9,25},{17,1},{25,9},{2,18},{10... | collective-permute-start | bytes 98312 | tf_op jit(solution)/shard_map/ppermute | solution.py:37
  40.8 3.2 %collective-permute-start.21 = (f32[1,32,256]{2,1,0:T(8,128)S(1)}, f32[1,32,256]{2,1,0:T(8,128)S(1)}, u32[]{:S(2)}, u32[]{:S(2)}) collective-permute-start(f32[1,32,256]{2,1,0:T(8,128)S(1)} %get-tuple-element.39), channel_id=1, source_target_pairs={{0,8},{8,0},{16,24},{24,16},{1,9},{9,1},{17,25},{25,17},{2,10},{10... | collective-permute-start | bytes 98312 | tf_op jit(solution)/shard_map/ppermute | solution.py:37

commit v6 on v5

--- a/solution.py
+++ b/solution.py
@@ -53,11 +53,28 @@
     return slots
 
 
-def slot_index(me, digits, steps):
-    for (stride, radix), step in zip(digits, steps):
-        if step:
+def twisted(step, odd):
+    return (0, 1 + odd, 2 - odd, 3)[step]
+
+
+def slot_index(me, digits, steps, odd=None):
+    for turn, ((stride, radix), step) in enumerate(zip(digits, steps)):
+        if step and turn == 0 and radix == 4 and odd is not None:
+            me = me ^ (twisted(step, odd) * stride)
+        elif step:
             me = moved(me, stride, radix, step)
     return me
+
+
+def send_twisted(value, n_rows, n_cols, stride, radix, step):
+    if radix != 4:
+        return send(value, "col", n_cols, stride, radix, step)
+    pairs = [
+        (row * n_cols + col, row * n_cols + (col ^ (twisted(step, row & 1) * stride)))
+        for row in range(n_rows)
+        for col in range(n_cols)
+    ]
+    return lax.ppermute(value, ("row", "col"), pairs)
 
 
 def sizes_of(digits):
@@ -168,10 +185,10 @@
         products(code_ref, tiles_ref, vec, acc, True, turned)
         slots = slots_of(cols)
         for i in range(held):
-            keep_ref[i] = acc[slot_index(me_c, cols, slots[i])]
+            keep_ref[i] = acc[slot_index(me_c, cols, slots[i], me_r & 1)]
         for step, out in enumerate(outs, 1):
             for i in range(held):
-                value = acc[slot_index(me_c, cols, slots[step * held + i])]
+                value = acc[slot_index(me_c, cols, slots[step * held + i], me_r & 1)]
                 high = value.astype(jnp.bfloat16)
                 out[i] = high
                 out[held + i] = (value - high.astype(jnp.float32)).astype(jnp.bfloat16)
@@ -209,10 +226,10 @@
         where = iter(slots_of(cols))
         for piece in ins[:n_own]:
             for i in range(piece.shape[0]):
-                vec[slot_index(me_c, cols, next(where))] = piece[i]
+                vec[slot_index(me_c, cols, next(where), me_r & 1)] = piece[i]
         for piece in ins[n_own:]:
             for i in range(held):
-                vec[slot_index(me_c, cols, next(where))] = piece[2 * held + i]
+                vec[slot_index(me_c, cols, next(where), me_r & 1)] = piece[2 * held + i]
         products(code_ref, tiles_ref, vec, acc, False)
         where = iter(slots_of(rows))
         for out in outs:
@@ -244,7 +261,7 @@
         colset = gather(vec, kept, "row", n_rows, rows)
         own = gather(vec, kept, "col", n_cols, outer)
         keep, *packed = direct_half(codes, colset, own, turned if again else tiles, rows, cols, again)
-        got = [send(value, "col", n_cols, *inner, step) for step, value in enumerate(packed, 1)]
+        got = [send_twisted(value, n_rows, n_cols, *inner, step) for step, value in enumerate(packed, 1)]
         held, at, pieces = keep.shape[0], 0, []
         for size in sizes_of(outer):
             value = keep[at : at + size]

time: 44.8 us -> 44.6 us (level)
    ppermute x22 -> x16, waiting for transfers between devices: 15.6 us -> 6.55 us  [send(): return lax.ppermute(value, axis, pairs)]
    ppermute x0 -> x6, waiting for transfers between devices: none -> 8.86 us  [send_twisted(): return lax.ppermute(value, ('row', 'col'), pairs)]
    ppermute x0 -> x6, starting transfers between devices: none -> 7.11 us  [send_twisted(): return lax.ppermute(value, ('row', 'col'), pairs)]
    ppermute x22 -> x16, starting transfers between devices: 22.4 us -> 15.3 us  [send(): return lax.ppermute(value, axis, pairs)]
  transfers between devices with their start and end apart: 22 -> 22, of which waited for: 13 -> 12; matrix products, arithmetic and copies ran while one was open for 0% -> 0% of each run, Pallas kernels for 7% -> 7%
where the time goes in v6:
time: 44.6 us; the launch traced here: 44.4 us
  starting transfers between devices  22.4 us (50%)
  waiting for transfers between devices  15.4 us (35%)
  Pallas kernels  4.52 us (10%)
  between operations  1.41 us (3%)
  other arithmetic  0.7 us (2%)
    ppermute x16, starting transfers between devices, send(): return lax.ppermute(value, axis, pairs)  15.3 us
    ppermute x6, waiting for transfers between devices, send_twisted(): return lax.ppermute(value, ('row', 'col'), pairs)  8.86 us
    ppermute x6, starting transfers between devices, send_twisted(): return lax.ppermute(value, ('row', 'col'), pairs)  7.11 us
    ppermute x16, waiting for transfers between devices, send(): return lax.ppermute(value, axis, pairs)  6.55 us
    pallas_call x1, Pallas kernels, fetch(): pl.pallas_call(fetch_kernel, out_shape=[jax.ShapeDtypeStruct(tiles.shape,...  1.63 us
    pallas_call x2, Pallas kernels, direct_half(): pl.pallas_call(body, out_shape=[jax.ShapeDtypeStruct((held, width, size),...  1.31 us
    pallas_call x2, Pallas kernels, mirror_half(): pl.pallas_call(body, out_shape=[jax.ShapeDtypeStruct((n, width, size), jn...  0.99 us
  transfers between devices with their start and end apart: 22, of which 12 were waited for; matrix products, arithmetic and copies ran while one was open for 0% of the time, Pallas kernels for 7%

profile of v6, /device:TPU:0, one launch (start us, length us, event | category | flops | bytes accessed | tf_op | source)
XLA Modules:
  0.0 44.4 jit_solution(8939493638978927864)
XLA Ops:
  0.6 4.1 %collective-permute-start.3 = (bf16[1,32,256]{2,1,0:T(8,128)(2,1)}, bf16[1,32,256]{2,1,0:T(8,128)(2,1)S(1)}, u32[]{:S(2)}, u32[]{:S(2)}) collective-permute-start(bf16[1,32,256]{2,1,0:T(8,128)(2,1)} %bitcast.11), channel_id=1, source_target_pairs={{0,4},{1,5},{2,6},{3,7},{4,0},{5,1},{6,2},{7,3},{8,12},{9,13},{10,... | collective-permute-start | bytes 49160 | tf_op jit(solution)/shard_map/ppermute | solution.py:37
  4.7 0.7 %collective-permute-start.2 = (bf16[1,32,256]{2,1,0:T(8,128)(2,1)}, bf16[1,32,256]{2,1,0:T(8,128)(2,1)S(1)}, u32[]{:S(2)}, u32[]{:S(2)}) collective-permute-start(bf16[1,32,256]{2,1,0:T(8,128)(2,1)} %bitcast.12), channel_id=1, source_target_pairs={{0,24},{8,16},{16,8},{24,0},{1,25},{9,17},{17,9},{25,1},{2,26},{10... | collective-permute-start | bytes 49160 | tf_op jit(solution)/shard_map/ppermute | solution.py:37
  5.4 0.9 %collective-permute-start.1 = (bf16[1,32,256]{2,1,0:T(8,128)(2,1)}, bf16[1,32,256]{2,1,0:T(8,128)(2,1)S(1)}, u32[]{:S(2)}, u32[]{:S(2)}) collective-permute-start(bf16[1,32,256]{2,1,0:T(8,128)(2,1)} %bitcast.13), channel_id=1, source_target_pairs={{0,16},{8,24},{16,0},{24,8},{1,17},{9,25},{17,1},{25,9},{2,18},{10... | collective-permute-start | bytes 49160 | tf_op jit(solution)/shard_map/ppermute | solution.py:37
  7.2 1.6 %fetch.1 = (bf16[16,256,256]{2,1,0:T(8,128)(2,1)S(1)}, bf16[32,256]{1,0:T(8,128)(2,1)S(1)}, s32[16,128]{1,0:T(8,128)S(1)}) custom-call(bf16[16,256,256]{2,1,0:T(8,128)(2,1)} %tiles_hbm.1, bf16[32,256]{1,0:T(8,128)(2,1)} %vec_hbm.1, s32[16]{0:T(128)} %rows_hbm.1, s32[16]{0:T(128)} %cols_hbm.1, s32[1]{0:T(128)S(6)} %copy.7.live_ref), custom_call_target="tpu_custom_call" | custom-call | bytes 8388608 | tf_op jit(solution)/shard_map/fetch/pallas_call | solution.py:124
  8.9 0.6 %collective-permute-done.1.refs_2_ = bf16[1,32,256]{2,1,0:T(8,128)(2,1)S(1)} collective-permute-done((bf16[1,32,256]{2,1,0:T(8,128)(2,1)}, bf16[1,32,256]{2,1,0:T(8,128)(2,1)S(1)}, u32[]{:S(2)}, u32[]{:S(2)}) %collective-permute-start.1) | collective-permute-done | bytes 16416 | tf_op jit(solution)/shard_map/ppermute | solution.py:37
  9.5 0.8 %direct.2 = (f32[2,32,256]{2,1,0:T(8,128)S(1)}, bf16[6,32,256]{2,1,0:T(8,128)(2,1)S(1)}, bf16[6,32,256]{2,1,0:T(8,128)(2,1)S(1)}, bf16[6,32,256]{2,1,0:T(8,128)(2,1)S(1)}) custom-call(s32[16,128]{1,0:T(8,128)S(1)} %get-tuple-element.21.code_ref, bf16[1,32,256]{2,1,0:T(8,128)(2,1)S(1)} %bitcast.7, bf16[1,32,256]{2,1,0:T(8,128)(2,1)S(1)} %collective-permute-done.refs_1_, ...), custom_call_target="tpu_custom_call" | custom-call | tf_op jit(solution)/shard_map/direct/pallas_call | solution.py:201
  10.3 2.6 %collective-permute-start.4 = (bf16[6,32,256]{2,1,0:T(8,128)(2,1)S(1)}, bf16[6,32,256]{2,1,0:T(8,128)(2,1)S(1)}, u32[]{:S(2)}, u32[]{:S(2)}) collective-permute-start(bf16[6,32,256]{2,1,0:T(8,128)(2,1)S(1)} %get-tuple-element.25), channel_id=1, source_target_pairs={{0,3},{1,2},{2,1},{3,0},{4,7},{5,6},{6,5},{7,4},{8,11},{9,10},{10,... | collective-permute-start | bytes 294920 | tf_op jit(solution)/shard_map/ppermute | solution.py:77
  13.8 2.3 %collective-permute-done.4.refs_4_ = bf16[6,32,256]{2,1,0:T(8,128)(2,1)S(1)} collective-permute-done((bf16[6,32,256]{2,1,0:T(8,128)(2,1)S(1)}, bf16[6,32,256]{2,1,0:T(8,128)(2,1)S(1)}, u32[]{:S(2)}, u32[]{:S(2)}) %collective-permute-start.4) | collective-permute-done | bytes 98336 | tf_op jit(solution)/shard_map/ppermute | solution.py:77
  16.1 2.1 %collective-permute-done.5.refs_3_ = bf16[6,32,256]{2,1,0:T(8,128)(2,1)S(1)} collective-permute-done((bf16[6,32,256]{2,1,0:T(8,128)(2,1)S(1)}, bf16[6,32,256]{2,1,0:T(8,128)(2,1)S(1)}, u32[]{:S(2)}, u32[]{:S(2)}) %collective-permute-start.5) | collective-permute-done | bytes 98336 | tf_op jit(solution)/shard_map/ppermute | solution.py:77
  19.2 1.2 %collective-permute-start.9 = (f32[1,32,256]{2,1,0:T(8,128)S(1)}, f32[1,32,256]{2,1,0:T(8,128)S(1)}, u32[]{:S(2)}, u32[]{:S(2)}) collective-permute-start(f32[1,32,256]{2,1,0:T(8,128)S(1)} %get-tuple-element.30), channel_id=1, source_target_pairs={{0,16},{8,24},{16,0},{24,8},{1,17},{9,25},{17,1},{25,9},{2,18},{10... | collective-permute-start | bytes 98312 | tf_op jit(solution)/shard_map/ppermute | solution.py:37
  20.4 0.7 %collective-permute-start.10 = (f32[1,32,256]{2,1,0:T(8,128)S(1)}, f32[1,32,256]{2,1,0:T(8,128)S(1)}, u32[]{:S(2)}, u32[]{:S(2)}) collective-permute-start(f32[1,32,256]{2,1,0:T(8,128)S(1)} %get-tuple-element.31), channel_id=1, source_target_pairs={{0,8},{8,0},{16,24},{24,16},{1,9},{9,1},{17,25},{25,17},{2,10},{10... | collective-permute-start | bytes 98312 | tf_op jit(solution)/shard_map/ppermute | solution.py:37
  21.0 2.1 %collective-permute-done.7 = f32[1,32,256]{2,1,0:T(8,128)S(1)} collective-permute-done((f32[1,32,256]{2,1,0:T(8,128)S(1)}, f32[1,32,256]{2,1,0:T(8,128)S(1)}, u32[]{:S(2)}, u32[]{:S(2)}) %collective-permute-start.7) | collective-permute-done | bytes 32800 | tf_op jit(solution)/shard_map/ppermute | solution.py:37
  23.4 2.8 %collective-permute-start.14 = (bf16[1,32,256]{2,1,0:T(8,128)(2,1)S(1)}, bf16[1,32,256]{2,1,0:T(8,128)(2,1)S(1)}, u32[]{:S(2)}, u32[]{:S(2)}) collective-permute-start(bf16[1,32,256]{2,1,0:T(8,128)(2,1)S(1)} %add_convert_fusion.refs_0_.refs_4_), channel_id=1, source_target_pairs={{0,4},{1,5},{2,6},{3,7},{4,0},{5,1},{6,2},{7,3},{8,12},{9,13},{10,... | collective-permute-start | bytes 49160 | tf_op jit(solution)/shard_map/ppermute | solution.py:37
  26.3 1.3 %collective-permute-start.12 = (bf16[1,32,256]{2,1,0:T(8,128)(2,1)S(1)}, bf16[1,32,256]{2,1,0:T(8,128)(2,1)S(1)}, u32[]{:S(2)}, u32[]{:S(2)}) collective-permute-start(bf16[1,32,256]{2,1,0:T(8,128)(2,1)S(1)} %add_convert_fusion.refs_0_.refs_4_), channel_id=1, source_target_pairs={{0,16},{8,24},{16,0},{24,8},{1,17},{9,25},{17,1},{25,9},{2,18},{10... | collective-permute-start | bytes 49160 | tf_op jit(solution)/shard_map/ppermute | solution.py:37
  28.6 0.8 %collective-permute-done.13.refs_3_ = bf16[1,32,256]{2,1,0:T(8,128)(2,1)S(1)} collective-permute-done((bf16[1,32,256]{2,1,0:T(8,128)(2,1)S(1)}, bf16[1,32,256]{2,1,0:T(8,128)(2,1)S(1)}, u32[]{:S(2)}, u32[]{:S(2)}) %collective-permute-start.13) | collective-permute-done | bytes 16416 | tf_op jit(solution)/shard_map/ppermute | solution.py:37
  29.4 0.6 %collective-permute-done.12.refs_2_ = bf16[1,32,256]{2,1,0:T(8,128)(2,1)S(1)} collective-permute-done((bf16[1,32,256]{2,1,0:T(8,128)(2,1)S(1)}, bf16[1,32,256]{2,1,0:T(8,128)(2,1)S(1)}, u32[]{:S(2)}, u32[]{:S(2)}) %collective-permute-start.12) | collective-permute-done | bytes 16416 | tf_op jit(solution)/shard_map/ppermute | solution.py:37
  30.6 2.0 %collective-permute-start.15 = (bf16[6,32,256]{2,1,0:T(8,128)(2,1)S(1)}, bf16[6,32,256]{2,1,0:T(8,128)(2,1)S(1)}, u32[]{:S(2)}, u32[]{:S(2)}) collective-permute-start(bf16[6,32,256]{2,1,0:T(8,128)(2,1)S(1)} %get-tuple-element.33), channel_id=1, source_target_pairs={{0,3},{1,2},{2,1},{3,0},{4,7},{5,6},{6,5},{7,4},{8,11},{9,10},{10,... | collective-permute-start | bytes 294920 | tf_op jit(solution)/shard_map/ppermute | solution.py:77
  32.6 1.4 %collective-permute-start.16 = (bf16[6,32,256]{2,1,0:T(8,128)(2,1)S(1)}, bf16[6,32,256]{2,1,0:T(8,128)(2,1)S(1)}, u32[]{:S(2)}, u32[]{:S(2)}) collective-permute-start(bf16[6,32,256]{2,1,0:T(8,128)(2,1)S(1)} %get-tuple-element.34), channel_id=1, source_target_pairs={{0,2},{1,3},{2,0},{3,1},{4,6},{5,7},{6,4},{7,5},{8,9},{9,8},{10,11... | collective-permute-start | bytes 294920 | tf_op jit(solution)/shard_map/ppermute | solution.py:77
  34.1 2.6 %collective-permute-done.15.refs_4_ = bf16[6,32,256]{2,1,0:T(8,128)(2,1)S(1)} collective-permute-done((bf16[6,32,256]{2,1,0:T(8,128)(2,1)S(1)}, bf16[6,32,256]{2,1,0:T(8,128)(2,1)S(1)}, u32[]{:S(2)}, u32[]{:S(2)}) %collective-permute-start.15) | collective-permute-done | bytes 98336 | tf_op jit(solution)/shard_map/ppermute | solution.py:77
  36.7 1.7 %collective-permute-done.16.refs_3_ = bf16[6,32,256]{2,1,0:T(8,128)(2,1)S(1)} collective-permute-done((bf16[6,32,256]{2,1,0:T(8,128)(2,1)S(1)}, bf16[6,32,256]{2,1,0:T(8,128)(2,1)S(1)}, u32[]{:S(2)}, u32[]{:S(2)}) %collective-permute-start.16) | collective-permute-done | bytes 98336 | tf_op jit(solution)/shard_map/ppermute | solution.py:77
  39.7 1.2 %collective-permute-start.20 = (f32[1,32,256]{2,1,0:T(8,128)S(1)}, f32[1,32,256]{2,1,0:T(8,128)S(1)}, u32[]{:S(2)}, u32[]{:S(2)}) collective-permute-start(f32[1,32,256]{2,1,0:T(8,128)S(1)} %get-tuple-element.38), channel_id=1, source_target_pairs={{0,16},{8,24},{16,0},{24,8},{1,17},{9,25},{17,1},{25,9},{2,18},{10... | collective-permute-start | bytes 98312 | tf_op jit(solution)/shard_map/ppermute | solution.py:37
  41.0 0.6 %collective-permute-start.21 = (f32[1,32,256]{2,1,0:T(8,128)S(1)}, f32[1,32,256]{2,1,0:T(8,128)S(1)}, u32[]{:S(2)}, u32[]{:S(2)}) collective-permute-start(f32[1,32,256]{2,1,0:T(8,128)S(1)} %get-tuple-element.39), channel_id=1, source_target_pairs={{0,8},{8,0},{16,24},{24,16},{1,9},{9,1},{17,25},{25,17},{2,10},{10... | collective-permute-start | bytes 98312 | tf_op jit(solution)/shard_map/ppermute | solution.py:37
  41.6 1.9 %collective-permute-done.18 = f32[1,32,256]{2,1,0:T(8,128)S(1)} collective-permute-done((f32[1,32,256]{2,1,0:T(8,128)S(1)}, f32[1,32,256]{2,1,0:T(8,128)S(1)}, u32[]{:S(2)}, u32[]{:S(2)}) %collective-permute-start.18) | collective-permute-done | bytes 32800 | tf_op jit(solution)/shard_map/ppermute | solution.py:37
  43.8 0.6 %fusion = bf16[32,256]{1,0:T(8,128)(2,1)} fusion(bf16[32,256]{1,0:T(8,128)(2,1)S(1)} %get-tuple-element.22, f32[1,32,256]{2,1,0:T(8,128)S(1)} %collective-permute-done.21, f32[1,32,256]{2,1,0:T(8,128)S(1)} %collective-permute-done.20, f32[1,32,256]{2,1,0:T(8,128)S(1)} %get-tuple-element.36, f32[1,32,256]{2,1,0:T(8,128)S(1)} %collective-permute-done.19, ...), kind=kLoop, calls=%fused_computation.1 | loop fusion | flops 172032 | bytes 327680 | tf_op jit(solution)/shard_map/convert_element_type | solution.py:278
  (32 shorter events, 6.0 us)
Async XLA Ops:
  0.6 8.3 %collective-permute-start.3 = (bf16[1,32,256]{2,1,0:T(8,128)(2,1)}, bf16[1,32,256]{2,1,0:T(8,128)(2,1)S(1)}, u32[]{:S(2)}, u32[]{:S(2)}) collective-permute-start(bf16[1,32,256]{2,1,0:T(8,128)(2,1)} %bitcast.11), channel_id=1, source_target_pairs={{0,4},{1,5},{2,6},{3,7},{4,0},{5,1},{6,2},{7,3},{8,12},{9,13},{10,... | collective-permute-start | bytes 49160 | tf_op jit(solution)/shard_map/ppermute | solution.py:37
  4.7 4.2 %collective-permute-start.2 = (bf16[1,32,256]{2,1,0:T(8,128)(2,1)}, bf16[1,32,256]{2,1,0:T(8,128)(2,1)S(1)}, u32[]{:S(2)}, u32[]{:S(2)}) collective-permute-start(bf16[1,32,256]{2,1,0:T(8,128)(2,1)} %bitcast.12), channel_id=1, source_target_pairs={{0,24},{8,16},{16,8},{24,0},{1,25},{9,17},{17,9},{25,1},{2,26},{10... | collective-permute-start | bytes 49160 | tf_op jit(solution)/shard_map/ppermute | solution.py:37
  5.4 4.1 %collective-permute-start.1 = (bf16[1,32,256]{2,1,0:T(8,128)(2,1)}, bf16[1,32,256]{2,1,0:T(8,128)(2,1)S(1)}, u32[]{:S(2)}, u32[]{:S(2)}) collective-permute-start(bf16[1,32,256]{2,1,0:T(8,128)(2,1)} %bitcast.13), channel_id=1, source_target_pairs={{0,16},{8,24},{16,0},{24,8},{1,17},{9,25},{17,1},{25,9},{2,18},{10... | collective-permute-start | bytes 49160 | tf_op jit(solution)/shard_map/ppermute | solution.py:37
  6.3 3.2 %collective-permute-start = (bf16[1,32,256]{2,1,0:T(8,128)(2,1)}, bf16[1,32,256]{2,1,0:T(8,128)(2,1)S(1)}, u32[]{:S(2)}, u32[]{:S(2)}) collective-permute-start(bf16[1,32,256]{2,1,0:T(8,128)(2,1)} %bitcast.14), channel_id=1, source_target_pairs={{0,8},{8,0},{16,24},{24,16},{1,9},{9,1},{17,25},{25,17},{2,10},{10... | collective-permute-start | bytes 49160 | tf_op jit(solution)/shard_map/ppermute | solution.py:37
  10.3 5.8 %collective-permute-start.4 = (bf16[6,32,256]{2,1,0:T(8,128)(2,1)S(1)}, bf16[6,32,256]{2,1,0:T(8,128)(2,1)S(1)}, u32[]{:S(2)}, u32[]{:S(2)}) collective-permute-start(bf16[6,32,256]{2,1,0:T(8,128)(2,1)S(1)} %get-tuple-element.25), channel_id=1, source_target_pairs={{0,3},{1,2},{2,1},{3,0},{4,7},{5,6},{6,5},{7,4},{8,11},{9,10},{10,... | collective-permute-start | bytes 294920 | tf_op jit(solution)/shard_map/ppermute | solution.py:77
  12.9 5.3 %collective-permute-start.5 = (bf16[6,32,256]{2,1,0:T(8,128)(2,1)S(1)}, bf16[6,32,256]{2,1,0:T(8,128)(2,1)S(1)}, u32[]{:S(2)}, u32[]{:S(2)}) collective-permute-start(bf16[6,32,256]{2,1,0:T(8,128)(2,1)S(1)} %get-tuple-element.26), channel_id=1, source_target_pairs={{0,2},{1,3},{2,0},{3,1},{4,6},{5,7},{6,4},{7,5},{8,9},{9,8},{10,11... | collective-permute-start | bytes 294920 | tf_op jit(solution)/shard_map/ppermute | solution.py:77
  13.3 4.9 %collective-permute-start.6 = (bf16[6,32,256]{2,1,0:T(8,128)(2,1)S(1)}, bf16[6,32,256]{2,1,0:T(8,128)(2,1)S(1)}, u32[]{:S(2)}, u32[]{:S(2)}) collective-permute-start(bf16[6,32,256]{2,1,0:T(8,128)(2,1)S(1)} %get-tuple-element.27), channel_id=1, source_target_pairs={{0,1},{1,0},{2,3},{3,2},{4,5},{5,4},{6,7},{7,6},{8,10},{9,11},{10,... | collective-permute-start | bytes 294920 | tf_op jit(solution)/shard_map/ppermute | solution.py:77
  18.2 4.9 %collective-permute-start.7 = (f32[1,32,256]{2,1,0:T(8,128)S(1)}, f32[1,32,256]{2,1,0:T(8,128)S(1)}, u32[]{:S(2)}, u32[]{:S(2)}) collective-permute-start(f32[1,32,256]{2,1,0:T(8,128)S(1)} %add_add_fusion.1), channel_id=1, source_target_pairs={{0,4},{1,5},{2,6},{3,7},{4,0},{5,1},{6,2},{7,3},{8,12},{9,13},{10,... | collective-permute-start | bytes 98312 | tf_op jit(solution)/shard_map/ppermute | solution.py:37
  19.1 4.0 %collective-permute-start.8 = (f32[1,32,256]{2,1,0:T(8,128)S(1)}, f32[1,32,256]{2,1,0:T(8,128)S(1)}, u32[]{:S(2)}, u32[]{:S(2)}) collective-permute-start(f32[1,32,256]{2,1,0:T(8,128)S(1)} %get-tuple-element.29), channel_id=1, source_target_pairs={{0,24},{8,16},{16,8},{24,0},{1,25},{9,17},{17,9},{25,1},{2,26},{10... | collective-permute-start | bytes 98312 | tf_op jit(solution)/shard_map/ppermute | solution.py:37
  19.2 4.2 %collective-permute-start.9 = (f32[1,32,256]{2,1,0:T(8,128)S(1)}, f32[1,32,256]{2,1,0:T(8,128)S(1)}, u32[]{:S(2)}, u32[]{:S(2)}) collective-permute-start(f32[1,32,256]{2,1,0:T(8,128)S(1)} %get-tuple-element.30), channel_id=1, source_target_pairs={{0,16},{8,24},{16,0},{24,8},{1,17},{9,25},{17,1},{25,9},{2,18},{10... | collective-permute-start | bytes 98312 | tf_op jit(solution)/shard_map/ppermute | solution.py:37
  20.4 3.0 %collective-permute-start.10 = (f32[1,32,256]{2,1,0:T(8,128)S(1)}, f32[1,32,256]{2,1,0:T(8,128)S(1)}, u32[]{:S(2)}, u32[]{:S(2)}) collective-permute-start(f32[1,32,256]{2,1,0:T(8,128)S(1)} %get-tuple-element.31), channel_id=1, source_target_pairs={{0,8},{8,0},{16,24},{24,16},{1,9},{9,1},{17,25},{25,17},{2,10},{10... | collective-permute-start | bytes 98312 | tf_op jit(solution)/shard_map/ppermute | solution.py:37
  23.4 15.7 %copy-start = (bf16[1,32,256]{2,1,0:T(8,128)(2,1)}, bf16[1,32,256]{2,1,0:T(8,128)(2,1)S(1)}, u32[]{:S(2)}) copy-start(bf16[1,32,256]{2,1,0:T(8,128)(2,1)S(1)} %add_convert_fusion.refs_0_.refs_4_) | copy-start | bytes 49156
  23.4 5.2 %collective-permute-start.14 = (bf16[1,32,256]{2,1,0:T(8,128)(2,1)S(1)}, bf16[1,32,256]{2,1,0:T(8,128)(2,1)S(1)}, u32[]{:S(2)}, u32[]{:S(2)}) collective-permute-start(bf16[1,32,256]{2,1,0:T(8,128)(2,1)S(1)} %add_convert_fusion.refs_0_.refs_4_), channel_id=1, source_target_pairs={{0,4},{1,5},{2,6},{3,7},{4,0},{5,1},{6,2},{7,3},{8,12},{9,13},{10,... | collective-permute-start | bytes 49160 | tf_op jit(solution)/shard_map/ppermute | solution.py:37
  26.2 3.3 %collective-permute-start.13 = (bf16[1,32,256]{2,1,0:T(8,128)(2,1)S(1)}, bf16[1,32,256]{2,1,0:T(8,128)(2,1)S(1)}, u32[]{:S(2)}, u32[]{:S(2)}) collective-permute-start(bf16[1,32,256]{2,1,0:T(8,128)(2,1)S(1)} %add_convert_fusion.refs_0_.refs_4_), channel_id=1, source_target_pairs={{0,24},{8,16},{16,8},{24,0},{1,25},{9,17},{17,9},{25,1},{2,26},{10... | collective-permute-start | bytes 49160 | tf_op jit(solution)/shard_map/ppermute | solution.py:37
  26.3 3.7 %collective-permute-start.12 = (bf16[1,32,256]{2,1,0:T(8,128)(2,1)S(1)}, bf16[1,32,256]{2,1,0:T(8,128)(2,1)S(1)}, u32[]{:S(2)}, u32[]{:S(2)}) collective-permute-start(bf16[1,32,256]{2,1,0:T(8,128)(2,1)S(1)} %add_convert_fusion.refs_0_.refs_4_), channel_id=1, source_target_pairs={{0,16},{8,24},{16,0},{24,8},{1,17},{9,25},{17,1},{25,9},{2,18},{10... | collective-permute-start | bytes 49160 | tf_op jit(solution)/shard_map/ppermute | solution.py:37
  27.5 2.5 %collective-permute-start.11 = (bf16[1,32,256]{2,1,0:T(8,128)(2,1)S(1)}, bf16[1,32,256]{2,1,0:T(8,128)(2,1)S(1)}, u32[]{:S(2)}, u32[]{:S(2)}) collective-permute-start(bf16[1,32,256]{2,1,0:T(8,128)(2,1)S(1)} %add_convert_fusion.refs_0_.refs_4_), channel_id=1, source_target_pairs={{0,8},{8,0},{16,24},{24,16},{1,9},{9,1},{17,25},{25,17},{2,10},{10... | collective-permute-start | bytes 49160 | tf_op jit(solution)/shard_map/ppermute | solution.py:37
  30.6 6.2 %collective-permute-start.15 = (bf16[6,32,256]{2,1,0:T(8,128)(2,1)S(1)}, bf16[6,32,256]{2,1,0:T(8,128)(2,1)S(1)}, u32[]{:S(2)}, u32[]{:S(2)}) collective-permute-start(bf16[6,32,256]{2,1,0:T(8,128)(2,1)S(1)} %get-tuple-element.33), channel_id=1, source_target_pairs={{0,3},{1,2},{2,1},{3,0},{4,7},{5,6},{6,5},{7,4},{8,11},{9,10},{10,... | collective-permute-start | bytes 294920 | tf_op jit(solution)/shard_map/ppermute | solution.py:77
  32.6 5.8 %collective-permute-start.16 = (bf16[6,32,256]{2,1,0:T(8,128)(2,1)S(1)}, bf16[6,32,256]{2,1,0:T(8,128)(2,1)S(1)}, u32[]{:S(2)}, u32[]{:S(2)}) collective-permute-start(bf16[6,32,256]{2,1,0:T(8,128)(2,1)S(1)} %get-tuple-element.34), channel_id=1, source_target_pairs={{0,2},{1,3},{2,0},{3,1},{4,6},{5,7},{6,4},{7,5},{8,9},{9,8},{10,11... | collective-permute-start | bytes 294920 | tf_op jit(solution)/shard_map/ppermute | solution.py:77
  34.0 4.6 %collective-permute-start.17 = (bf16[6,32,256]{2,1,0:T(8,128)(2,1)S(1)}, bf16[6,32,256]{2,1,0:T(8,128)(2,1)S(1)}, u32[]{:S(2)}, u32[]{:S(2)}) collective-permute-start(bf16[6,32,256]{2,1,0:T(8,128)(2,1)S(1)} %get-tuple-element.35), channel_id=1, source_target_pairs={{0,1},{1,0},{2,3},{3,2},{4,5},{5,4},{6,7},{7,6},{8,10},{9,11},{10,... | collective-permute-start | bytes 294920 | tf_op jit(solution)/shard_map/ppermute | solution.py:77
  38.6 4.9 %collective-permute-start.18 = (f32[1,32,256]{2,1,0:T(8,128)S(1)}, f32[1,32,256]{2,1,0:T(8,128)S(1)}, u32[]{:S(2)}, u32[]{:S(2)}) collective-permute-start(f32[1,32,256]{2,1,0:T(8,128)S(1)} %add_add_fusion), channel_id=1, source_target_pairs={{0,4},{1,5},{2,6},{3,7},{4,0},{5,1},{6,2},{7,3},{8,12},{9,13},{10,... | collective-permute-start | bytes 98312 | tf_op jit(solution)/shard_map/ppermute | solution.py:37
  39.6 3.9 %collective-permute-start.19 = (f32[1,32,256]{2,1,0:T(8,128)S(1)}, f32[1,32,256]{2,1,0:T(8,128)S(1)}, u32[]{:S(2)}, u32[]{:S(2)}) collective-permute-start(f32[1,32,256]{2,1,0:T(8,128)S(1)} %get-tuple-element.37), channel_id=1, source_target_pairs={{0,24},{8,16},{16,8},{24,0},{1,25},{9,17},{17,9},{25,1},{2,26},{10... | collective-permute-start | bytes 98312 | tf_op jit(solution)/shard_map/ppermute | solution.py:37
  39.7 4.1 %collective-permute-start.20 = (f32[1,32,256]{2,1,0:T(8,128)S(1)}, f32[1,32,256]{2,1,0:T(8,128)S(1)}, u32[]{:S(2)}, u32[]{:S(2)}) collective-permute-start(f32[1,32,256]{2,1,0:T(8,128)S(1)} %get-tuple-element.38), channel_id=1, source_target_pairs={{0,16},{8,24},{16,0},{24,8},{1,17},{9,25},{17,1},{25,9},{2,18},{10... | collective-permute-start | bytes 98312 | tf_op jit(solution)/shard_map/ppermute | solution.py:37
  41.0 2.8 %collective-permute-start.21 = (f32[1,32,256]{2,1,0:T(8,128)S(1)}, f32[1,32,256]{2,1,0:T(8,128)S(1)}, u32[]{:S(2)}, u32[]{:S(2)}) collective-permute-start(f32[1,32,256]{2,1,0:T(8,128)S(1)} %get-tuple-element.39), channel_id=1, source_target_pairs={{0,8},{8,0},{16,24},{24,16},{1,9},{9,1},{17,25},{25,17},{2,10},{10... | collective-permute-start | bytes 98312 | tf_op jit(solution)/shard_map/ppermute | solution.py:37
